TPU v7x, 256 devices: a whole 4x4x8 slice. The times are simulated.
256 devices in a mesh: band: 16 (over y, x_lo, core), cols: 16 (over x_hi, z).
Axes of the slice: x: 4 (x_hi: 2, x_lo: 2; x = x_hi * 2 + x_lo), y: 4, z: 8, core: 2. Of those that a mesh axis runs over, the one named last changes fastest.
Arguments:
- band_diagonals: float32 [256, 6144], P('cols', 'band'), may hold values from -0.4 to 0.4, as said below
- eigenvectors: float32 [6144, 2048], P('band', 'cols'), may hold values from -4 to 4
Outputs:
- band_result: float32 [256, 6144], P('cols', 'band')
- transformed: float32 [6144, 2048], P('band', 'cols')
Inputs may be any that keep to these rules, and one draw needn't show every extreme that they name: `band_diagonals`: entry [k, r] is the matrix's entry in row r and column r - k; it is zero where k > 128 or r < k.
All inputs are finite; a program needn't handle non-finite values.
Results may differ from a plain program's by a relative error of at most 0.0003.
Values sent between devices are 32-bit elements; how exact they have to be, the bound alone decides.
No kernel may reach another device: no remote copies, remote signals or barrier semaphores. Data moves between devices by JAX's collectives and lax.ppermute only.
A program may use at most 64 MiB of HBM per device.

v0:
```python
import jax
import jax.numpy as jnp
from jax import lax
from jax.sharding import PartitionSpec as P

SWEEPS = 4


HIGHEST = lax.Precision.HIGHEST


def laid_out(pieces, dim):
    dims = list(pieces.shape[1:])
    dims[dim] *= pieces.shape[0]
    return jnp.moveaxis(pieces, 0, dim).reshape(dims)


def copy_for_each(x, axis):
    peers = lax.axis_size(axis)
    return lax.all_to_all(jnp.broadcast_to(x[None], (peers, *x.shape)), axis, 0, 0, tiled=True)


def gather_directly(x, axis, dim):
    return laid_out(copy_for_each(x, axis), dim)


def padded_2(x, sides, width):
    for axis, dim in sides:
        peers, length = (lax.axis_size(axis), x.shape[dim])
        up = [(i, (i + 1) % peers) for i in range(peers - 1)]
        down = [(j, i) for i, j in up]
        last = lax.slice_in_dim(x, length - width, length, axis=dim)
        first = lax.slice_in_dim(x, 0, width, axis=dim)
        before = lax.ppermute(last, axis, up)
        after = lax.ppermute(first, axis, down)
        x = jnp.concatenate([before, x, after], axis=dim)
    return x


def from_behind(x, axis, by):
    peers = lax.axis_size(axis)
    pairs = [(i, i + by) for i in range(peers) if 0 <= i + by < peers]
    return lax.ppermute(x, axis, pairs)


def skew_rows(block_rows):
    row_count, col_count = block_rows.shape
    flipped = block_rows[:, ::-1]
    padded = jnp.pad(flipped, ((0, 0), (0, row_count)))
    flat_cells = padded.reshape(-1)[: row_count * (col_count + row_count - 1)]
    return flat_cells.reshape(row_count, col_count + row_count - 1)


def unskew_rows(dense_rows, col_count):
    row_count = dense_rows.shape[0]
    flat_cells = jnp.pad(dense_rows.reshape(-1), (0, row_count))
    grid_cells = flat_cells.reshape(row_count, col_count + row_count)
    return grid_cells[:, :col_count][:, ::-1]


def chase_step(region, first_step):
    double = region.shape[0]
    half_width = double // 2
    dense_rows = skew_rows(region)
    offset = half_width - 1
    upper_rows = dense_rows[:half_width, offset : offset + double]
    lower_rows = dense_rows[half_width:, offset + half_width : offset + double]
    left_part = upper_rows[:, :half_width]
    window = upper_rows[:, half_width:]
    column = jnp.where(first_step, left_part[:, half_width - 1], left_part[:, 0])
    length = jnp.sqrt(jnp.sum(column * column))
    vector = column.at[0].add(length)
    factor = 2.0 / jnp.sum(vector * vector)
    mirror = window + window.T - jnp.diag(jnp.diag(window))
    across = factor * jnp.dot(vector, left_part, precision=HIGHEST)
    inside = factor * jnp.dot(mirror, vector, precision=HIGHEST)
    beneath = factor * jnp.dot(lower_rows, vector, precision=HIGHEST)
    inside = inside - 0.5 * factor * jnp.dot(vector, inside, precision=HIGHEST) * vector
    left_part = left_part - vector[:, None] * across[None, :]
    window = window - jnp.tril(
        vector[:, None] * inside[None, :] + inside[:, None] * vector[None, :]
    )
    lower_rows = lower_rows - beneath[:, None] * vector[None, :]
    cleared = jnp.zeros_like(column).at[0].set(-length)
    left_part = jnp.where(
        first_step, left_part.at[:, half_width - 1].set(cleared), left_part.at[:, 0].set(cleared)
    )
    dense_rows = dense_rows.at[:half_width, offset : offset + double].set(
        jnp.concatenate([left_part, window], 1)
    )
    dense_rows = dense_rows.at[half_width:, offset + half_width : offset + double].set(lower_rows)
    return (unskew_rows(dense_rows, double), vector, factor)


def section_active(device, section_index, sweeps):
    offset = section_index - device
    return (offset >= 0) & (offset % 2 == 0) & (offset < 2 * sweeps)


def keep_same(operand):
    return operand


def body(band_diagonals, eigenvectors):
    pieces = gather_directly(band_diagonals, "cols", 0)
    own_rows = pieces.T
    rows_dev = own_rows.shape[0]
    double = own_rows.shape[1]
    half_width = double // 2
    blocks_dev = rows_dev // half_width
    columns = eigenvectors.shape[1]
    devices = lax.axis_size("band")
    device = lax.axis_index("band")
    sweeps = SWEEPS
    depth = half_width + sweeps
    state = jnp.concatenate([own_rows, jnp.zeros((double, double), jnp.float32)], 0)
    vectors = jnp.zeros((sweeps, blocks_dev, half_width), jnp.float32)
    factors = jnp.zeros((sweeps, blocks_dev), jnp.float32)
    local_steps = jnp.where(device == devices - 1, blocks_dev - 2, blocks_dev)
    sections = 2 * (sweeps - 1) + devices

    def run_sweep(operand):
        state, vectors, factors, sweep_index = operand

        def advance(step_index, carry):

            def apply_step(inner):
                state, vec_rows, tau_row = inner
                anchor = sweep_index + 1 + step_index * half_width
                region = lax.dynamic_slice_in_dim(state, anchor, double, 0)
                first_step = (device == 0) & (step_index == 0)
                region, vector, factor = chase_step(region, first_step)
                state = lax.dynamic_update_slice_in_dim(state, region, anchor, 0)
                vec_rows = vec_rows.at[step_index].set(vector)
                tau_row = tau_row.at[step_index].set(factor)
                return (state, vec_rows, tau_row)

            return lax.cond(step_index < local_steps, apply_step, keep_same, carry)

        vec_rows = jnp.zeros((blocks_dev, half_width), jnp.float32)
        tau_row = jnp.zeros((blocks_dev,), jnp.float32)
        state, vec_rows, tau_row = lax.fori_loop(0, blocks_dev, advance, (state, vec_rows, tau_row))
        vectors = lax.dynamic_update_slice_in_dim(vectors, vec_rows[None], sweep_index, 0)
        factors = lax.dynamic_update_slice_in_dim(factors, tau_row[None], sweep_index, 0)
        return (state, vectors, factors, sweep_index)

    def section(section_index, carry):
        state, vectors, factors = carry
        outgoing = jnp.concatenate([state[:depth], state[rows_dev : rows_dev + depth]], 0)
        padded = padded_2(outgoing, (("band", 0),), depth)
        from_prev = padded[:depth]
        from_next = padded[3 * depth :]
        take_prev = (device > 0) & section_active(device - 1, section_index - 1, sweeps)
        take_next = (section_index == 0) | section_active(device + 1, section_index - 1, sweeps)
        state = state.at[:depth].set(jnp.where(take_prev, from_prev, state[:depth]))
        state = state.at[rows_dev : rows_dev + depth].set(
            jnp.where(take_next, from_next, state[rows_dev : rows_dev + depth])
        )
        busy = section_active(device, section_index, sweeps)
        sweep_index = jnp.clip((section_index - device) // 2, 0, sweeps - 1)
        outcome = lax.cond(busy, run_sweep, keep_same, (state, vectors, factors, sweep_index))
        return (outcome[0], outcome[1], outcome[2])

    state, vectors, factors = lax.fori_loop(0, sections + 1, section, (state, vectors, factors))
    piece_count = band_diagonals.shape[0]
    band_slice = lax.dynamic_slice_in_dim(
        state[:rows_dev].T, lax.axis_index("cols") * piece_count, piece_count, 0
    )
    result = eigenvectors
    for sweep_number in reversed(range(sweeps)):
        vec_rows = vectors[sweep_number]
        tau_row = factors[sweep_number]
        lead_rows = sweep_number + 1
        fetched = from_behind(result[:half_width], "band", -1)
        extended = jnp.concatenate([result, fetched], 0)
        blocks = extended[lead_rows : lead_rows + rows_dev].reshape(blocks_dev, half_width, columns)
        inner_sums = jnp.einsum("kb,kbc->kc", vec_rows, blocks, precision=HIGHEST)
        blocks = blocks - (tau_row[:, None] * vec_rows)[:, :, None] * inner_sums[:, None, :]
        extended = extended.at[lead_rows : lead_rows + rows_dev].set(
            blocks.reshape(rows_dev, columns)
        )
        returned = from_behind(extended[rows_dev:], "band", 1)
        replace = (lax.broadcasted_iota(jnp.int32, (half_width, 1), 0) < lead_rows) & (device > 0)
        head_rows = jnp.where(replace, returned, extended[:half_width])
        result = jnp.concatenate([head_rows, extended[half_width:rows_dev]], 0)
    return (band_slice, result)


def solution(mesh):
    return jax.shard_map(
        body,
        mesh=mesh,
        in_specs=(P("cols", "band"), P("band", "cols")),
        out_specs=(P("cols", "band"), P("band", "cols")),
        check_vma=False,
    )
```

profile of v0, /device:TPU:24, one launch (start us, length us, event | category | flops | bytes accessed | tf_op | source)
XLA Modules:
  0.0 1920.6 jit_solution(2174040310176470332)
XLA Ops:
  2.1 11.2 all-to-all-start
  17.2 10.3 all-to-all-done
  27.7 1827.8 %while.55 = (s32[]{:T(128)}, f32[640,256]{1,0:T(8,128)S(1)}, f32[4,3,128]{2,1,0:T(4,128)S(1)}, f32[4,3]{1,0:T(4,128)S(1)}, s32[]{:T(128)}, /*index=5*/s32[]{:T(1...) while((s32[]{:T(128)}, f32[640,256]{1,0:T(8,128)S(1)}, ...), condition=%wide.region_12.13_spmd, body=%wide.region_0.12_spmd.sunk | while | flops 971127 | bytes 14984969 | solution.py:164
  29.7 5.3 collective-permute-done
  42.6 5.5 collective-permute-done
  55.6 5.5 collective-permute-done
  68.7 5.5 collective-permute-done
  81.7 5.5 collective-permute-done
  94.8 5.5 collective-permute-done
  107.8 5.5 collective-permute-done
  113.3 49.9 %collective-permute-start.1 = (f32[132,256]{1,0:T(8,128)S(1)}, f32[132,256]{1,0:T(8,128)S(1)}, u32[]{:S(2)}, u32[]{:S(2)}) collective-permute-start(f32[132,256]{1,0:T(8,128)S(1)} %get-tuple-element.856), channel_id=1, source_target_pairs={{16,0},{32,16},{48,32},{64,48},{80,64},{96,80},{112,96},{128,112},... | collective-permute-start | bytes 405512 | tf_op jit(solution)/shard_map/while/body/eval_jaxpr/ppermute | solution.py:35
  168.9 81.2 %collective-permute-done = f32[132,256]{1,0:T(8,128)S(1)} collective-permute-done((f32[132,256]{1,0:T(8,128)S(1)}, f32[132,256]{1,0:T(8,128)S(1)}, u32[]{:S(2)}, u32[]{:S(2)}) %collective-permute-start) | collective-permute-done | bytes 135200 | tf_op jit(solution)/shard_map/while/body/eval_jaxpr/ppermute | solution.py:34
  250.2 74.0 %collective-permute-start.1 = (f32[132,256]{1,0:T(8,128)S(1)}, f32[132,256]{1,0:T(8,128)S(1)}, u32[]{:S(2)}, u32[]{:S(2)}) collective-permute-start(f32[132,256]{1,0:T(8,128)S(1)} %get-tuple-element.856), channel_id=1, source_target_pairs={{16,0},{32,16},{48,32},{64,48},{80,64},{96,80},{112,96},{128,112},... | collective-permute-start | bytes 405512 | tf_op jit(solution)/shard_map/while/body/eval_jaxpr/ppermute | solution.py:35
  329.9 81.7 %collective-permute-done = f32[132,256]{1,0:T(8,128)S(1)} collective-permute-done((f32[132,256]{1,0:T(8,128)S(1)}, f32[132,256]{1,0:T(8,128)S(1)}, u32[]{:S(2)}, u32[]{:S(2)}) %collective-permute-start) | collective-permute-done | bytes 135200 | tf_op jit(solution)/shard_map/while/body/eval_jaxpr/ppermute | solution.py:34
  411.6 74.5 %collective-permute-start.1 = (f32[132,256]{1,0:T(8,128)S(1)}, f32[132,256]{1,0:T(8,128)S(1)}, u32[]{:S(2)}, u32[]{:S(2)}) collective-permute-start(f32[132,256]{1,0:T(8,128)S(1)} %get-tuple-element.856), channel_id=1, source_target_pairs={{16,0},{32,16},{48,32},{64,48},{80,64},{96,80},{112,96},{128,112},... | collective-permute-start | bytes 405512 | tf_op jit(solution)/shard_map/while/body/eval_jaxpr/ppermute | solution.py:35
  491.7 81.5 %collective-permute-done = f32[132,256]{1,0:T(8,128)S(1)} collective-permute-done((f32[132,256]{1,0:T(8,128)S(1)}, f32[132,256]{1,0:T(8,128)S(1)}, u32[]{:S(2)}, u32[]{:S(2)}) %collective-permute-start) | collective-permute-done | bytes 135200 | tf_op jit(solution)/shard_map/while/body/eval_jaxpr/ppermute | solution.py:34
  573.3 75.0 %collective-permute-start.1 = (f32[132,256]{1,0:T(8,128)S(1)}, f32[132,256]{1,0:T(8,128)S(1)}, u32[]{:S(2)}, u32[]{:S(2)}) collective-permute-start(f32[132,256]{1,0:T(8,128)S(1)} %get-tuple-element.856), channel_id=1, source_target_pairs={{16,0},{32,16},{48,32},{64,48},{80,64},{96,80},{112,96},{128,112},... | collective-permute-start | bytes 405512 | tf_op jit(solution)/shard_map/while/body/eval_jaxpr/ppermute | solution.py:35
  653.9 80.8 %collective-permute-done = f32[132,256]{1,0:T(8,128)S(1)} collective-permute-done((f32[132,256]{1,0:T(8,128)S(1)}, f32[132,256]{1,0:T(8,128)S(1)}, u32[]{:S(2)}, u32[]{:S(2)}) %collective-permute-start) | collective-permute-done | bytes 135200 | tf_op jit(solution)/shard_map/while/body/eval_jaxpr/ppermute | solution.py:34
  734.6 75.4 %collective-permute-start.1 = (f32[132,256]{1,0:T(8,128)S(1)}, f32[132,256]{1,0:T(8,128)S(1)}, u32[]{:S(2)}, u32[]{:S(2)}) collective-permute-start(f32[132,256]{1,0:T(8,128)S(1)} %get-tuple-element.856), channel_id=1, source_target_pairs={{16,0},{32,16},{48,32},{64,48},{80,64},{96,80},{112,96},{128,112},... | collective-permute-start | bytes 405512 | tf_op jit(solution)/shard_map/while/body/eval_jaxpr/ppermute | solution.py:35
  815.7 80.6 %collective-permute-done = f32[132,256]{1,0:T(8,128)S(1)} collective-permute-done((f32[132,256]{1,0:T(8,128)S(1)}, f32[132,256]{1,0:T(8,128)S(1)}, u32[]{:S(2)}, u32[]{:S(2)}) %collective-permute-start) | collective-permute-done | bytes 135200 | tf_op jit(solution)/shard_map/while/body/eval_jaxpr/ppermute | solution.py:34
  896.3 75.9 %collective-permute-start.1 = (f32[132,256]{1,0:T(8,128)S(1)}, f32[132,256]{1,0:T(8,128)S(1)}, u32[]{:S(2)}, u32[]{:S(2)}) collective-permute-start(f32[132,256]{1,0:T(8,128)S(1)} %get-tuple-element.856), channel_id=1, source_target_pairs={{16,0},{32,16},{48,32},{64,48},{80,64},{96,80},{112,96},{128,112},... | collective-permute-start | bytes 405512 | tf_op jit(solution)/shard_map/while/body/eval_jaxpr/ppermute | solution.py:35
  977.8 79.9 %collective-permute-done = f32[132,256]{1,0:T(8,128)S(1)} collective-permute-done((f32[132,256]{1,0:T(8,128)S(1)}, f32[132,256]{1,0:T(8,128)S(1)}, u32[]{:S(2)}, u32[]{:S(2)}) %collective-permute-start) | collective-permute-done | bytes 135200 | tf_op jit(solution)/shard_map/while/body/eval_jaxpr/ppermute | solution.py:34
  1063.3 74.4 %conditional.4 = ((f32[640,256]{1,0:T(8,128)S(1)}, f32[4,3,128]{2,1,0:T(4,128)S(1)}, f32[4,3]{1,0:T(4,128)S(1)})) conditional(s32[]{:T(128)} %convert_element_type.24, (f32[640,256]{1,0:T(8,128)S(1)}, f32[4,3,128]{2,1,0:T(4,128)S(1)}, f32[4,3]{1,0:T(4,128)S(1)}) %tuple.184, (s32[]{:T(128)}, s32[]{:T(128)}, pred[]{:T(512)}, s32[]{:T(128)}, s32[]{:T(128)}, ...), branch_computations={%region_1.1_spmd, %region_2.11_spmd} | conditional | flops 903485 | bytes 12145628 | solution.py:161
  1063.3 74.3 %while.54 = (s32[]{:T(128)}, f32[640,256]{1,0:T(8,128)S(1)}, f32[3,128]{1,0:T(4,128)S(1)}, f32[3]{0:T(128)S(1)}, s32[]{:T(128)}, /*index=5*/s32[]{:T(128)}, s32[]{:T(128)}, s32[]{:T(128)}) while((s32[]{:T(128)}, f32[640,256]{1,0:T(8,128)S(1)}, f32[3,128]{1,0:T(4,128)S(1)}, f32[3]{0:T(128)S(1)}, s32[]{:T(128)}, /*index=5*/s32[]{:T(128)}, ...), condition=%wide.region_11.10_spmd, body=%wide.region_3.0_spmd.sunk | while | flops 903471 | bytes 12139696 | solution.py:142
  1063.4 24.9 %conditional.5 = ((f32[640,256]{1,0:T(8,128)S(1)}, f32[3,128]{1,0:T(4,128)S(1)}, f32[3]{0:T(128)S(1)})) conditional(s32[]{:T(128)} %convert_element_type.25, (f32[640,256]{1,0:T(8,128)S(1)}, f32[3,128]{1,0:T(4,128)S(1)}, f32[3]{0:T(128)S(1)}) %tuple.187, (s32[]{:T(128)}, s32[]{:T(128)}, f32[640,256]{1,0:T(8,128)S(1)}, s32[]{:T(128)}, ...), branch_computations={%region_4.2_spmd, %region_5.8_spmd} | conditional | flops 903467 | bytes 12139525 | solution.py:138
  1078.5 4.3 scatter.26
  1088.3 24.9 %conditional.5 = ((f32[640,256]{1,0:T(8,128)S(1)}, f32[3,128]{1,0:T(4,128)S(1)}, f32[3]{0:T(128)S(1)})) conditional(s32[]{:T(128)} %convert_element_type.25, (f32[640,256]{1,0:T(8,128)S(1)}, f32[3,128]{1,0:T(4,128)S(1)}, f32[3]{0:T(128)S(1)}) %tuple.187, (s32[]{:T(128)}, s32[]{:T(128)}, f32[640,256]{1,0:T(8,128)S(1)}, s32[]{:T(128)}, ...), branch_computations={%region_4.2_spmd, %region_5.8_spmd} | conditional | flops 903467 | bytes 12139525 | solution.py:138
  1103.4 4.3 scatter.26
  1113.2 24.5 %conditional.5 = ((f32[640,256]{1,0:T(8,128)S(1)}, f32[3,128]{1,0:T(4,128)S(1)}, f32[3]{0:T(128)S(1)})) conditional(s32[]{:T(128)} %convert_element_type.25, (f32[640,256]{1,0:T(8,128)S(1)}, f32[3,128]{1,0:T(4,128)S(1)}, f32[3]{0:T(128)S(1)}) %tuple.187, (s32[]{:T(128)}, s32[]{:T(128)}, f32[640,256]{1,0:T(8,128)S(1)}, s32[]{:T(128)}, ...), branch_computations={%region_4.2_spmd, %region_5.8_spmd} | conditional | flops 903467 | bytes 12139525 | solution.py:138
  1128.3 4.3 scatter.26
  1139.7 5.3 collective-permute-done
  1150.6 75.4 %collective-permute-start = (f32[132,256]{1,0:T(8,128)S(1)}, f32[132,256]{1,0:T(8,128)S(1)}, u32[]{:S(2)}, u32[]{:S(2)}) collective-permute-start(f32[132,256]{1,0:T(8,128)S(1)} %slice.505), channel_id=1, source_target_pairs={{0,16},{16,32},{32,48},{48,64},{64,80},{80,96},{96,112},{112,128},... | collective-permute-start | bytes 405512 | tf_op jit(solution)/shard_map/while/body/eval_jaxpr/ppermute | solution.py:34
  1226.0 6.4 collective-permute-done
  1238.0 74.4 %conditional.4 = ((f32[640,256]{1,0:T(8,128)S(1)}, f32[4,3,128]{2,1,0:T(4,128)S(1)}, f32[4,3]{1,0:T(4,128)S(1)})) conditional(s32[]{:T(128)} %convert_element_type.24, (f32[640,256]{1,0:T(8,128)S(1)}, f32[4,3,128]{2,1,0:T(4,128)S(1)}, f32[4,3]{1,0:T(4,128)S(1)}) %tuple.184, (s32[]{:T(128)}, s32[]{:T(128)}, pred[]{:T(512)}, s32[]{:T(128)}, s32[]{:T(128)}, ...), branch_computations={%region_1.1_spmd, %region_2.11_spmd} | conditional | flops 903485 | bytes 12145628 | solution.py:161
  1238.1 74.3 %while.54 = (s32[]{:T(128)}, f32[640,256]{1,0:T(8,128)S(1)}, f32[3,128]{1,0:T(4,128)S(1)}, f32[3]{0:T(128)S(1)}, s32[]{:T(128)}, /*index=5*/s32[]{:T(128)}, s32[]{:T(128)}, s32[]{:T(128)}) while((s32[]{:T(128)}, f32[640,256]{1,0:T(8,128)S(1)}, f32[3,128]{1,0:T(4,128)S(1)}, f32[3]{0:T(128)S(1)}, s32[]{:T(128)}, /*index=5*/s32[]{:T(128)}, ...), condition=%wide.region_11.10_spmd, body=%wide.region_3.0_spmd.sunk | while | flops 903471 | bytes 12139696 | solution.py:142
  1238.1 24.9 %conditional.5 = ((f32[640,256]{1,0:T(8,128)S(1)}, f32[3,128]{1,0:T(4,128)S(1)}, f32[3]{0:T(128)S(1)})) conditional(s32[]{:T(128)} %convert_element_type.25, (f32[640,256]{1,0:T(8,128)S(1)}, f32[3,128]{1,0:T(4,128)S(1)}, f32[3]{0:T(128)S(1)}) %tuple.187, (s32[]{:T(128)}, s32[]{:T(128)}, f32[640,256]{1,0:T(8,128)S(1)}, s32[]{:T(128)}, ...), branch_computations={%region_4.2_spmd, %region_5.8_spmd} | conditional | flops 903467 | bytes 12139525 | solution.py:138
  1263.0 24.9 %conditional.5 = ((f32[640,256]{1,0:T(8,128)S(1)}, f32[3,128]{1,0:T(4,128)S(1)}, f32[3]{0:T(128)S(1)})) conditional(s32[]{:T(128)} %convert_element_type.25, (f32[640,256]{1,0:T(8,128)S(1)}, f32[3,128]{1,0:T(4,128)S(1)}, f32[3]{0:T(128)S(1)}) %tuple.187, (s32[]{:T(128)}, s32[]{:T(128)}, f32[640,256]{1,0:T(8,128)S(1)}, s32[]{:T(128)}, ...), branch_computations={%region_4.2_spmd, %region_5.8_spmd} | conditional | flops 903467 | bytes 12139525 | solution.py:138
  1287.9 24.5 %conditional.5 = ((f32[640,256]{1,0:T(8,128)S(1)}, f32[3,128]{1,0:T(4,128)S(1)}, f32[3]{0:T(128)S(1)})) conditional(s32[]{:T(128)} %convert_element_type.25, (f32[640,256]{1,0:T(8,128)S(1)}, f32[3,128]{1,0:T(4,128)S(1)}, f32[3]{0:T(128)S(1)}) %tuple.187, (s32[]{:T(128)}, s32[]{:T(128)}, f32[640,256]{1,0:T(8,128)S(1)}, s32[]{:T(128)}, ...), branch_computations={%region_4.2_spmd, %region_5.8_spmd} | conditional | flops 903467 | bytes 12139525 | solution.py:138
  1303.1 4.3 scatter.26
  1314.4 5.3 collective-permute-done
  1325.4 75.4 %collective-permute-start = (f32[132,256]{1,0:T(8,128)S(1)}, f32[132,256]{1,0:T(8,128)S(1)}, u32[]{:S(2)}, u32[]{:S(2)}) collective-permute-start(f32[132,256]{1,0:T(8,128)S(1)} %slice.505), channel_id=1, source_target_pairs={{0,16},{16,32},{32,48},{48,64},{64,80},{80,96},{96,112},{112,128},... | collective-permute-start | bytes 405512 | tf_op jit(solution)/shard_map/while/body/eval_jaxpr/ppermute | solution.py:34
  1400.8 6.4 collective-permute-done
  1412.8 74.4 %conditional.4 = ((f32[640,256]{1,0:T(8,128)S(1)}, f32[4,3,128]{2,1,0:T(4,128)S(1)}, f32[4,3]{1,0:T(4,128)S(1)})) conditional(s32[]{:T(128)} %convert_element_type.24, (f32[640,256]{1,0:T(8,128)S(1)}, f32[4,3,128]{2,1,0:T(4,128)S(1)}, f32[4,3]{1,0:T(4,128)S(1)}) %tuple.184, (s32[]{:T(128)}, s32[]{:T(128)}, pred[]{:T(512)}, s32[]{:T(128)}, s32[]{:T(128)}, ...), branch_computations={%region_1.1_spmd, %region_2.11_spmd} | conditional | flops 903485 | bytes 12145628 | solution.py:161
  1412.8 74.3 %while.54 = (s32[]{:T(128)}, f32[640,256]{1,0:T(8,128)S(1)}, f32[3,128]{1,0:T(4,128)S(1)}, f32[3]{0:T(128)S(1)}, s32[]{:T(128)}, /*index=5*/s32[]{:T(128)}, s32[]{:T(128)}, s32[]{:T(128)}) while((s32[]{:T(128)}, f32[640,256]{1,0:T(8,128)S(1)}, f32[3,128]{1,0:T(4,128)S(1)}, f32[3]{0:T(128)S(1)}, s32[]{:T(128)}, /*index=5*/s32[]{:T(128)}, ...), condition=%wide.region_11.10_spmd, body=%wide.region_3.0_spmd.sunk | while | flops 903471 | bytes 12139696 | solution.py:142
  1412.9 24.9 %conditional.5 = ((f32[640,256]{1,0:T(8,128)S(1)}, f32[3,128]{1,0:T(4,128)S(1)}, f32[3]{0:T(128)S(1)})) conditional(s32[]{:T(128)} %convert_element_type.25, (f32[640,256]{1,0:T(8,128)S(1)}, f32[3,128]{1,0:T(4,128)S(1)}, f32[3]{0:T(128)S(1)}) %tuple.187, (s32[]{:T(128)}, s32[]{:T(128)}, f32[640,256]{1,0:T(8,128)S(1)}, s32[]{:T(128)}, ...), branch_computations={%region_4.2_spmd, %region_5.8_spmd} | conditional | flops 903467 | bytes 12139525 | solution.py:138
  1437.8 24.9 %conditional.5 = ((f32[640,256]{1,0:T(8,128)S(1)}, f32[3,128]{1,0:T(4,128)S(1)}, f32[3]{0:T(128)S(1)})) conditional(s32[]{:T(128)} %convert_element_type.25, (f32[640,256]{1,0:T(8,128)S(1)}, f32[3,128]{1,0:T(4,128)S(1)}, f32[3]{0:T(128)S(1)}) %tuple.187, (s32[]{:T(128)}, s32[]{:T(128)}, f32[640,256]{1,0:T(8,128)S(1)}, s32[]{:T(128)}, ...), branch_computations={%region_4.2_spmd, %region_5.8_spmd} | conditional | flops 903467 | bytes 12139525 | solution.py:138
  1462.7 24.5 %conditional.5 = ((f32[640,256]{1,0:T(8,128)S(1)}, f32[3,128]{1,0:T(4,128)S(1)}, f32[3]{0:T(128)S(1)})) conditional(s32[]{:T(128)} %convert_element_type.25, (f32[640,256]{1,0:T(8,128)S(1)}, f32[3,128]{1,0:T(4,128)S(1)}, f32[3]{0:T(128)S(1)}) %tuple.187, (s32[]{:T(128)}, s32[]{:T(128)}, f32[640,256]{1,0:T(8,128)S(1)}, s32[]{:T(128)}, ...), branch_computations={%region_4.2_spmd, %region_5.8_spmd} | conditional | flops 903467 | bytes 12139525 | solution.py:138
  1489.2 5.3 collective-permute-done
  1500.1 75.4 %collective-permute-start = (f32[132,256]{1,0:T(8,128)S(1)}, f32[132,256]{1,0:T(8,128)S(1)}, u32[]{:S(2)}, u32[]{:S(2)}) collective-permute-start(f32[132,256]{1,0:T(8,128)S(1)} %slice.505), channel_id=1, source_target_pairs={{0,16},{16,32},{32,48},{48,64},{64,80},{80,96},{96,112},{112,128},... | collective-permute-start | bytes 405512 | tf_op jit(solution)/shard_map/while/body/eval_jaxpr/ppermute | solution.py:34
  1575.5 6.4 collective-permute-done
  1587.5 74.4 %conditional.4 = ((f32[640,256]{1,0:T(8,128)S(1)}, f32[4,3,128]{2,1,0:T(4,128)S(1)}, f32[4,3]{1,0:T(4,128)S(1)})) conditional(s32[]{:T(128)} %convert_element_type.24, (f32[640,256]{1,0:T(8,128)S(1)}, f32[4,3,128]{2,1,0:T(4,128)S(1)}, f32[4,3]{1,0:T(4,128)S(1)}) %tuple.184, (s32[]{:T(128)}, s32[]{:T(128)}, pred[]{:T(512)}, s32[]{:T(128)}, s32[]{:T(128)}, ...), branch_computations={%region_1.1_spmd, %region_2.11_spmd} | conditional | flops 903485 | bytes 12145628 | solution.py:161
  1587.6 74.3 %while.54 = (s32[]{:T(128)}, f32[640,256]{1,0:T(8,128)S(1)}, f32[3,128]{1,0:T(4,128)S(1)}, f32[3]{0:T(128)S(1)}, s32[]{:T(128)}, /*index=5*/s32[]{:T(128)}, s32[]{:T(128)}, s32[]{:T(128)}) while((s32[]{:T(128)}, f32[640,256]{1,0:T(8,128)S(1)}, f32[3,128]{1,0:T(4,128)S(1)}, f32[3]{0:T(128)S(1)}, s32[]{:T(128)}, /*index=5*/s32[]{:T(128)}, ...), condition=%wide.region_11.10_spmd, body=%wide.region_3.0_spmd.sunk | while | flops 903471 | bytes 12139696 | solution.py:142
  1587.6 24.9 %conditional.5 = ((f32[640,256]{1,0:T(8,128)S(1)}, f32[3,128]{1,0:T(4,128)S(1)}, f32[3]{0:T(128)S(1)})) conditional(s32[]{:T(128)} %convert_element_type.25, (f32[640,256]{1,0:T(8,128)S(1)}, f32[3,128]{1,0:T(4,128)S(1)}, f32[3]{0:T(128)S(1)}) %tuple.187, (s32[]{:T(128)}, s32[]{:T(128)}, f32[640,256]{1,0:T(8,128)S(1)}, s32[]{:T(128)}, ...), branch_computations={%region_4.2_spmd, %region_5.8_spmd} | conditional | flops 903467 | bytes 12139525 | solution.py:138
  1602.8 4.3 scatter.26
  1612.5 24.9 %conditional.5 = ((f32[640,256]{1,0:T(8,128)S(1)}, f32[3,128]{1,0:T(4,128)S(1)}, f32[3]{0:T(128)S(1)})) conditional(s32[]{:T(128)} %convert_element_type.25, (f32[640,256]{1,0:T(8,128)S(1)}, f32[3,128]{1,0:T(4,128)S(1)}, f32[3]{0:T(128)S(1)}) %tuple.187, (s32[]{:T(128)}, s32[]{:T(128)}, f32[640,256]{1,0:T(8,128)S(1)}, s32[]{:T(128)}, ...), branch_computations={%region_4.2_spmd, %region_5.8_spmd} | conditional | flops 903467 | bytes 12139525 | solution.py:138
  1627.7 4.3 scatter.26
  1637.4 24.5 %conditional.5 = ((f32[640,256]{1,0:T(8,128)S(1)}, f32[3,128]{1,0:T(4,128)S(1)}, f32[3]{0:T(128)S(1)})) conditional(s32[]{:T(128)} %convert_element_type.25, (f32[640,256]{1,0:T(8,128)S(1)}, f32[3,128]{1,0:T(4,128)S(1)}, f32[3]{0:T(128)S(1)}) %tuple.187, (s32[]{:T(128)}, s32[]{:T(128)}, f32[640,256]{1,0:T(8,128)S(1)}, s32[]{:T(128)}, ...), branch_computations={%region_4.2_spmd, %region_5.8_spmd} | conditional | flops 903467 | bytes 12139525 | solution.py:138
  1663.9 5.3 collective-permute-done
  1674.9 75.4 %collective-permute-start = (f32[132,256]{1,0:T(8,128)S(1)}, f32[132,256]{1,0:T(8,128)S(1)}, u32[]{:S(2)}, u32[]{:S(2)}) collective-permute-start(f32[132,256]{1,0:T(8,128)S(1)} %slice.505), channel_id=1, source_target_pairs={{0,16},{16,32},{32,48},{48,64},{64,80},{80,96},{96,112},{112,128},... | collective-permute-start | bytes 405512 | tf_op jit(solution)/shard_map/while/body/eval_jaxpr/ppermute | solution.py:34
  1756.9 5.5 collective-permute-start
  1767.4 74.1 %collective-permute-done.1 = f32[132,256]{1,0:T(8,128)S(1)} collective-permute-done((f32[132,256]{1,0:T(8,128)S(1)}, f32[132,256]{1,0:T(8,128)S(1)}, u32[]{:S(2)}, u32[]{:S(2)}) %collective-permute-start.1) | collective-permute-done | bytes 135200 | tf_op jit(solution)/shard_map/while/body/eval_jaxpr/ppermute | solution.py:35
  1842.6 6.2 collective-permute-start
  1857.0 26.0 %collective-permute-start.3 = (f32[128,128]{1,0:T(8,128)S(1)}, f32[128,128]{1,0:T(8,128)S(1)}, u32[]{:S(2)}, u32[]{:S(2)}) collective-permute-start(f32[128,128]{1,0:T(8,128)S(1)} %slice.442), channel_id=1, source_target_pairs={{0,16},{16,32},{32,48},{48,64},{64,80},{80,96},{96,112},{112,128},... | collective-permute-start | bytes 196616 | tf_op jit(solution)/shard_map/ppermute | solution.py:43
  1889.3 4.7 collective-permute-start.5
  (888 shorter events, 434.6 us)
Async XLA Ops:
  2.1 11.2 copy-start.1
  2.1 25.3 %all-to-all-start = ((f32[16,16,384]{2,1,0:T(8,128)}), f32[16,16,384]{2,1,0:T(8,128)S(1)}, u32[]{:S(2)}, u32[]{:S(2)}) async-start(f32[16,16,384]{2,1,0:T(8,128)} %broadcast_in_dim.85), calls=%async_computation | async-start | bytes 786432 | tf_op jit(solution)/shard_map/all_to_all | solution.py:20
  13.3 3.8 collective-permute-start.2
  27.7 7.3 collective-permute-start
  35.0 4.5 collective-permute-start.1
  40.6 7.4 collective-permute-start
  48.1 4.5 collective-permute-start.1
  53.7 7.4 collective-permute-start
  61.1 4.5 collective-permute-start.1
  66.7 7.4 collective-permute-start
  74.2 4.5 collective-permute-start.1
  79.8 7.4 collective-permute-start
  87.2 4.5 collective-permute-start.1
  92.8 7.4 collective-permute-start
  100.3 4.5 collective-permute-start.1
  105.9 7.4 collective-permute-start
  113.3 52.5 %collective-permute-start.1 = (f32[132,256]{1,0:T(8,128)S(1)}, f32[132,256]{1,0:T(8,128)S(1)}, u32[]{:S(2)}, u32[]{:S(2)}) collective-permute-start(f32[132,256]{1,0:T(8,128)S(1)} %get-tuple-element.856), channel_id=1, source_target_pairs={{16,0},{32,16},{48,32},{64,48},{80,64},{96,80},{112,96},{128,112},... | collective-permute-start | bytes 405512 | tf_op jit(solution)/shard_map/while/body/eval_jaxpr/ppermute | solution.py:35
  167.0 83.2 %collective-permute-start = (f32[132,256]{1,0:T(8,128)S(1)}, f32[132,256]{1,0:T(8,128)S(1)}, u32[]{:S(2)}, u32[]{:S(2)}) collective-permute-start(f32[132,256]{1,0:T(8,128)S(1)} %slice.505), channel_id=1, source_target_pairs={{0,16},{16,32},{32,48},{48,64},{64,80},{80,96},{96,112},{112,128},... | collective-permute-start | bytes 405512 | tf_op jit(solution)/shard_map/while/body/eval_jaxpr/ppermute | solution.py:34
  250.2 76.6 %collective-permute-start.1 = (f32[132,256]{1,0:T(8,128)S(1)}, f32[132,256]{1,0:T(8,128)S(1)}, u32[]{:S(2)}, u32[]{:S(2)}) collective-permute-start(f32[132,256]{1,0:T(8,128)S(1)} %get-tuple-element.856), channel_id=1, source_target_pairs={{16,0},{32,16},{48,32},{64,48},{80,64},{96,80},{112,96},{128,112},... | collective-permute-start | bytes 405512 | tf_op jit(solution)/shard_map/while/body/eval_jaxpr/ppermute | solution.py:35
  327.9 83.6 %collective-permute-start = (f32[132,256]{1,0:T(8,128)S(1)}, f32[132,256]{1,0:T(8,128)S(1)}, u32[]{:S(2)}, u32[]{:S(2)}) collective-permute-start(f32[132,256]{1,0:T(8,128)S(1)} %slice.505), channel_id=1, source_target_pairs={{0,16},{16,32},{32,48},{48,64},{64,80},{80,96},{96,112},{112,128},... | collective-permute-start | bytes 405512 | tf_op jit(solution)/shard_map/while/body/eval_jaxpr/ppermute | solution.py:34
  411.6 77.1 %collective-permute-start.1 = (f32[132,256]{1,0:T(8,128)S(1)}, f32[132,256]{1,0:T(8,128)S(1)}, u32[]{:S(2)}, u32[]{:S(2)}) collective-permute-start(f32[132,256]{1,0:T(8,128)S(1)} %get-tuple-element.856), channel_id=1, source_target_pairs={{16,0},{32,16},{48,32},{64,48},{80,64},{96,80},{112,96},{128,112},... | collective-permute-start | bytes 405512 | tf_op jit(solution)/shard_map/while/body/eval_jaxpr/ppermute | solution.py:35
  489.7 83.5 %collective-permute-start = (f32[132,256]{1,0:T(8,128)S(1)}, f32[132,256]{1,0:T(8,128)S(1)}, u32[]{:S(2)}, u32[]{:S(2)}) collective-permute-start(f32[132,256]{1,0:T(8,128)S(1)} %slice.505), channel_id=1, source_target_pairs={{0,16},{16,32},{32,48},{48,64},{64,80},{80,96},{96,112},{112,128},... | collective-permute-start | bytes 405512 | tf_op jit(solution)/shard_map/while/body/eval_jaxpr/ppermute | solution.py:34
  573.3 77.5 %collective-permute-start.1 = (f32[132,256]{1,0:T(8,128)S(1)}, f32[132,256]{1,0:T(8,128)S(1)}, u32[]{:S(2)}, u32[]{:S(2)}) collective-permute-start(f32[132,256]{1,0:T(8,128)S(1)} %get-tuple-element.856), channel_id=1, source_target_pairs={{16,0},{32,16},{48,32},{64,48},{80,64},{96,80},{112,96},{128,112},... | collective-permute-start | bytes 405512 | tf_op jit(solution)/shard_map/while/body/eval_jaxpr/ppermute | solution.py:35
  651.9 82.7 %collective-permute-start = (f32[132,256]{1,0:T(8,128)S(1)}, f32[132,256]{1,0:T(8,128)S(1)}, u32[]{:S(2)}, u32[]{:S(2)}) collective-permute-start(f32[132,256]{1,0:T(8,128)S(1)} %slice.505), channel_id=1, source_target_pairs={{0,16},{16,32},{32,48},{48,64},{64,80},{80,96},{96,112},{112,128},... | collective-permute-start | bytes 405512 | tf_op jit(solution)/shard_map/while/body/eval_jaxpr/ppermute | solution.py:34
  734.6 78.0 %collective-permute-start.1 = (f32[132,256]{1,0:T(8,128)S(1)}, f32[132,256]{1,0:T(8,128)S(1)}, u32[]{:S(2)}, u32[]{:S(2)}) collective-permute-start(f32[132,256]{1,0:T(8,128)S(1)} %get-tuple-element.856), channel_id=1, source_target_pairs={{16,0},{32,16},{48,32},{64,48},{80,64},{96,80},{112,96},{128,112},... | collective-permute-start | bytes 405512 | tf_op jit(solution)/shard_map/while/body/eval_jaxpr/ppermute | solution.py:35
  813.7 82.6 %collective-permute-start = (f32[132,256]{1,0:T(8,128)S(1)}, f32[132,256]{1,0:T(8,128)S(1)}, u32[]{:S(2)}, u32[]{:S(2)}) collective-permute-start(f32[132,256]{1,0:T(8,128)S(1)} %slice.505), channel_id=1, source_target_pairs={{0,16},{16,32},{32,48},{48,64},{64,80},{80,96},{96,112},{112,128},... | collective-permute-start | bytes 405512 | tf_op jit(solution)/shard_map/while/body/eval_jaxpr/ppermute | solution.py:34
  896.3 78.4 %collective-permute-start.1 = (f32[132,256]{1,0:T(8,128)S(1)}, f32[132,256]{1,0:T(8,128)S(1)}, u32[]{:S(2)}, u32[]{:S(2)}) collective-permute-start(f32[132,256]{1,0:T(8,128)S(1)} %get-tuple-element.856), channel_id=1, source_target_pairs={{16,0},{32,16},{48,32},{64,48},{80,64},{96,80},{112,96},{128,112},... | collective-permute-start | bytes 405512 | tf_op jit(solution)/shard_map/while/body/eval_jaxpr/ppermute | solution.py:35
  975.9 81.8 %collective-permute-start = (f32[132,256]{1,0:T(8,128)S(1)}, f32[132,256]{1,0:T(8,128)S(1)}, u32[]{:S(2)}, u32[]{:S(2)}) collective-permute-start(f32[132,256]{1,0:T(8,128)S(1)} %slice.505), channel_id=1, source_target_pairs={{0,16},{16,32},{32,48},{48,64},{64,80},{80,96},{96,112},{112,128},... | collective-permute-start | bytes 405512 | tf_op jit(solution)/shard_map/while/body/eval_jaxpr/ppermute | solution.py:34
  1057.7 4.5 collective-permute-start.1
  1072.2 0.7 copy-start.2
  1076.4 0.7 copy-start.3
  1097.1 0.7 copy-start.2
  1137.7 7.3 collective-permute-start
  1145.0 4.5 collective-permute-start.1
  1150.6 81.8 %collective-permute-start = (f32[132,256]{1,0:T(8,128)S(1)}, f32[132,256]{1,0:T(8,128)S(1)}, u32[]{:S(2)}, u32[]{:S(2)}) collective-permute-start(f32[132,256]{1,0:T(8,128)S(1)} %slice.505), channel_id=1, source_target_pairs={{0,16},{16,32},{32,48},{48,64},{64,80},{80,96},{96,112},{112,128},... | collective-permute-start | bytes 405512 | tf_op jit(solution)/shard_map/while/body/eval_jaxpr/ppermute | solution.py:34
  1232.5 4.5 collective-permute-start.1
  1276.0 0.7 copy-start.3
  1296.7 0.7 copy-start.2
  1300.9 0.7 copy-start.3
  1312.5 7.3 collective-permute-start
  1319.8 4.5 collective-permute-start.1
  1325.4 81.8 %collective-permute-start = (f32[132,256]{1,0:T(8,128)S(1)}, f32[132,256]{1,0:T(8,128)S(1)}, u32[]{:S(2)}, u32[]{:S(2)}) collective-permute-start(f32[132,256]{1,0:T(8,128)S(1)} %slice.505), channel_id=1, source_target_pairs={{0,16},{16,32},{32,48},{48,64},{64,80},{80,96},{96,112},{112,128},... | collective-permute-start | bytes 405512 | tf_op jit(solution)/shard_map/while/body/eval_jaxpr/ppermute | solution.py:34
  1407.2 4.5 collective-permute-start.1
  1487.2 7.3 collective-permute-start
  1494.5 4.5 collective-permute-start.1
  1500.1 81.8 %collective-permute-start = (f32[132,256]{1,0:T(8,128)S(1)}, f32[132,256]{1,0:T(8,128)S(1)}, u32[]{:S(2)}, u32[]{:S(2)}) collective-permute-start(f32[132,256]{1,0:T(8,128)S(1)} %slice.505), channel_id=1, source_target_pairs={{0,16},{16,32},{32,48},{48,64},{64,80},{80,96},{96,112},{112,128},... | collective-permute-start | bytes 405512 | tf_op jit(solution)/shard_map/while/body/eval_jaxpr/ppermute | solution.py:34
  1582.0 4.5 collective-permute-start.1
  1662.0 7.3 collective-permute-start
  1669.3 4.5 collective-permute-start.1
  1674.9 76.4 %collective-permute-start = (f32[132,256]{1,0:T(8,128)S(1)}, f32[132,256]{1,0:T(8,128)S(1)}, u32[]{:S(2)}, u32[]{:S(2)}) collective-permute-start(f32[132,256]{1,0:T(8,128)S(1)} %slice.505), channel_id=1, source_target_pairs={{0,16},{16,32},{32,48},{48,64},{64,80},{80,96},{96,112},{112,128},... | collective-permute-start | bytes 405512 | tf_op jit(solution)/shard_map/while/body/eval_jaxpr/ppermute | solution.py:34
  1751.3 4.5 collective-permute-start.1
  1756.9 7.4 collective-permute-start
  1764.3 77.1 %collective-permute-start.1 = (f32[132,256]{1,0:T(8,128)S(1)}, f32[132,256]{1,0:T(8,128)S(1)}, u32[]{:S(2)}, u32[]{:S(2)}) collective-permute-start(f32[132,256]{1,0:T(8,128)S(1)} %get-tuple-element.856), channel_id=1, source_target_pairs={{16,0},{32,16},{48,32},{64,48},{80,64},{96,80},{112,96},{128,112},... | collective-permute-start | bytes 405512 | tf_op jit(solution)/shard_map/while/body/eval_jaxpr/ppermute | solution.py:35
  1842.6 7.3 collective-permute-start
  1849.9 4.5 collective-permute-start.1
  1857.0 26.9 %collective-permute-start.3 = (f32[128,128]{1,0:T(8,128)S(1)}, f32[128,128]{1,0:T(8,128)S(1)}, u32[]{:S(2)}, u32[]{:S(2)}) collective-permute-start(f32[128,128]{1,0:T(8,128)S(1)} %slice.442), channel_id=1, source_target_pairs={{0,16},{16,32},{32,48},{48,64},{64,80},{80,96},{96,112},{112,128},... | collective-permute-start | bytes 196616 | tf_op jit(solution)/shard_map/ppermute | solution.py:43
  1884.0 3.8 collective-permute-start.4
  1889.3 6.5 collective-permute-start.5
  1896.0 3.8 collective-permute-start.6
  1901.3 6.5 collective-permute-start.7
  1907.9 3.8 collective-permute-start.8
  1910.1 0.8 copy-start
  1912.0 4.2 slice-start
  1913.3 6.5 collective-permute-start.9
  (18 other events, 11.9 us)
where the time goes:
time: 1920 us
  starting transfers between devices  860 us (45%)
  waiting for transfers between devices  699 us (36%)
  local copies, waits for them, and re-layouts  241 us (13%)
  other arithmetic  72 us (4%)
  loops' own time  30.9 us (2%)
    ppermute x23, waiting for transfers between devices, padded_2(): before = lax.ppermute(last, axis, up)  568 us
    ppermute x23, starting transfers between devices, padded_2(): after = lax.ppermute(first, axis, down)  457 us
    ppermute x23, starting transfers between devices, padded_2(): before = lax.ppermute(last, axis, up)  346 us
    ppermute x23, waiting for transfers between devices, padded_2(): after = lax.ppermute(first, axis, down)  106 us
    scatter x12, local copies, waits for them, and re-layouts, chase_step(): dense_rows.at[:half_width, offset:offset + double]  52 us
    ppermute x8, starting transfers between devices, from_behind(): return lax.ppermute(x, axis, pairs)  45.2 us
    another operation x72, other arithmetic  41.1 us
  transfers between devices with their start and end apart: 55, of which 55 were waited for; matrix products, arithmetic and copies ran while one was open for 1% of the time, Pallas kernels for 0%

commit v1 on v0

v1 whole, which is shorter than its diff:
```python
import jax
import jax.numpy as jnp
from jax import lax
from jax.experimental import pallas as pl
from jax.experimental.pallas import tpu as pltpu
from jax.sharding import PartitionSpec as P

SWEEPS = 4
BW = 128
OFF = 255
HALO = 512
TAIL = 8
SLOTS = 8


def lane_sum(x):
    return jnp.sum(x, axis=1, keepdims=True)


def row_sum(x):
    return jnp.sum(x, axis=0, keepdims=True)


def spread(x):
    return jnp.broadcast_to(x, (x.shape[0], BW))


def chase_kernel(place, reversed_diags, last_diag, slab, band_out, slab_out, *scratch):
    lefts = scratch[0:5]
    diags = scratch[5:10]
    kept, beneath, rows, work = scratch[10:14]
    order = reversed_diags.shape[1]
    steps = order // BW - 2
    device, slice_index = place[0], place[1]
    first_window = (device * slab_out.shape[0]) // BW - HALO // BW

    lane = lax.broadcasted_iota(jnp.int32, (BW, BW), 1)
    sub = lax.broadcasted_iota(jnp.int32, (BW, BW), 0)
    line = lax.broadcasted_iota(jnp.int32, (1, BW), 1)
    turn = (lane - sub) & (BW - 1)

    zero_block = jnp.zeros((BW, BW), jnp.float32)
    for ref in lefts + diags:
        for block in range(4):
            ref[pl.ds(block * BW, BW), :] = zero_block
    for ref in (lefts[0], diags[0]):
        start = (order + OFF) // 8 * 8
        ref[pl.ds(start, ref.shape[0] - start), :] = jnp.zeros((ref.shape[0] - start, BW), jnp.float32)
    for s in range(SWEEPS):
        beneath[s] = zero_block
        rows[s] = jnp.zeros((8, BW), jnp.float32)
        for slot in range(SLOTS):
            kept[s, slot] = zero_block

    own = (sub - 1) & (BW - 1)

    def lay_out(block, carry):
        begin = pl.multiple_of(block * BW, BW)
        tile = reversed_diags[:, pl.ds(begin, BW)].T
        tile = pltpu.roll(tile, 0, 1, stride=1, stride_axis=0)
        far = pltpu.roll(spread_rows(last_diag[:, pl.ds(begin, BW)]), BW - 1, 1)
        left = jnp.where(lane > own, tile, jnp.where(lane == own, far, 0.0))
        lefts[0][pl.ds(begin + OFF, BW), :] = left
        diags[0][pl.ds(begin + OFF, BW), :] = jnp.where(lane <= own, tile, 0.0)
        return carry

    def spread_rows(x):
        return jnp.broadcast_to(x[0:1, :], (BW, BW))

    lax.fori_loop(0, order // BW, lay_out, 0)

    def mirror(block, carry):
        at = pl.ds(pl.multiple_of(block * BW, 8), BW)
        lower = diags[0][at, :]
        diags[0][at, :] = jnp.where(lane <= sub, lower, lower.T)
        return carry

    lax.fori_loop(1, order // BW + 2, mirror, 0)

    def slot_of(window):
        index = window - first_window
        return jnp.where((index >= 0) & (index < SLOTS - 1), index, SLOTS - 1)

    def left_over(s, last):
        entries = jnp.zeros((1, BW), jnp.float32)
        for back in range(1, s + 1):
            entry = work[s - back, back : back + 1, :]
            entries = jnp.where((line == s - back) & last, entry, entries)
        return entries

    def stage(t, carry):
        for s in reversed(range(SWEEPS)):
            k = jnp.maximum(t - 2 * s, -1)
            following = t - 2 * s + 1
            base = k * BW + (s + 1 + OFF)
            here = pl.ds(base, BW)
            below = pl.ds(base + BW, BW)
            u_col = kept[s, slot_of(jnp.where(following == k + 1, k, -1000))]
            b_before = beneath[s]
            u_row = rows[s, 0:1, :]
            u_before = rows[s, 1:2, :]
            u_head = rows[s, 2:3, :]
            corner = rows[s, 3:4, :]

            low = lefts[s][below, :]
            if s > 0:
                other = rows[s - 1, 3:4, :]
                patch = jnp.where(line == s - 1, other, left_over(s - 1, k == steps - 2))
                low = jnp.where(sub == BW - 1, patch, low)
            b = lane_sum(low * u_row)
            pick = jnp.where(following == 0, (s - 1) % BW, s)
            first = lane_sum(jnp.where(lane == pick, low, 0.0))
            b = spread(b)
            x_col = spread(first) - b * u_head
            x_row = row_sum(jnp.where(turn == s, x_col, 0.0))
            x_head = x_col[0:1, :]
            rest_row = jnp.where(line == s, 0.0, x_row)
            rest = spread(lane_sum(rest_row * rest_row))
            length = jnp.sqrt(rest + x_head * x_head)
            head = x_head + length
            size = rest + head * head
            valid = (following >= 0) & (following < steps)
            scale = jnp.where(valid, jnp.sqrt(2.0 / size), 0.0)
            next_head = jnp.where(valid, scale * head, 0.0)
            next_row = scale * rest_row + jnp.where(line == s, next_head, 0.0)
            next_col = jnp.where(sub == 0, next_head, scale * x_col)
            next_corner = jnp.where(valid, -length, x_head)

            left = lefts[s][here, :] - b_before * u_before
            a_row = row_sum(u_col * left)
            left = left - u_col * a_row
            mid = diags[s][here, :]
            if s > 0:
                edge = lane_sum(jnp.where(turn == s, mid[BW - 1 : BW, :], 0.0))
                mid = jnp.where((lane == s - 1) & (sub < BW - 1), edge, mid)
            y_row = row_sum(u_col * mid)
            y_col = lane_sum(mid * u_row)
            half = 0.5 * lane_sum(u_row * y_row)
            z_row = y_row - half * u_row
            z_col = y_col - half * u_col
            mid = mid - u_col * z_row - z_col * u_row
            new_left = jnp.where(lane == s, mid, left)
            new_left = jnp.where(
                sub == 0, jnp.where(line == s, corner, left_over(s, k == steps)), new_left
            )
            new_mid = jnp.where((sub == 0) & (lane != s), left, mid)
            lefts[s + 1][here, :] = new_left
            diags[s + 1][here, :] = new_mid
            beneath[s] = b
            rows[s, 0:1, :] = next_row
            rows[s, 1:2, :] = u_row
            rows[s, 2:3, :] = next_head
            rows[s, 3:4, :] = next_corner
            kept[s, slot_of(following)] = next_col

            @pl.when(following == steps)
            def _():
                work[s] = x_col

            @pl.when(following == 1)
            def _():
                column = line == (s - 1) % BW
                cleared = jnp.where(column | (sub == 0), 0.0, new_left)
                lefts[s + 1][here, :] = cleared
                top = pl.ds(base, 1)
                diags[s + 1][top, :] = jnp.where(column, corner, new_mid[0:1, :])

        return carry

    lax.fori_loop(-1, steps + 2 * SWEEPS, stage, 0)

    count = band_out.shape[1]
    for block in range(count // BW):
        begin = device * count + block * BW
        low = lefts[4][pl.ds(begin + OFF, BW), :]
        mid = diags[4][pl.ds(begin + OFF, BW), :]
        row = begin + sub
        place_i = (row - (SWEEPS + 1)) & (BW - 1)
        place_j = (lane - SWEEPS) & (BW - 1)
        inner = jnp.where(place_j <= place_i, mid, low)
        outer = jnp.where(place_j <= place_i, low, 0.0)
        for s in range(SWEEPS):
            top = steps * BW + s + 1
            gap = (begin - top) & (BW - 1)
            tail = pltpu.roll(work[s], BW - gap, 0)
            inside = (row > steps * BW + SWEEPS) & (row < top + BW) & (lane == s)
            outer = jnp.where(inside, tail, outer)
        chosen = jnp.where(slice_index < SWEEPS * 2, inner, outer)
        chosen = pltpu.roll(chosen, 1, 1)
        for bit in range(7):
            step = 1 << bit
            chosen = jnp.where((sub & step) != 0, pltpu.roll(chosen, BW - step, 1), chosen)
        work[SWEEPS] = chosen.T
        for index in range(band_out.shape[0]):
            source = (-(slice_index * band_out.shape[0] + index)) & (BW - 1)
            band_out[index : index + 1, pl.ds(block * BW, BW)] = work[SWEEPS, pl.ds(source, 1), :]

    held = scratch[14]
    held[...] = slab[...]
    for s in reversed(range(SWEEPS)):
        for window in range(SWEEPS - 1 - s, SLOTS - 1):
            at = pl.ds(window * BW + s + 1, BW)
            block = held[at, :]
            u_col = kept[s, window]
            held[at, :] = block - u_col * row_sum(u_col * block)
    slab_out[...] = held[pl.ds(HALO, slab_out.shape[0]), :]


def run_chase(place, reversed_diags, last_diag, slab, band_shape, slab_shape):
    order = reversed_diags.shape[1]
    rows = (OFF + (order // BW + 7) * BW + 2 * BW) // 8 * 8
    vmem = pl.BlockSpec(memory_space=pltpu.VMEM)
    return pl.pallas_call(
        chase_kernel,
        out_shape=(
            jax.ShapeDtypeStruct(band_shape, jnp.float32),
            jax.ShapeDtypeStruct(slab_shape, jnp.float32),
        ),
        in_specs=[pl.BlockSpec(memory_space=pltpu.SMEM), vmem, vmem, vmem],
        out_specs=(vmem, vmem),
        scratch_shapes=[pltpu.VMEM((rows, BW), jnp.float32)] * 10
        + [
            pltpu.VMEM((SWEEPS, SLOTS, BW, BW), jnp.float32),
            pltpu.VMEM((SWEEPS, BW, BW), jnp.float32),
            pltpu.VMEM((SWEEPS, 8, BW), jnp.float32),
            pltpu.VMEM((SWEEPS + 1, BW, BW), jnp.float32),
            pltpu.VMEM((HALO + slab_shape[0] + TAIL, slab_shape[1]), jnp.float32),
        ],
        compiler_params=pltpu.CompilerParams(vmem_limit_bytes=60 << 20),
    )(place, reversed_diags, last_diag, slab)


def body(band_diagonals, eigenvectors):
    device = lax.axis_index("band")
    column = lax.axis_index("cols")
    rows_dev, columns = eigenvectors.shape
    devices = lax.axis_size("band")
    order = rows_dev * devices
    up = lambda by: [(i, i + by) for i in range(devices) if 0 <= i + by < devices]
    above_1 = lax.ppermute(eigenvectors, "band", up(1))
    above_2 = lax.ppermute(eigenvectors[rows_dev - (HALO - rows_dev) :], "band", up(2))
    beyond = lax.ppermute(eigenvectors[:TAIL], "band", up(-1))
    slab = jnp.concatenate([above_2, above_1, eigenvectors, beyond], 0)

    pieces = lax.all_gather(band_diagonals, "cols", axis=0, tiled=True)[: BW + 8]
    pieces = lax.all_gather(pieces, "band", axis=1, tiled=True)
    reversed_diags = pieces[:BW][::-1]
    last_diag = pieces[BW : BW + 8]
    place = jnp.stack([device, column]).astype(jnp.int32)

    return run_chase(place, reversed_diags, last_diag, slab, band_diagonals.shape, eigenvectors.shape)


def solution(mesh):
    return jax.shard_map(
        body,
        mesh=mesh,
        in_specs=(P("cols", "band"), P("band", "cols")),
        out_specs=(P("cols", "band"), P("band", "cols")),
        check_vma=False,
    )
```

time: 1920 us -> 187 us (0.10)
  the two profiles are of different devices: /device:TPU:24 before, /device:TPU:1 now
where the time goes in v1:
time: 187 us; the launch traced here: 186 us
  Pallas kernels  70.9 us (38%)
  blocking collectives  40.1 us (21%)
  local copies, waits for them, and re-layouts  21.6 us (12%)
  waiting for transfers between devices  21.5 us (11%)
  starting transfers between devices  15.9 us (9%)
  between operations  14.1 us (8%)
  other arithmetic  2.4 us (1%)
    pallas_call x1, Pallas kernels, run_chase(): pl.pallas_call(chase_kernel, out_shape=(jax.ShapeDtypeStruct(band_shape,...  70.9 us
    all_gather x1, blocking collectives, body(): pieces = lax.all_gather(band_diagonals, 'cols', axis=0, tiled=True)[:BW + 8]  40.1 us
    all_gather x1, waiting for transfers between devices, body(): pieces = lax.all_gather(pieces, 'band', axis=1, tiled=True)  19 us
    rev x1, local copies, waits for them, and re-layouts, body(): reversed_diags = pieces[:BW][::-1]  15.8 us
    ppermute x1, starting transfers between devices, body(): above_1 = lax.ppermute(eigenvectors, 'band', up(1))  9.89 us
    ppermute x1, starting transfers between devices, body(): lax.ppermute(eigenvectors[rows_dev - (HALO - rows_dev):], 'band', up(2))  4.04 us
  transfers between devices with their start and end apart: 4, of which 2 were waited for; matrix products, arithmetic and copies ran while one was open for 2% of the time, Pallas kernels for 0%

profile of v1, /device:TPU:1, one launch (start us, length us, event | category | flops | bytes accessed | tf_op | source)
XLA Modules:
  0.0 186.5 jit_solution(13167142477275109638)
XLA Ops:
  7.2 0.0 all-gather.2.cloned.1.call-start
  7.2 40.1 %all_gather.6 = f32[256,384]{1,0:T(8,128)S(1)} all-gather(f32[16,384]{1,0:T(8,128)} %param.2), channel_id=1, replica_groups=mesh['band'=16,'cols'=16] {'cols'}, dimensions={0}, use_global_device_ids=true | all-gather | bytes 417792 | tf_op jit(solution)/shard_map/all_gather | solution.py:245
  47.3 0.7 slice.20
  48.0 0.0 all-gather.2.cloned.1.call-update
  48.0 9.9 %collective-permute-start.1 = (f32[384,128]{1,0:T(8,128)}, f32[384,128]{1,0:T(8,128)S(1)}, u32[]{:S(2)}, u32[]{:S(2)}) collective-permute-start(f32[384,128]{1,0:T(8,128)} %param.3), channel_id=1, source_target_pairs={{0,16},{16,32},{32,48},{48,64},{64,80},{80,96},{96,112},{112,128},... | collective-permute-start | bytes 589832 | tf_op jit(solution)/shard_map/ppermute | solution.py:240
  57.9 0.7 slice.19
  58.6 1.9 %collective-permute-start.2 = (f32[8,128]{1,0:T(8,128)S(1)}, f32[8,128]{1,0:T(8,128)S(1)}, u32[]{:S(2)}, u32[]{:S(2)}) collective-permute-start(f32[8,128]{1,0:T(8,128)S(1)} %slice.19), channel_id=1, source_target_pairs={{16,0},{32,16},{48,32},{64,48},{80,64},{96,80},{112,96},{128,112},... | collective-permute-start | bytes 12296 | tf_op jit(solution)/shard_map/ppermute | solution.py:242
  60.5 0.8 slice.18
  61.4 4.0 %collective-permute-start = (f32[128,128]{1,0:T(8,128)S(1)}, f32[128,128]{1,0:T(8,128)S(1)}, u32[]{:S(2)}, u32[]{:S(2)}) collective-permute-start(f32[128,128]{1,0:T(8,128)S(1)} %slice.18), channel_id=1, source_target_pairs={{0,32},{16,48},{32,64},{48,80},{64,96},{80,112},{96,128},{112,144}... | collective-permute-start | bytes 196616 | tf_op jit(solution)/shard_map/ppermute | solution.py:241
  65.4 0.7 pad_add_fusion.place
  66.1 0.0 collective-permute-done.2
  66.1 2.5 %collective-permute-done = f32[128,128]{1,0:T(8,128)S(1)} collective-permute-done((f32[128,128]{1,0:T(8,128)S(1)}, f32[128,128]{1,0:T(8,128)S(1)}, u32[]{:S(2)}, u32[]{:S(2)}) %collective-permute-start) | collective-permute-done | bytes 65568 | tf_op jit(solution)/shard_map/ppermute | solution.py:241
  68.6 0.0 collective-permute-done.1
  68.6 1.7 pad_maximum_fusion.slab
  70.3 19.0 %all-gather.2.cloned.1.call-done = f32[136,6144]{1,0:T(8,128)} async-done(((f32[136,384]{1,0:T(8,128)}), f32[136,6144]{1,0:T(8,128)}) %all-gather.2.cloned.1.call-update) | async-done | bytes 3342352 | tf_op jit(solution)/shard_map/all_gather | solution.py:246
  89.3 0.0 slice-start
  89.3 1.9 %slice-done = f32[128,6144]{1,0:T(8,128)S(1)} async-done(((f32[136,6144]{1,0:T(8,128)}), f32[128,6144]{1,0:T(8,128)S(1)}, s32[]{:S(2)}) %slice-start) | async-done | bytes 3145752 | tf_op jit(solution)/shard_map/slice | solution.py:247
  91.2 15.8 %rev.3.reversed_diags = f32[128,6144]{1,0:T(8,128)} reverse(f32[128,6144]{1,0:T(8,128)S(1)} %slice-done), dimensions={0} | reverse | bytes 6291456 | tf_op jit(solution)/shard_map/rev | solution.py:247
  107.0 1.6 slice.22.last_diag
  108.7 70.9 %shard_map.41 = (f32[16,384]{1,0:T(8,128)}, f32[384,128]{1,0:T(8,128)}) custom-call(s32[2]{0:T(128)} %pad_add_fusion.place, f32[128,6144]{1,0:T(8,128)} %rev.3.reversed_diags, f32[8,6144]{1,0:T(8,128)} %slice.22.last_diag, f32[904,128]{1,0:T(8,128)} %pad_maximum_fusion.slab), custom_call_target="tpu_custom_call" | custom-call | tf_op jit(solution)/shard_map/pallas_call | solution.py:213
Async XLA Ops:
  7.2 82.2 %all-gather.2.cloned.1.call-start = ((), (), s32[]{:S(2)}) async-start(), calls=%async_computation | async-start | bytes 3551232 | tf_op jit(solution)/shard_map/all_gather | solution.py:246
  48.0 20.6 %collective-permute-start.1 = (f32[384,128]{1,0:T(8,128)}, f32[384,128]{1,0:T(8,128)S(1)}, u32[]{:S(2)}, u32[]{:S(2)}) collective-permute-start(f32[384,128]{1,0:T(8,128)} %param.3), channel_id=1, source_target_pairs={{0,16},{16,32},{32,48},{48,64},{64,80},{80,96},{96,112},{112,128},... | collective-permute-start | bytes 589832 | tf_op jit(solution)/shard_map/ppermute | solution.py:240
  58.6 7.5 %collective-permute-start.2 = (f32[8,128]{1,0:T(8,128)S(1)}, f32[8,128]{1,0:T(8,128)S(1)}, u32[]{:S(2)}, u32[]{:S(2)}) collective-permute-start(f32[8,128]{1,0:T(8,128)S(1)} %slice.19), channel_id=1, source_target_pairs={{16,0},{32,16},{48,32},{64,48},{80,64},{96,80},{112,96},{128,112},... | collective-permute-start | bytes 12296 | tf_op jit(solution)/shard_map/ppermute | solution.py:242
  61.4 7.2 %collective-permute-start = (f32[128,128]{1,0:T(8,128)S(1)}, f32[128,128]{1,0:T(8,128)S(1)}, u32[]{:S(2)}, u32[]{:S(2)}) collective-permute-start(f32[128,128]{1,0:T(8,128)S(1)} %slice.18), channel_id=1, source_target_pairs={{0,32},{16,48},{32,64},{48,80},{64,96},{80,112},{96,128},{112,144}... | collective-permute-start | bytes 196616 | tf_op jit(solution)/shard_map/ppermute | solution.py:241
  89.3 1.9 %slice-start = ((f32[136,6144]{1,0:T(8,128)}), f32[128,6144]{1,0:T(8,128)S(1)}, s32[]{:S(2)}) async-start(f32[136,6144]{1,0:T(8,128)} %all-gather.2.cloned.1.call-done), calls=%async_computation.1 | async-start | bytes 6291456 | tf_op jit(solution)/shard_map/slice | solution.py:247
Sparse Core Ops, SparseCore 0:
  48.1 41.1 all-gather.1

commit v2 on v1

--- a/solution.py
+++ b/solution.py
@@ -25,11 +25,13 @@
     return jnp.broadcast_to(x, (x.shape[0], BW))
 
 
-def chase_kernel(place, reversed_diags, last_diag, slab, band_out, slab_out, *scratch):
+def chase_kernel(place, segments, slab, band_out, slab_out, *scratch):
     lefts = scratch[0:5]
     diags = scratch[5:10]
-    kept, beneath, rows, work = scratch[10:14]
-    order = reversed_diags.shape[1]
+    beneath, rows, work, held = scratch[10:14]
+    kept = scratch[14:18]
+    segment = segments.shape[2] // BW
+    order = segments.shape[0] * segments.shape[2]
     steps = order // BW - 2
     device, slice_index = place[0], place[1]
     first_window = (device * slab_out.shape[0]) // BW - HALO // BW
@@ -50,22 +52,21 @@
         beneath[s] = zero_block
         rows[s] = jnp.zeros((8, BW), jnp.float32)
         for slot in range(SLOTS):
-            kept[s, slot] = zero_block
+            kept[s][slot] = zero_block
 
     own = (sub - 1) & (BW - 1)
 
     def lay_out(block, carry):
         begin = pl.multiple_of(block * BW, BW)
-        tile = reversed_diags[:, pl.ds(begin, BW)].T
+        source = pl.ds(pl.multiple_of((block % segment) * BW, BW), BW)
+        tile = segments[block // segment, 0:BW, source].T
         tile = pltpu.roll(tile, 0, 1, stride=1, stride_axis=0)
-        far = pltpu.roll(spread_rows(last_diag[:, pl.ds(begin, BW)]), BW - 1, 1)
+        far = pltpu.roll(segments[block // segment, BW : BW + 8, source], BW - 1, 1)
+        far = jnp.broadcast_to(far[7:8, :], (BW, BW))
         left = jnp.where(lane > own, tile, jnp.where(lane == own, far, 0.0))
         lefts[0][pl.ds(begin + OFF, BW), :] = left
         diags[0][pl.ds(begin + OFF, BW), :] = jnp.where(lane <= own, tile, 0.0)
         return carry
-
-    def spread_rows(x):
-        return jnp.broadcast_to(x[0:1, :], (BW, BW))
 
     lax.fori_loop(0, order // BW, lay_out, 0)
 
@@ -95,7 +96,7 @@
             base = k * BW + (s + 1 + OFF)
             here = pl.ds(base, BW)
             below = pl.ds(base + BW, BW)
-            u_col = kept[s, slot_of(jnp.where(following == k + 1, k, -1000))]
+            u_col = kept[s][slot_of(jnp.where(following == k + 1, k, -1000))]
             b_before = beneath[s]
             u_row = rows[s, 0:1, :]
             u_before = rows[s, 1:2, :]
@@ -151,19 +152,29 @@
             rows[s, 1:2, :] = u_row
             rows[s, 2:3, :] = next_head
             rows[s, 3:4, :] = next_corner
-            kept[s, slot_of(following)] = next_col
-
-            @pl.when(following == steps)
-            def _():
-                work[s] = x_col
-
-            @pl.when(following == 1)
-            def _():
-                column = line == (s - 1) % BW
-                cleared = jnp.where(column | (sub == 0), 0.0, new_left)
-                lefts[s + 1][here, :] = cleared
-                top = pl.ds(base, 1)
-                diags[s + 1][top, :] = jnp.where(column, corner, new_mid[0:1, :])
+            kept[s][slot_of(following)] = next_col
+            rows[s, 4:5, :] = corner
+
+        @pl.when((t < 2 * SWEEPS) | (t >= steps - 1))
+        def _():
+            for s in range(SWEEPS):
+                base = jnp.maximum(t - 2 * s, -1) * BW + (s + 1 + OFF)
+
+                @pl.when(t - 2 * s == steps - 1)
+                def _():
+                    low = lefts[s][pl.ds(base + BW, BW), :]
+                    low = jnp.where((lane == s) & (sub < BW - 1 + (s == 0)), low, 0.0)
+                    head = lane_sum(jnp.where(line == s, rows[s, 1:2, :], 0.0))
+                    work[s] = spread(lane_sum(low)) - beneath[s] * head
+
+                @pl.when(t == 2 * s)
+                def _():
+                    column = line == (s - 1) % BW
+                    at = pl.ds(base, BW)
+                    left = lefts[s + 1][at, :]
+                    lefts[s + 1][at, :] = jnp.where(column | (sub == 0), 0.0, left)
+                    top = pl.ds(base, 1)
+                    diags[s + 1][top, :] = jnp.where(column, rows[s, 4:5, :], diags[s + 1][top, :])
 
         return carry
 
@@ -195,19 +206,18 @@
             source = (-(slice_index * band_out.shape[0] + index)) & (BW - 1)
             band_out[index : index + 1, pl.ds(block * BW, BW)] = work[SWEEPS, pl.ds(source, 1), :]
 
-    held = scratch[14]
     held[...] = slab[...]
     for s in reversed(range(SWEEPS)):
         for window in range(SWEEPS - 1 - s, SLOTS - 1):
             at = pl.ds(window * BW + s + 1, BW)
             block = held[at, :]
-            u_col = kept[s, window]
+            u_col = kept[s][window]
             held[at, :] = block - u_col * row_sum(u_col * block)
     slab_out[...] = held[pl.ds(HALO, slab_out.shape[0]), :]
 
 
-def run_chase(place, reversed_diags, last_diag, slab, band_shape, slab_shape):
-    order = reversed_diags.shape[1]
+def run_chase(place, segments, slab, band_shape, slab_shape):
+    order = segments.shape[0] * segments.shape[2]
     rows = (OFF + (order // BW + 7) * BW + 2 * BW) // 8 * 8
     vmem = pl.BlockSpec(memory_space=pltpu.VMEM)
     return pl.pallas_call(
@@ -216,18 +226,18 @@
             jax.ShapeDtypeStruct(band_shape, jnp.float32),
             jax.ShapeDtypeStruct(slab_shape, jnp.float32),
         ),
-        in_specs=[pl.BlockSpec(memory_space=pltpu.SMEM), vmem, vmem, vmem],
+        in_specs=[pl.BlockSpec(memory_space=pltpu.SMEM), vmem, vmem],
         out_specs=(vmem, vmem),
         scratch_shapes=[pltpu.VMEM((rows, BW), jnp.float32)] * 10
         + [
-            pltpu.VMEM((SWEEPS, SLOTS, BW, BW), jnp.float32),
             pltpu.VMEM((SWEEPS, BW, BW), jnp.float32),
             pltpu.VMEM((SWEEPS, 8, BW), jnp.float32),
             pltpu.VMEM((SWEEPS + 1, BW, BW), jnp.float32),
             pltpu.VMEM((HALO + slab_shape[0] + TAIL, slab_shape[1]), jnp.float32),
-        ],
+        ]
+        + [pltpu.VMEM((SLOTS, BW, BW), jnp.float32)] * SWEEPS,
         compiler_params=pltpu.CompilerParams(vmem_limit_bytes=60 << 20),
-    )(place, reversed_diags, last_diag, slab)
+    )(place, segments, slab)
 
 
 def body(band_diagonals, eigenvectors):
@@ -242,13 +252,15 @@
     beyond = lax.ppermute(eigenvectors[:TAIL], "band", up(-1))
     slab = jnp.concatenate([above_2, above_1, eigenvectors, beyond], 0)
 
-    pieces = lax.all_gather(band_diagonals, "cols", axis=0, tiled=True)[: BW + 8]
-    pieces = lax.all_gather(pieces, "band", axis=1, tiled=True)
-    reversed_diags = pieces[:BW][::-1]
-    last_diag = pieces[BW : BW + 8]
+    peers = lax.axis_size("cols")
+    turned = band_diagonals[::-1]
+    pieces = lax.all_to_all(jnp.broadcast_to(turned[None], (peers, *turned.shape)), "cols", 0, 0, tiled=True)
+    count = BW // turned.shape[0]
+    parts = [pieces[i] for i in reversed(range(count))] + [pieces[count, -8:]]
+    segments = lax.all_gather(jnp.concatenate(parts, 0), "band", axis=0)
     place = jnp.stack([device, column]).astype(jnp.int32)
 
-    return run_chase(place, reversed_diags, last_diag, slab, band_diagonals.shape, eigenvectors.shape)
+    return run_chase(place, segments, slab, band_diagonals.shape, eigenvectors.shape)
 
 
 def solution(mesh):

time: 187 us -> 135 us (0.72)
  local copies, waits for them, and re-layouts: 21.6 us -> 3.69 us
  blocking collectives: 40.1 us -> 23.6 us
  Pallas kernels: 70.9 us -> 55.9 us
  starting transfers between devices: 15.9 us -> 11 us
  waiting for transfers between devices: 21.5 us -> 23.7 us
    all_gather x1 -> x0, blocking collectives: 40.1 us -> none  [body(): pieces = lax.all_gather(band_diagonals, 'cols', axis=0, tiled=True)[:BW + 8]]
    all_to_all x0 -> x1, blocking collectives: none -> 23.6 us  [body(): lax.all_to_all(jnp.broadcast_to(turned[None], (peers, *turned.shape)), 'c...]
    pallas_call x1, Pallas kernels: 70.9 us -> 55.9 us  [run_chase(): pl.pallas_call(chase_kernel, out_shape=(jax.ShapeDtypeStruct(band_shape,...]
    rev x1, local copies, waits for them, and re-layouts: 15.8 us -> 1.4 us  [body(): turned = band_diagonals[::-1]]
    ppermute x1, starting transfers between devices: 9.89 us -> 4.98 us  [body(): above_1 = lax.ppermute(eigenvectors, 'band', up(1))]
    slice x4 -> x0, local copies, waits for them, and re-layouts: 4.21 us -> none  [the longest x2 1.89 us: body(): reversed_diags = pieces[:BW][::-1]]
    all_gather x1, waiting for transfers between devices: 19 us -> 22.3 us  [body(): segments = lax.all_gather(jnp.concatenate(parts, 0), 'band', axis=0)]
  transfers between devices with their start and end apart: 4 -> 4, of which waited for: 2 -> 2; matrix products, arithmetic and copies ran while one was open for 2% -> 3% of each run, Pallas kernels for 0% -> 0%
where the time goes in v2:
time: 135 us; the launch traced here: 134 us
  Pallas kernels  55.9 us (41%)
  waiting for transfers between devices  23.7 us (18%)
  blocking collectives  23.6 us (17%)
  between operations  14.1 us (10%)
  starting transfers between devices  11 us (8%)
  local copies, waits for them, and re-layouts  3.69 us (3%)
  other arithmetic  2.41 us (2%)
    pallas_call x1, Pallas kernels, run_chase(): pl.pallas_call(chase_kernel, out_shape=(jax.ShapeDtypeStruct(band_shape,...  55.9 us
    all_to_all x1, blocking collectives, body(): lax.all_to_all(jnp.broadcast_to(turned[None], (peers, *turned.shape)), 'c...  23.6 us
    all_gather x1, waiting for transfers between devices, body(): segments = lax.all_gather(jnp.concatenate(parts, 0), 'band', axis=0)  22.3 us
    ppermute x1, starting transfers between devices, body(): above_1 = lax.ppermute(eigenvectors, 'band', up(1))  4.98 us
    ppermute x1, starting transfers between devices, body(): lax.ppermute(eigenvectors[rows_dev - (HALO - rows_dev):], 'band', up(2))  4.03 us
  transfers between devices with their start and end apart: 4, of which 2 were waited for; matrix products, arithmetic and copies ran while one was open for 3% of the time, Pallas kernels for 0%

profile of v2, /device:TPU:1, one launch (start us, length us, event | category | flops | bytes accessed | tf_op | source)
XLA Modules:
  0.0 134.4 jit_solution(3033990314689545929)
XLA Ops:
  7.2 0.0 all-gather.3.cloned.1.call-start
  7.2 1.4 %rev.3 = f32[16,384]{1,0:T(8,128)S(1)} reverse(f32[16,384]{1,0:T(8,128)} %param.2), dimensions={0} | reverse | bytes 49152 | tf_op jit(solution)/shard_map/rev | solution.py:256
  8.6 23.6 %all_to_all.5 = f32[16,16,384]{2,1,0:T(8,128)S(1)} all-to-all(f32[16,16,384]{2,1,0:T(8,128)S(1)} %broadcast_in_dim.2), channel_id=1, replica_groups=mesh['band'=16,'cols'=16] {'cols'}, dimensions={0} | all-to-all | bytes 786432 | tf_op jit(solution)/shard_map/all_to_all | solution.py:257
  32.3 0.0 copy-start
  32.3 0.7 copy-done
  33.0 0.0 all-gather.3.cloned.1.call-update
  33.1 5.0 %collective-permute-start.1 = (f32[384,128]{1,0:T(8,128)}, f32[384,128]{1,0:T(8,128)S(1)}, u32[]{:S(2)}, u32[]{:S(2)}) collective-permute-start(f32[384,128]{1,0:T(8,128)} %param.3), channel_id=1, source_target_pairs={{0,16},{16,32},{32,48},{48,64},{64,80},{80,96},{96,112},{112,128},... | collective-permute-start | bytes 589832 | tf_op jit(solution)/shard_map/ppermute | solution.py:250
  38.0 0.7 slice.43
  38.7 1.9 %collective-permute-start.2 = (f32[8,128]{1,0:T(8,128)S(1)}, f32[8,128]{1,0:T(8,128)S(1)}, u32[]{:S(2)}, u32[]{:S(2)}) collective-permute-start(f32[8,128]{1,0:T(8,128)S(1)} %slice.43), channel_id=1, source_target_pairs={{16,0},{32,16},{48,32},{64,48},{80,64},{96,80},{112,96},{128,112},... | collective-permute-start | bytes 12296 | tf_op jit(solution)/shard_map/ppermute | solution.py:252
  40.7 0.8 slice.42
  41.5 4.0 %collective-permute-start = (f32[128,128]{1,0:T(8,128)S(1)}, f32[128,128]{1,0:T(8,128)S(1)}, u32[]{:S(2)}, u32[]{:S(2)}) collective-permute-start(f32[128,128]{1,0:T(8,128)S(1)} %slice.42), channel_id=1, source_target_pairs={{0,32},{16,48},{32,64},{48,80},{64,96},{80,112},{96,128},{112,144}... | collective-permute-start | bytes 196616 | tf_op jit(solution)/shard_map/ppermute | solution.py:251
  45.6 0.7 pad_add_fusion.place
  46.2 0.0 collective-permute-done.2
  46.2 1.4 %collective-permute-done = f32[128,128]{1,0:T(8,128)S(1)} collective-permute-done((f32[128,128]{1,0:T(8,128)S(1)}, f32[128,128]{1,0:T(8,128)S(1)}, u32[]{:S(2)}, u32[]{:S(2)}) %collective-permute-start) | collective-permute-done | bytes 65568 | tf_op jit(solution)/shard_map/ppermute | solution.py:251
  47.7 0.0 collective-permute-done.1
  47.7 1.7 %pad_maximum_fusion.slab = f32[904,128]{1,0:T(8,128)} fusion(f32[8,128]{1,0:T(8,128)S(1)} %collective-permute-done.2, f32[384,128]{1,0:T(8,128)} %param.3, f32[384,128]{1,0:T(8,128)S(1)} %collective-permute-done.1, f32[128,128]{1,0:T(8,128)S(1)} %collective-permute-done), kind=kLoop, calls=%fused_computation | loop fusion | flops 347136 | bytes 925696 | tf_op jit(solution)/shard_map/concatenate | solution.py:253
  49.4 22.3 %all-gather.3.cloned.1.call-done = f32[2176,384]{1,0:T(8,128)} async-done(((f32[136,384]{1,0:T(8,128)}), f32[2176,384]{1,0:T(8,128)}) %all-gather.3.cloned.1.call-update) | async-done | bytes 3342352 | tf_op jit(solution)/shard_map/all_gather | solution.py:260
  71.7 55.9 %shard_map.41 = (f32[16,384]{1,0:T(8,128)}, f32[384,128]{1,0:T(8,128)}) custom-call(s32[2]{0:T(128)} %pad_add_fusion.place, f32[16,136,384]{2,1,0:T(8,128)} %bitcast.39, f32[904,128]{1,0:T(8,128)} %pad_maximum_fusion.slab), custom_call_target="tpu_custom_call" | custom-call | tf_op jit(solution)/shard_map/pallas_call | solution.py:223
  (10 shorter events, 0.1 us)
Async XLA Ops:
  7.2 64.5 %all-gather.3.cloned.1.call-start = ((), (), s32[]{:S(2)}) async-start(), calls=%async_computation.1 | async-start | bytes 3551232 | tf_op jit(solution)/shard_map/all_gather | solution.py:260
  32.3 0.7 copy-start
  33.1 14.6 %collective-permute-start.1 = (f32[384,128]{1,0:T(8,128)}, f32[384,128]{1,0:T(8,128)S(1)}, u32[]{:S(2)}, u32[]{:S(2)}) collective-permute-start(f32[384,128]{1,0:T(8,128)} %param.3), channel_id=1, source_target_pairs={{0,16},{16,32},{32,48},{48,64},{64,80},{80,96},{96,112},{112,128},... | collective-permute-start | bytes 589832 | tf_op jit(solution)/shard_map/ppermute | solution.py:250
  38.7 7.5 %collective-permute-start.2 = (f32[8,128]{1,0:T(8,128)S(1)}, f32[8,128]{1,0:T(8,128)S(1)}, u32[]{:S(2)}, u32[]{:S(2)}) collective-permute-start(f32[8,128]{1,0:T(8,128)S(1)} %slice.43), channel_id=1, source_target_pairs={{16,0},{32,16},{48,32},{64,48},{80,64},{96,80},{112,96},{128,112},... | collective-permute-start | bytes 12296 | tf_op jit(solution)/shard_map/ppermute | solution.py:252
  41.5 6.2 %collective-permute-start = (f32[128,128]{1,0:T(8,128)S(1)}, f32[128,128]{1,0:T(8,128)S(1)}, u32[]{:S(2)}, u32[]{:S(2)}) collective-permute-start(f32[128,128]{1,0:T(8,128)S(1)} %slice.42), channel_id=1, source_target_pairs={{0,32},{16,48},{32,64},{48,80},{64,96},{80,112},{96,128},{112,144}... | collective-permute-start | bytes 196616 | tf_op jit(solution)/shard_map/ppermute | solution.py:251
Sparse Core Ops, SparseCore 0:
  33.2 38.4 all-gather.2

commit v3 on v2

--- a/solution.py
+++ b/solution.py
@@ -1,3 +1,5 @@
+import functools
+
 import jax
 import jax.numpy as jnp
 from jax import lax
@@ -25,13 +27,52 @@
     return jnp.broadcast_to(x, (x.shape[0], BW))
 
 
-def chase_kernel(place, segments, slab, band_out, slab_out, *scratch):
+def in_three(x):
+    high = x.astype(jnp.bfloat16).astype(jnp.float32)
+    rest = x - high
+    middle = rest.astype(jnp.bfloat16).astype(jnp.float32)
+    return high, middle, rest - middle
+
+
+def fill(index, base, values):
+    for places, value in values:
+        mask = index == places[0]
+        for place in places[1:]:
+            mask = mask | (index == place)
+        base = jnp.where(mask, value, base)
+    return base
+
+
+def outer_sum(u, y, entering, unit):
+    index = lax.broadcasted_iota(jnp.int32, (16, BW), 0)
+    u1, u2, u3 = in_three(u)
+    left = fill(index, jnp.zeros((16, BW), jnp.float32), [((0, 1, 2), u1), ((3, 4), u2), ((5,), u3)])
+    right = fill(index, jnp.zeros((16, BW), jnp.float32), [((6, 7, 8), u1), ((9, 10), u2), ((11,), u3)])
+    if entering is not None:
+        e1, e2, e3 = in_three(entering)
+        left = fill(index, left, [((12,), e1), ((13,), e2), ((14,), e3)])
+        right = fill(index, right, [((12, 13, 14), unit)])
+    y1, y2, y3 = in_three(y)
+    left = fill(index, left, [((6, 9, 11), y1), ((7, 10), y2), ((8,), y3)])
+    right = fill(index, right, [((0, 3, 5), y1), ((1, 4), y2), ((2,), y3)])
+    return lax.dot_general(
+        left.astype(jnp.bfloat16),
+        right.astype(jnp.bfloat16),
+        (((0,), (0,)), ((), ())),
+        preferred_element_type=jnp.float32,
+    )
+
+
+def chase_kernel(kinds, *refs):
+    place, slab = refs[0:2]
+    parts = refs[2 : 2 + len(kinds)]
+    band_out, slab_out = refs[2 + len(kinds) : 4 + len(kinds)]
+    scratch = refs[4 + len(kinds) :]
     lefts = scratch[0:5]
     diags = scratch[5:10]
-    beneath, rows, work, held = scratch[10:14]
-    kept = scratch[14:18]
-    segment = segments.shape[2] // BW
-    order = segments.shape[0] * segments.shape[2]
+    beneath, rows, work, held, turned = scratch[10:15]
+    kept = scratch[15:19]
+    order = kinds[0][3]
     steps = order // BW - 2
     device, slice_index = place[0], place[1]
     first_window = (device * slab_out.shape[0]) // BW - HALO // BW
@@ -56,27 +97,33 @@
 
     own = (sub - 1) & (BW - 1)
 
-    def lay_out(block, carry):
-        begin = pl.multiple_of(block * BW, BW)
-        source = pl.ds(pl.multiple_of((block % segment) * BW, BW), BW)
-        tile = segments[block // segment, 0:BW, source].T
-        tile = pltpu.roll(tile, 0, 1, stride=1, stride_axis=0)
-        far = pltpu.roll(segments[block // segment, BW : BW + 8, source], BW - 1, 1)
-        far = jnp.broadcast_to(far[7:8, :], (BW, BW))
-        left = jnp.where(lane > own, tile, jnp.where(lane == own, far, 0.0))
-        lefts[0][pl.ds(begin + OFF, BW), :] = left
-        diags[0][pl.ds(begin + OFF, BW), :] = jnp.where(lane <= own, tile, 0.0)
+    for part, (core, side, first, _) in zip(parts, kinds):
+        length = part.shape[2]
+
+        def lay_out(index, carry):
+            owner = (index + first) * 4 + ((device & 3) ^ (2 * side + core))
+            for block in range(length // BW):
+                source = pl.ds(block * BW, BW)
+                begin = pl.multiple_of(owner * length + block * BW, BW) + OFF
+                tile = part[index, 0:BW, source].T
+                tile = pltpu.roll(tile, 0, 1, stride=1, stride_axis=0)
+                far = pltpu.roll(part[index, BW : BW + 8, source], BW - 1, 1)
+                far = jnp.broadcast_to(far[7:8, :], (BW, BW))
+                left = jnp.where(lane > own, tile, jnp.where(lane == own, far, 0.0))
+                lefts[0][pl.ds(begin, BW), :] = left
+                diags[0][pl.ds(begin, BW), :] = jnp.where(lane <= own, tile, 0.0)
+            return carry
+
+        lax.fori_loop(0, part.shape[0], lay_out, 0)
+
+    def mirror(index, carry):
+        places = [pl.ds(pl.multiple_of((index * 7 + i) * BW + BW, 8), BW) for i in range(7)]
+        lowers = [diags[0][at, :] for at in places]
+        for at, lower in zip(places, lowers):
+            diags[0][at, :] = jnp.where(lane <= sub, lower, lower.T)
         return carry
 
-    lax.fori_loop(0, order // BW, lay_out, 0)
-
-    def mirror(block, carry):
-        at = pl.ds(pl.multiple_of(block * BW, 8), BW)
-        lower = diags[0][at, :]
-        diags[0][at, :] = jnp.where(lane <= sub, lower, lower.T)
-        return carry
-
-    lax.fori_loop(1, order // BW + 2, mirror, 0)
+    lax.fori_loop(0, (order // BW + 1) // 7, mirror, 0)
 
     def slot_of(window):
         index = window - first_window
@@ -116,12 +163,13 @@
             x_row = row_sum(jnp.where(turn == s, x_col, 0.0))
             x_head = x_col[0:1, :]
             rest_row = jnp.where(line == s, 0.0, x_row)
-            rest = spread(lane_sum(rest_row * rest_row))
+            rest_col = jnp.where(sub == 0, 0.0, x_col)
+            rest = row_sum(rest_col * rest_col)
             length = jnp.sqrt(rest + x_head * x_head)
             head = x_head + length
             size = rest + head * head
             valid = (following >= 0) & (following < steps)
-            scale = jnp.where(valid, jnp.sqrt(2.0 / size), 0.0)
+            scale = jnp.where(valid, lax.rsqrt(0.5 * size), 0.0)
             next_head = jnp.where(valid, scale * head, 0.0)
             next_row = scale * rest_row + jnp.where(line == s, next_head, 0.0)
             next_col = jnp.where(sub == 0, next_head, scale * x_col)
@@ -131,15 +179,22 @@
             a_row = row_sum(u_col * left)
             left = left - u_col * a_row
             mid = diags[s][here, :]
+            y_row = row_sum(u_col * mid)
+            entering, unit = None, None
             if s > 0:
-                edge = lane_sum(jnp.where(turn == s, mid[BW - 1 : BW, :], 0.0))
-                mid = jnp.where((lane == s - 1) & (sub < BW - 1), edge, mid)
-            y_row = row_sum(u_col * mid)
-            y_col = lane_sum(mid * u_row)
-            half = 0.5 * lane_sum(u_row * y_row)
-            z_row = y_row - half * u_row
-            z_col = y_col - half * u_col
-            mid = mid - u_col * z_row - z_col * u_row
+                last_row = mid[BW - 1 : BW, :]
+                column = line == s - 1
+                y_row = jnp.where(column, lane_sum(u_row * last_row), y_row)
+                mid = jnp.where((lane == s - 1) & (sub < BW - 1), 0.0, mid)
+                entering = jnp.where(column, 0.0, last_row)
+                unit = jnp.where(column, -1.0, 0.0)
+            product = lane_sum(u_row * y_row)
+            change = outer_sum(u_row, y_row, entering, unit)
+            if s > 0:
+                turned[s, 0:BW, :] = change
+                turned[s, BW : BW + 8, :] = change[0:8, :]
+                change = turned[s, s : s + BW, :]
+            mid = mid + u_col * (product * u_row) - change
             new_left = jnp.where(lane == s, mid, left)
             new_left = jnp.where(
                 sub == 0, jnp.where(line == s, corner, left_over(s, k == steps)), new_left
@@ -216,17 +271,17 @@
     slab_out[...] = held[pl.ds(HALO, slab_out.shape[0]), :]
 
 
-def run_chase(place, segments, slab, band_shape, slab_shape):
-    order = segments.shape[0] * segments.shape[2]
+def run_chase(place, slab, parts, kinds, band_shape, slab_shape):
+    order = kinds[0][3]
     rows = (OFF + (order // BW + 7) * BW + 2 * BW) // 8 * 8
     vmem = pl.BlockSpec(memory_space=pltpu.VMEM)
     return pl.pallas_call(
-        chase_kernel,
+        functools.partial(chase_kernel, kinds),
         out_shape=(
             jax.ShapeDtypeStruct(band_shape, jnp.float32),
             jax.ShapeDtypeStruct(slab_shape, jnp.float32),
         ),
-        in_specs=[pl.BlockSpec(memory_space=pltpu.SMEM), vmem, vmem],
+        in_specs=[pl.BlockSpec(memory_space=pltpu.SMEM)] + [vmem] * (1 + len(parts)),
         out_specs=(vmem, vmem),
         scratch_shapes=[pltpu.VMEM((rows, BW), jnp.float32)] * 10
         + [
@@ -234,10 +289,11 @@
             pltpu.VMEM((SWEEPS, 8, BW), jnp.float32),
             pltpu.VMEM((SWEEPS + 1, BW, BW), jnp.float32),
             pltpu.VMEM((HALO + slab_shape[0] + TAIL, slab_shape[1]), jnp.float32),
+            pltpu.VMEM((SWEEPS, BW + 8, BW), jnp.float32),
         ]
         + [pltpu.VMEM((SLOTS, BW, BW), jnp.float32)] * SWEEPS,
         compiler_params=pltpu.CompilerParams(vmem_limit_bytes=60 << 20),
-    )(place, segments, slab)
+    )(place, slab, *parts)
 
 
 def body(band_diagonals, eigenvectors):
@@ -257,10 +313,28 @@
     pieces = lax.all_to_all(jnp.broadcast_to(turned[None], (peers, *turned.shape)), "cols", 0, 0, tiled=True)
     count = BW // turned.shape[0]
     parts = [pieces[i] for i in reversed(range(count))] + [pieces[count, -8:]]
-    segments = lax.all_gather(jnp.concatenate(parts, 0), "band", axis=0)
+    own_part = jnp.concatenate(parts, 0)
+    quarter = devices // 4
+    groups = [[y * 4 + i for y in range(quarter)] for i in range(4)]
+    part_y = lax.all_gather(own_part, "band", axis=0, axis_index_groups=groups)
+
+    def swap(x, band_bits, cols_bits):
+        pairs = [
+            (i * peers + j, (i ^ band_bits) * peers + (j ^ cols_bits))
+            for i in range(devices)
+            for j in range(peers)
+        ]
+        return lax.ppermute(x, ("band", "cols"), pairs)
+
+    half = quarter // 2
+    part_a = swap(part_y[:half], 2, 0)
+    part_b = swap(part_y[half:], 2, peers // 2)
+    parts = [part_y, part_a, part_b]
+    parts += [swap(part, 1, 0) for part in parts]
+    kinds = [(core, side, first, order) for core in (0, 1) for side, first in ((0, 0), (1, 0), (1, half))]
     place = jnp.stack([device, column]).astype(jnp.int32)
 
-    return run_chase(place, segments, slab, band_diagonals.shape, eigenvectors.shape)
+    return run_chase(place, slab, parts, kinds, band_diagonals.shape, eigenvectors.shape)
 
 
 def solution(mesh):

time: 135 us -> 105 us (0.78)
  waiting for transfers between devices: 23.7 us -> 2.21 us
  Pallas kernels: 55.9 us -> 35 us
  starting transfers between devices: 11 us -> 24.8 us
  between operations: 14.1 us -> 0.77 us
  blocking collectives: 23.6 us -> 35.2 us
    all_gather x1 -> x0, waiting for transfers between devices: 22.3 us -> none  [body(): segments = lax.all_gather(jnp.concatenate(parts, 0), 'band', axis=0)]
    pallas_call x1, Pallas kernels: 55.9 us -> 35 us  [run_chase(): pl.pallas_call(functools.partial(chase_kernel, kinds), out_shape=(jax.Sha...]
    ppermute x0 -> x5, starting transfers between devices: none -> 16 us  [swap(): return lax.ppermute(x, ('band', 'cols'), pairs)]
    all_gather x0 -> x1, blocking collectives: none -> 11.6 us  [body(): part_y = lax.all_gather(own_part, 'band', axis=0, axis_index_groups=groups)]
    ppermute x1, starting transfers between devices: 4.98 us -> 1.91 us  [body(): above_1 = lax.ppermute(eigenvectors, 'band', up(1))]
  transfers between devices with their start and end apart: 4 -> 8, of which waited for: 2 -> 2; matrix products, arithmetic and copies ran while one was open for 3% -> 3% of each run, Pallas kernels for 0% -> 0%
where the time goes in v3:
time: 105 us; the launch traced here: 104 us
  blocking collectives  35.2 us (34%)
  Pallas kernels  35 us (33%)
  starting transfers between devices  24.8 us (24%)
  local copies, waits for them, and re-layouts  4.11 us (4%)
  other arithmetic  2.41 us (2%)
  waiting for transfers between devices  2.21 us (2%)
    pallas_call x1, Pallas kernels, run_chase(): pl.pallas_call(functools.partial(chase_kernel, kinds), out_shape=(jax.Sha...  35 us
    all_to_all x1, blocking collectives, body(): lax.all_to_all(jnp.broadcast_to(turned[None], (peers, *turned.shape)), 'c...  23.6 us
    ppermute x5, starting transfers between devices, swap(): return lax.ppermute(x, ('band', 'cols'), pairs)  16 us
    all_gather x1, blocking collectives, body(): part_y = lax.all_gather(own_part, 'band', axis=0, axis_index_groups=groups)  11.6 us
    ppermute x1, starting transfers between devices, body(): lax.ppermute(eigenvectors[rows_dev - (HALO - rows_dev):], 'band', up(2))  3.89 us
    ppermute x1, starting transfers between devices, body(): beyond = lax.ppermute(eigenvectors[:TAIL], 'band', up(-1))  3.06 us
  transfers between devices with their start and end apart: 8, of which 2 were waited for; matrix products, arithmetic and copies ran while one was open for 3% of the time, Pallas kernels for 0%

profile of v3, /device:TPU:1, one launch (start us, length us, event | category | flops | bytes accessed | tf_op | source)
XLA Modules:
  0.0 104.5 jit_solution(8860549814398558239)
XLA Ops:
  0.6 1.4 %rev.3 = f32[16,384]{1,0:T(8,128)S(1)} reverse(f32[16,384]{1,0:T(8,128)} %param.2), dimensions={0} | reverse | bytes 49152 | tf_op jit(solution)/shard_map/rev | solution.py:312
  2.1 23.6 %all_to_all.5 = f32[16,16,384]{2,1,0:T(8,128)S(1)} all-to-all(f32[16,16,384]{2,1,0:T(8,128)S(1)} %broadcast_in_dim.2), channel_id=1, replica_groups=mesh['band'=16,'cols'=16] {'cols'}, dimensions={0} | all-to-all | bytes 786432 | tf_op jit(solution)/shard_map/all_to_all | solution.py:313
  25.8 11.6 %all-gather = f32[544,384]{1,0:T(8,128)S(1)} all-gather(f32[136,384]{1,0:T(8,128)S(1)} %constant_dynamic-update-slice_fusion), channel_id=2, replica_groups={{0,64,128,192},{16,80,144,208},{32,96,160,224},{48,112,176,240},{1,65,1..., dimensions={0}, use_global_device_ids=true | all-gather | bytes 1044480 | tf_op jit(solution)/shard_map/all_gather | solution.py:319
  37.3 0.0 copy-start
  37.3 0.0 copy-start.6
  37.3 0.1 fusion.8
  37.4 0.4 collective-permute-start.3
  37.8 0.3 collective-permute-start.4
  38.1 0.1 copy-done
  38.2 7.3 %collective-permute-start.5 = (f32[4,136,384]{2,1,0:T(8,128)S(1)}, f32[4,136,384]{2,1,0:T(8,128)S(1)}, u32[]{:S(2)}, u32[]{:S(2)}) collective-permute-start(f32[4,136,384]{2,1,0:T(8,128)S(1)} %bitcast.41), channel_id=1, source_target_pairs={{0,16},{1,17},{2,18},{3,19},{4,20},{5,21},{6,22},{7,23},{8,24},{9,... | collective-permute-start | bytes 2506760 | tf_op jit(solution)/shard_map/ppermute | solution.py:327
  45.6 0.0 collective-permute-done.3.refs_3_
  45.6 0.0 copy-start.2
  45.6 6.1 %collective-permute-start.6 = (f32[2,136,384]{2,1,0:T(8,128)S(1)}, f32[2,136,384]{2,1,0:T(8,128)S(1)}, u32[]{:S(2)}, u32[]{:S(2)}) collective-permute-start(f32[2,136,384]{2,1,0:T(8,128)S(1)} %collective-permute-done.3.refs_3_), channel_id=1, source_target_pairs={{0,16},{1,17},{2,18},{3,19},{4,20},{5,21},{6,22},{7,23},{8,24},{9,... | collective-permute-start | bytes 1253384 | tf_op jit(solution)/shard_map/ppermute | solution.py:327
  51.7 0.0 collective-permute-done.4.refs_4_
  51.7 0.0 copy-start.3
  51.7 1.8 %collective-permute-start.7 = (f32[2,136,384]{2,1,0:T(8,128)S(1)}, f32[2,136,384]{2,1,0:T(8,128)S(1)}, u32[]{:S(2)}, u32[]{:S(2)}) collective-permute-start(f32[2,136,384]{2,1,0:T(8,128)S(1)} %collective-permute-done.4.refs_4_), channel_id=1, source_target_pairs={{0,16},{1,17},{2,18},{3,19},{4,20},{5,21},{6,22},{7,23},{8,24},{9,... | collective-permute-start | bytes 1253384 | tf_op jit(solution)/shard_map/ppermute | solution.py:327
  53.5 0.0 copy-done.6
  53.5 1.9 %collective-permute-start.1 = (f32[384,128]{1,0:T(8,128)S(1)}, f32[384,128]{1,0:T(8,128)}, u32[]{:S(2)}, u32[]{:S(2)}) collective-permute-start(f32[384,128]{1,0:T(8,128)S(1)} %copy-done.6), channel_id=1, source_target_pairs={{0,16},{16,32},{32,48},{48,64},{64,80},{80,96},{96,112},{112,128},... | collective-permute-start | bytes 589832 | tf_op jit(solution)/shard_map/ppermute | solution.py:306
  55.4 3.1 %collective-permute-start.2 = (f32[8,128]{1,0:T(8,128)S(1)}, f32[8,128]{1,0:T(8,128)S(1)}, u32[]{:S(2)}, u32[]{:S(2)}) collective-permute-start(f32[8,128]{1,0:T(8,128)S(1)} %slice.40), channel_id=1, source_target_pairs={{16,0},{32,16},{48,32},{64,48},{80,64},{96,80},{112,96},{128,112},... | collective-permute-start | bytes 12296 | tf_op jit(solution)/shard_map/ppermute | solution.py:308
  58.5 0.6 slice.39
  59.1 1.2 %collective-permute-done.2 = f32[8,128]{1,0:T(8,128)S(1)} collective-permute-done((f32[8,128]{1,0:T(8,128)S(1)}, f32[8,128]{1,0:T(8,128)S(1)}, u32[]{:S(2)}, u32[]{:S(2)}) %collective-permute-start.2) | collective-permute-done | bytes 4128 | tf_op jit(solution)/shard_map/ppermute | solution.py:308
  60.4 3.9 %collective-permute-start = (f32[128,128]{1,0:T(8,128)}, f32[128,128]{1,0:T(8,128)S(1)}, u32[]{:S(2)}, u32[]{:S(2)}) collective-permute-start(f32[128,128]{1,0:T(8,128)} %slice.39), channel_id=1, source_target_pairs={{0,32},{16,48},{32,64},{48,80},{64,96},{80,112},{96,128},{112,144}... | collective-permute-start | bytes 196616 | tf_op jit(solution)/shard_map/ppermute | solution.py:307
  64.3 0.6 pad_add_fusion.refs_0_
  64.9 1.0 collective-permute-done
  65.9 0.0 collective-permute-done.1
  65.9 1.8 %pad_maximum_fusion.refs_1_ = f32[904,128]{1,0:T(8,128)} fusion(f32[8,128]{1,0:T(8,128)S(1)} %collective-permute-done.2, f32[384,128]{1,0:T(8,128)S(1)} %copy-done.6, f32[384,128]{1,0:T(8,128)} %collective-permute-done.1, f32[128,128]{1,0:T(8,128)S(1)} %collective-permute-done), kind=kLoop, calls=%fused_computation | loop fusion | flops 347136 | bytes 925696 | tf_op jit(solution)/shard_map/concatenate | solution.py:309
  67.7 0.0 copy-done.2
  67.7 0.0 copy-done.3
  67.7 0.0 collective-permute-done.6.refs_6_
  67.7 0.0 copy-start.4
  67.7 0.0 collective-permute-done.7.refs_7_
  67.7 0.0 copy-start.5
  67.7 0.0 collective-permute-done.5.refs_5_
  67.7 0.7 copy-done.4
  68.4 0.2 copy-done.5
  68.6 0.0 copy-start.1
  68.6 0.9 copy-done.1
  69.5 35.0 %shard_map.41 = (f32[16,384]{1,0:T(8,128)}, f32[384,128]{1,0:T(8,128)}) custom-call(s32[2]{0:T(128)} %pad_add_fusion.refs_0_, f32[904,128]{1,0:T(8,128)} %pad_maximum_fusion.refs_1_, f32[4,136,384]{2,1,0:T(8,128)} %bitcast.42, f32[2,136,384]{2,1,0:T(8,128)} %copy-done.2, f32[2,136,384]{2,1,0:T(8,128)} %copy-done.3, f32[4,136,384]{2,1,0:T(8,128)} %copy-done.1, ...), custom_call_target="tpu_custom_call" | custom-call | tf_op jit(solution)/shard_map/pallas_call | solution.py:278
  (11 shorter events, 0.1 us)
Async XLA Ops:
  37.3 0.9 copy-start
  37.3 16.2 %copy-start.6 = (f32[384,128]{1,0:T(8,128)S(1)}, f32[384,128]{1,0:T(8,128)}, u32[]{:S(2)}) copy-start(f32[384,128]{1,0:T(8,128)} %param.3) | copy-start | bytes 589828
  37.4 8.2 %collective-permute-start.3 = (f32[2,136,384]{2,1,0:T(8,128)S(1)}, f32[2,136,384]{2,1,0:T(8,128)S(1)}, u32[]{:S(2)}, u32[]{:S(2)}) collective-permute-start(f32[2,136,384]{2,1,0:T(8,128)S(1)} %bitcast.44), channel_id=1, source_target_pairs={{0,32},{1,33},{2,34},{3,35},{4,36},{5,37},{6,38},{7,39},{8,40},{9,... | collective-permute-start | bytes 1253384 | tf_op jit(solution)/shard_map/ppermute | solution.py:327
  37.8 13.9 %collective-permute-start.4 = (f32[2,136,384]{2,1,0:T(8,128)S(1)}, f32[2,136,384]{2,1,0:T(8,128)S(1)}, u32[]{:S(2)}, u32[]{:S(2)}) collective-permute-start(f32[2,136,384]{2,1,0:T(8,128)S(1)} %bitcast.43), channel_id=1, source_target_pairs={{0,40},{1,41},{2,42},{3,43},{4,44},{5,45},{6,46},{7,47},{8,32},{9,... | collective-permute-start | bytes 1253384 | tf_op jit(solution)/shard_map/ppermute | solution.py:327
  38.2 29.5 %collective-permute-start.5 = (f32[4,136,384]{2,1,0:T(8,128)S(1)}, f32[4,136,384]{2,1,0:T(8,128)S(1)}, u32[]{:S(2)}, u32[]{:S(2)}) collective-permute-start(f32[4,136,384]{2,1,0:T(8,128)S(1)} %bitcast.41), channel_id=1, source_target_pairs={{0,16},{1,17},{2,18},{3,19},{4,20},{5,21},{6,22},{7,23},{8,24},{9,... | collective-permute-start | bytes 2506760 | tf_op jit(solution)/shard_map/ppermute | solution.py:327
  45.6 22.1 %copy-start.2 = (f32[2,136,384]{2,1,0:T(8,128)}, f32[2,136,384]{2,1,0:T(8,128)S(1)}, u32[]{:S(2)}) copy-start(f32[2,136,384]{2,1,0:T(8,128)S(1)} %collective-permute-done.3.refs_3_) | copy-start | bytes 1253380
  45.6 22.1 %collective-permute-start.6 = (f32[2,136,384]{2,1,0:T(8,128)S(1)}, f32[2,136,384]{2,1,0:T(8,128)S(1)}, u32[]{:S(2)}, u32[]{:S(2)}) collective-permute-start(f32[2,136,384]{2,1,0:T(8,128)S(1)} %collective-permute-done.3.refs_3_), channel_id=1, source_target_pairs={{0,16},{1,17},{2,18},{3,19},{4,20},{5,21},{6,22},{7,23},{8,24},{9,... | collective-permute-start | bytes 1253384 | tf_op jit(solution)/shard_map/ppermute | solution.py:327
  51.7 16.0 %copy-start.3 = (f32[2,136,384]{2,1,0:T(8,128)}, f32[2,136,384]{2,1,0:T(8,128)S(1)}, u32[]{:S(2)}) copy-start(f32[2,136,384]{2,1,0:T(8,128)S(1)} %collective-permute-done.4.refs_4_) | copy-start | bytes 1253380
  51.7 16.0 %collective-permute-start.7 = (f32[2,136,384]{2,1,0:T(8,128)S(1)}, f32[2,136,384]{2,1,0:T(8,128)S(1)}, u32[]{:S(2)}, u32[]{:S(2)}) collective-permute-start(f32[2,136,384]{2,1,0:T(8,128)S(1)} %collective-permute-done.4.refs_4_), channel_id=1, source_target_pairs={{0,16},{1,17},{2,18},{3,19},{4,20},{5,21},{6,22},{7,23},{8,24},{9,... | collective-permute-start | bytes 1253384 | tf_op jit(solution)/shard_map/ppermute | solution.py:327
  53.5 12.4 %collective-permute-start.1 = (f32[384,128]{1,0:T(8,128)S(1)}, f32[384,128]{1,0:T(8,128)}, u32[]{:S(2)}, u32[]{:S(2)}) collective-permute-start(f32[384,128]{1,0:T(8,128)S(1)} %copy-done.6), channel_id=1, source_target_pairs={{0,16},{16,32},{32,48},{48,64},{64,80},{80,96},{96,112},{112,128},... | collective-permute-start | bytes 589832 | tf_op jit(solution)/shard_map/ppermute | solution.py:306
  55.4 4.9 %collective-permute-start.2 = (f32[8,128]{1,0:T(8,128)S(1)}, f32[8,128]{1,0:T(8,128)S(1)}, u32[]{:S(2)}, u32[]{:S(2)}) collective-permute-start(f32[8,128]{1,0:T(8,128)S(1)} %slice.40), channel_id=1, source_target_pairs={{16,0},{32,16},{48,32},{64,48},{80,64},{96,80},{112,96},{128,112},... | collective-permute-start | bytes 12296 | tf_op jit(solution)/shard_map/ppermute | solution.py:308
  60.4 5.5 %collective-permute-start = (f32[128,128]{1,0:T(8,128)}, f32[128,128]{1,0:T(8,128)S(1)}, u32[]{:S(2)}, u32[]{:S(2)}) collective-permute-start(f32[128,128]{1,0:T(8,128)} %slice.39), channel_id=1, source_target_pairs={{0,32},{16,48},{32,64},{48,80},{64,96},{80,112},{96,128},{112,144}... | collective-permute-start | bytes 196616 | tf_op jit(solution)/shard_map/ppermute | solution.py:307
  67.7 0.8 copy-start.4
  67.7 0.9 copy-start.5
  68.6 0.9 copy-start.1

commit v4 on v3

--- a/solution.py
+++ b/solution.py
@@ -64,10 +64,10 @@
 
 
 def chase_kernel(kinds, *refs):
-    place, slab = refs[0:2]
-    parts = refs[2 : 2 + len(kinds)]
-    band_out, slab_out = refs[2 + len(kinds) : 4 + len(kinds)]
-    scratch = refs[4 + len(kinds) :]
+    place, slabs = refs[0], refs[1:5]
+    parts = refs[5 : 5 + len(kinds)]
+    band_out, slab_out = refs[5 + len(kinds) : 7 + len(kinds)]
+    scratch = refs[7 + len(kinds) :]
     lefts = scratch[0:5]
     diags = scratch[5:10]
     beneath, rows, work, held, turned = scratch[10:15]
@@ -261,7 +261,10 @@
             source = (-(slice_index * band_out.shape[0] + index)) & (BW - 1)
             band_out[index : index + 1, pl.ds(block * BW, BW)] = work[SWEEPS, pl.ds(source, 1), :]
 
-    held[...] = slab[...]
+    begin = 0
+    for slab in slabs:
+        held[begin : begin + slab.shape[0], :] = slab[...]
+        begin += slab.shape[0]
     for s in reversed(range(SWEEPS)):
         for window in range(SWEEPS - 1 - s, SLOTS - 1):
             at = pl.ds(window * BW + s + 1, BW)
@@ -271,7 +274,7 @@
     slab_out[...] = held[pl.ds(HALO, slab_out.shape[0]), :]
 
 
-def run_chase(place, slab, parts, kinds, band_shape, slab_shape):
+def run_chase(place, slabs, parts, kinds, band_shape, slab_shape):
     order = kinds[0][3]
     rows = (OFF + (order // BW + 7) * BW + 2 * BW) // 8 * 8
     vmem = pl.BlockSpec(memory_space=pltpu.VMEM)
@@ -281,7 +284,7 @@
             jax.ShapeDtypeStruct(band_shape, jnp.float32),
             jax.ShapeDtypeStruct(slab_shape, jnp.float32),
         ),
-        in_specs=[pl.BlockSpec(memory_space=pltpu.SMEM)] + [vmem] * (1 + len(parts)),
+        in_specs=[pl.BlockSpec(memory_space=pltpu.SMEM)] + [vmem] * (len(slabs) + len(parts)),
         out_specs=(vmem, vmem),
         scratch_shapes=[pltpu.VMEM((rows, BW), jnp.float32)] * 10
         + [
@@ -293,7 +296,7 @@
         ]
         + [pltpu.VMEM((SLOTS, BW, BW), jnp.float32)] * SWEEPS,
         compiler_params=pltpu.CompilerParams(vmem_limit_bytes=60 << 20),
-    )(place, slab, *parts)
+    )(place, *slabs, *parts)
 
 
 def body(band_diagonals, eigenvectors):
@@ -306,11 +309,12 @@
     above_1 = lax.ppermute(eigenvectors, "band", up(1))
     above_2 = lax.ppermute(eigenvectors[rows_dev - (HALO - rows_dev) :], "band", up(2))
     beyond = lax.ppermute(eigenvectors[:TAIL], "band", up(-1))
-    slab = jnp.concatenate([above_2, above_1, eigenvectors, beyond], 0)
 
     peers = lax.axis_size("cols")
     turned = band_diagonals[::-1]
     pieces = lax.all_to_all(jnp.broadcast_to(turned[None], (peers, *turned.shape)), "cols", 0, 0, tiled=True)
+    pieces, above_1, above_2, beyond = lax.optimization_barrier((pieces, above_1, above_2, beyond))
+    slabs = (above_2, above_1, eigenvectors, beyond)
     count = BW // turned.shape[0]
     parts = [pieces[i] for i in reversed(range(count))] + [pieces[count, -8:]]
     own_part = jnp.concatenate(parts, 0)
@@ -334,7 +338,7 @@
     kinds = [(core, side, first, order) for core in (0, 1) for side, first in ((0, 0), (1, 0), (1, half))]
     place = jnp.stack([device, column]).astype(jnp.int32)
 
-    return run_chase(place, slab, parts, kinds, band_diagonals.shape, eigenvectors.shape)
+    return run_chase(place, slabs, parts, kinds, band_diagonals.shape, eigenvectors.shape)
 
 
 def solution(mesh):

time: 105 us -> 93.7 us (0.89)
  blocking collectives: 35.2 us -> 12.3 us
  starting transfers between devices: 24.8 us -> 35.2 us
  waiting for transfers between devices: 2.21 us -> 4.87 us
  other arithmetic: 2.41 us -> 0.58 us
    all_to_all x1 -> x0, blocking collectives: 23.6 us -> none  [body(): lax.all_to_all(jnp.broadcast_to(turned[None], (peers, *turned.shape)), 'c...]
    all_to_all x0 -> x1, starting transfers between devices: none -> 11.7 us  [body(): lax.all_to_all(jnp.broadcast_to(turned[None], (peers, *turned.shape)), 'c...]
    ppermute x1, waiting for transfers between devices: 1.21 us -> 3.4 us  [body(): beyond = lax.ppermute(eigenvectors[:TAIL], 'band', up(-1))]
    concatenate x1 -> x0, other arithmetic: 1.76 us -> none  [body(): slab = jnp.concatenate([above_2, above_1, eigenvectors, beyond], 0)]
    ppermute x5, starting transfers between devices: 16 us -> 14.5 us  [swap(): return lax.ppermute(x, ('band', 'cols'), pairs)]
    ppermute x5, waiting for transfers between devices: 0.01 us -> 1.47 us  [swap(): return lax.ppermute(x, ('band', 'cols'), pairs)]
    ppermute x1, starting transfers between devices: 1.91 us -> 3.06 us  [body(): above_1 = lax.ppermute(eigenvectors, 'band', up(1))]
    ppermute x1, starting transfers between devices: 3.06 us -> 1.92 us  [body(): beyond = lax.ppermute(eigenvectors[:TAIL], 'band', up(-1))]
  transfers between devices with their start and end apart: 8 -> 9, of which waited for: 2 -> 3; matrix products, arithmetic and copies ran while one was open for 3% -> 1% of each run, Pallas kernels for 0% -> 0%
where the time goes in v4:
time: 93.7 us; the launch traced here: 93.4 us
  starting transfers between devices  35.2 us (38%)
  Pallas kernels  35 us (37%)
  blocking collectives  12.3 us (13%)
  waiting for transfers between devices  4.87 us (5%)
  local copies, waits for them, and re-layouts  4.61 us (5%)
    pallas_call x1, Pallas kernels, run_chase(): pl.pallas_call(functools.partial(chase_kernel, kinds), out_shape=(jax.Sha...  35 us
    ppermute x5, starting transfers between devices, swap(): return lax.ppermute(x, ('band', 'cols'), pairs)  14.5 us
    all_gather x1, blocking collectives, body(): part_y = lax.all_gather(own_part, 'band', axis=0, axis_index_groups=groups)  12.3 us
    all_to_all x1, starting transfers between devices, body(): lax.all_to_all(jnp.broadcast_to(turned[None], (peers, *turned.shape)), 'c...  11.7 us
    ppermute x1, starting transfers between devices, body(): lax.ppermute(eigenvectors[rows_dev - (HALO - rows_dev):], 'band', up(2))  4.07 us
    ppermute x1, waiting for transfers between devices, body(): beyond = lax.ppermute(eigenvectors[:TAIL], 'band', up(-1))  3.4 us
    ppermute x1, starting transfers between devices, body(): above_1 = lax.ppermute(eigenvectors, 'band', up(1))  3.06 us
    unnamed x28, local copies, waits for them, and re-layouts  2.37 us
  transfers between devices with their start and end apart: 9, of which 3 were waited for; matrix products, arithmetic and copies ran while one was open for 1% of the time, Pallas kernels for 0%

profile of v4, /device:TPU:1, one launch (start us, length us, event | category | flops | bytes accessed | tf_op | source)
XLA Modules:
  0.0 93.4 jit_solution(9640099506892862686)
XLA Ops:
  0.6 1.4 %rev.3 = f32[16,384]{1,0:T(8,128)S(1)} reverse(f32[16,384]{1,0:T(8,128)} %param.2), dimensions={0} | reverse | bytes 49152 | tf_op jit(solution)/shard_map/rev | solution.py:314
  2.0 0.8 broadcast_in_dim.2
  2.8 0.0 copy-start.6
  2.8 11.7 %all-to-all-start = ((f32[16,16,384]{2,1,0:T(8,128)}), f32[16,16,384]{2,1,0:T(8,128)S(1)}, u32[]{:S(2)}, u32[]{:S(2)}) async-start(f32[16,16,384]{2,1,0:T(8,128)} %broadcast_in_dim.2), calls=%async_computation | async-start | bytes 786432 | tf_op jit(solution)/shard_map/all_to_all | solution.py:315
  14.5 0.0 copy-done.6
  14.5 3.1 %collective-permute-start = (f32[384,128]{1,0:T(8,128)S(1)}, f32[384,128]{1,0:T(8,128)S(1)}, u32[]{:S(2)}, u32[]{:S(2)}) collective-permute-start(f32[384,128]{1,0:T(8,128)S(1)} %copy-done.6), channel_id=1, source_target_pairs={{0,16},{16,32},{32,48},{48,64},{64,80},{80,96},{96,112},{112,128},... | collective-permute-start | bytes 589832 | tf_op jit(solution)/shard_map/ppermute | solution.py:309
  17.6 4.1 %collective-permute-start.1 = (f32[128,128]{1,0:T(8,128)S(1)}, f32[128,128]{1,0:T(8,128)S(1)}, u32[]{:S(2)}, u32[]{:S(2)}) collective-permute-start(f32[128,128]{1,0:T(8,128)S(1)} %slice.39), channel_id=1, source_target_pairs={{0,32},{16,48},{32,64},{48,80},{64,96},{80,112},{96,128},{112,144}... | collective-permute-start | bytes 196616 | tf_op jit(solution)/shard_map/ppermute | solution.py:310
  21.7 1.9 %collective-permute-start.2 = (f32[8,128]{1,0:T(8,128)S(1)}, f32[8,128]{1,0:T(8,128)S(1)}, u32[]{:S(2)}, u32[]{:S(2)}) collective-permute-start(f32[8,128]{1,0:T(8,128)S(1)} %slice.40), channel_id=1, source_target_pairs={{16,0},{32,16},{48,32},{64,48},{80,64},{96,80},{112,96},{128,112},... | collective-permute-start | bytes 12296 | tf_op jit(solution)/shard_map/ppermute | solution.py:311
  23.6 3.4 %collective-permute-done.2.refs_4_ = f32[8,128]{1,0:T(8,128)S(1)} collective-permute-done((f32[8,128]{1,0:T(8,128)S(1)}, f32[8,128]{1,0:T(8,128)S(1)}, u32[]{:S(2)}, u32[]{:S(2)}) %collective-permute-start.2) | collective-permute-done | bytes 4128 | tf_op jit(solution)/shard_map/ppermute | solution.py:311
  27.0 0.0 copy-start.9
  27.0 0.0 collective-permute-done.1.refs_1_
  27.0 0.0 copy-start.8
  27.0 0.0 collective-permute-done.refs_2_
  27.1 0.0 copy-start.7
  27.1 0.0 all-to-all-done
  27.1 0.5 copy-done.9
  27.6 0.0 copy-done.8
  27.7 0.0 copy-done.7
  27.8 12.3 %all-gather = f32[544,384]{1,0:T(8,128)S(1)} all-gather(f32[136,384]{1,0:T(8,128)S(1)} %constant_dynamic-update-slice_fusion), channel_id=2, replica_groups={{0,64,128,192},{16,80,144,208},{32,96,160,224},{48,112,176,240},{1,65,1..., dimensions={0}, use_global_device_ids=true | all-gather | bytes 1044480 | tf_op jit(solution)/shard_map/all_gather | solution.py:323
  40.0 0.0 copy-start
  40.0 0.1 fusion
  40.1 1.3 %collective-permute-start.3 = (f32[2,136,384]{2,1,0:T(8,128)S(1)}, f32[2,136,384]{2,1,0:T(8,128)S(1)}, u32[]{:S(2)}, u32[]{:S(2)}) collective-permute-start(f32[2,136,384]{2,1,0:T(8,128)S(1)} %bitcast.26), channel_id=1, source_target_pairs={{0,32},{1,33},{2,34},{3,35},{4,36},{5,37},{6,38},{7,39},{8,40},{9,... | collective-permute-start | bytes 1253384 | tf_op jit(solution)/shard_map/ppermute | solution.py:331
  41.4 3.2 %collective-permute-start.4 = (f32[2,136,384]{2,1,0:T(8,128)S(1)}, f32[2,136,384]{2,1,0:T(8,128)S(1)}, u32[]{:S(2)}, u32[]{:S(2)}) collective-permute-start(f32[2,136,384]{2,1,0:T(8,128)S(1)} %bitcast.25), channel_id=1, source_target_pairs={{0,40},{1,41},{2,42},{3,43},{4,44},{5,45},{6,46},{7,47},{8,32},{9,... | collective-permute-start | bytes 1253384 | tf_op jit(solution)/shard_map/ppermute | solution.py:331
  44.6 0.0 copy-done
  44.6 1.8 %collective-permute-start.5 = (f32[4,136,384]{2,1,0:T(8,128)S(1)}, f32[4,136,384]{2,1,0:T(8,128)S(1)}, u32[]{:S(2)}, u32[]{:S(2)}) collective-permute-start(f32[4,136,384]{2,1,0:T(8,128)S(1)} %bitcast.23), channel_id=1, source_target_pairs={{0,16},{1,17},{2,18},{3,19},{4,20},{5,21},{6,22},{7,23},{8,24},{9,... | collective-permute-start | bytes 2506760 | tf_op jit(solution)/shard_map/ppermute | solution.py:331
  46.4 0.7 collective-permute-done.3.refs_6_
  47.1 0.0 copy-start.2
  47.1 5.6 %collective-permute-start.6 = (f32[2,136,384]{2,1,0:T(8,128)S(1)}, f32[2,136,384]{2,1,0:T(8,128)S(1)}, u32[]{:S(2)}, u32[]{:S(2)}) collective-permute-start(f32[2,136,384]{2,1,0:T(8,128)S(1)} %collective-permute-done.3.refs_6_), channel_id=1, source_target_pairs={{0,16},{1,17},{2,18},{3,19},{4,20},{5,21},{6,22},{7,23},{8,24},{9,... | collective-permute-start | bytes 1253384 | tf_op jit(solution)/shard_map/ppermute | solution.py:331
  52.7 0.0 collective-permute-done.4.refs_7_
  52.7 0.0 copy-start.3
  52.7 2.5 %collective-permute-start.7 = (f32[2,136,384]{2,1,0:T(8,128)S(1)}, f32[2,136,384]{2,1,0:T(8,128)S(1)}, u32[]{:S(2)}, u32[]{:S(2)}) collective-permute-start(f32[2,136,384]{2,1,0:T(8,128)S(1)} %collective-permute-done.4.refs_7_), channel_id=1, source_target_pairs={{0,16},{1,17},{2,18},{3,19},{4,20},{5,21},{6,22},{7,23},{8,24},{9,... | collective-permute-start | bytes 1253384 | tf_op jit(solution)/shard_map/ppermute | solution.py:331
  55.2 0.6 pad_add_fusion.refs_0_
  55.8 0.0 collective-permute-done.6.refs_9_
  55.8 0.0 copy-start.4
  55.8 0.8 collective-permute-done.7.refs_10_
  56.6 0.0 copy-start.5
  56.6 0.0 collective-permute-done.5.refs_8_
  56.6 0.0 copy-done.2
  56.6 0.0 copy-done.3
  56.6 0.0 copy-done.4
  56.6 0.7 copy-done.5
  57.4 0.0 copy-start.1
  57.4 1.0 %copy-done.1 = f32[4,136,384]{2,1,0:T(8,128)} copy-done((f32[4,136,384]{2,1,0:T(8,128)}, f32[4,136,384]{2,1,0:T(8,128)S(1)}, u32[]{:S(2)}) %copy-start.1) | copy-done | bytes 835608
  58.3 35.0 %shard_map.41 = (f32[16,384]{1,0:T(8,128)}, f32[384,128]{1,0:T(8,128)}) custom-call(s32[2]{0:T(128)} %pad_add_fusion.refs_0_, f32[128,128]{1,0:T(8,128)} %copy-done.8, f32[384,128]{1,0:T(8,128)} %copy-done.7, f32[384,128]{1,0:T(8,128)} %refs_3_.1, f32[8,128]{1,0:T(8,128)} %copy-done.9, f32[4,136,384]{2,1,0:T(8,128)} %bitcast.24, f32[2,136,384]{2,1,0:T(8,128)} %copy-done.2, ...), custom_call_target="tpu_custom_call" | custom-call | tf_op jit(solution)/shard_map/pallas_call | solution.py:281
  (11 shorter events, 0.0 us)
Async XLA Ops:
  2.8 11.7 %copy-start.6 = (f32[384,128]{1,0:T(8,128)S(1)}, f32[384,128]{1,0:T(8,128)}, u32[]{:S(2)}) copy-start(f32[384,128]{1,0:T(8,128)} %refs_3_.1) | copy-start | bytes 589828
  2.8 24.3 %all-to-all-start = ((f32[16,16,384]{2,1,0:T(8,128)}), f32[16,16,384]{2,1,0:T(8,128)S(1)}, u32[]{:S(2)}, u32[]{:S(2)}) async-start(f32[16,16,384]{2,1,0:T(8,128)} %broadcast_in_dim.2), calls=%async_computation | async-start | bytes 786432 | tf_op jit(solution)/shard_map/all_to_all | solution.py:315
  14.5 12.5 %collective-permute-start = (f32[384,128]{1,0:T(8,128)S(1)}, f32[384,128]{1,0:T(8,128)S(1)}, u32[]{:S(2)}, u32[]{:S(2)}) collective-permute-start(f32[384,128]{1,0:T(8,128)S(1)} %copy-done.6), channel_id=1, source_target_pairs={{0,16},{16,32},{32,48},{48,64},{64,80},{80,96},{96,112},{112,128},... | collective-permute-start | bytes 589832 | tf_op jit(solution)/shard_map/ppermute | solution.py:309
  17.6 9.4 %collective-permute-start.1 = (f32[128,128]{1,0:T(8,128)S(1)}, f32[128,128]{1,0:T(8,128)S(1)}, u32[]{:S(2)}, u32[]{:S(2)}) collective-permute-start(f32[128,128]{1,0:T(8,128)S(1)} %slice.39), channel_id=1, source_target_pairs={{0,32},{16,48},{32,64},{48,80},{64,96},{80,112},{96,128},{112,144}... | collective-permute-start | bytes 196616 | tf_op jit(solution)/shard_map/ppermute | solution.py:310
  21.7 5.3 %collective-permute-start.2 = (f32[8,128]{1,0:T(8,128)S(1)}, f32[8,128]{1,0:T(8,128)S(1)}, u32[]{:S(2)}, u32[]{:S(2)}) collective-permute-start(f32[8,128]{1,0:T(8,128)S(1)} %slice.40), channel_id=1, source_target_pairs={{16,0},{32,16},{48,32},{64,48},{80,64},{96,80},{112,96},{128,112},... | collective-permute-start | bytes 12296 | tf_op jit(solution)/shard_map/ppermute | solution.py:311
  27.0 0.6 copy-start.9
  27.0 0.6 copy-start.8
  27.1 0.7 copy-start.7
  40.0 4.6 %copy-start = (f32[544,384]{1,0:T(8,128)}, f32[544,384]{1,0:T(8,128)S(1)}, u32[]{:S(2)}) copy-start(f32[544,384]{1,0:T(8,128)S(1)} %all-gather) | copy-start | bytes 2506756
  40.1 7.0 %collective-permute-start.3 = (f32[2,136,384]{2,1,0:T(8,128)S(1)}, f32[2,136,384]{2,1,0:T(8,128)S(1)}, u32[]{:S(2)}, u32[]{:S(2)}) collective-permute-start(f32[2,136,384]{2,1,0:T(8,128)S(1)} %bitcast.26), channel_id=1, source_target_pairs={{0,32},{1,33},{2,34},{3,35},{4,36},{5,37},{6,38},{7,39},{8,40},{9,... | collective-permute-start | bytes 1253384 | tf_op jit(solution)/shard_map/ppermute | solution.py:331
  41.4 11.3 %collective-permute-start.4 = (f32[2,136,384]{2,1,0:T(8,128)S(1)}, f32[2,136,384]{2,1,0:T(8,128)S(1)}, u32[]{:S(2)}, u32[]{:S(2)}) collective-permute-start(f32[2,136,384]{2,1,0:T(8,128)S(1)} %bitcast.25), channel_id=1, source_target_pairs={{0,40},{1,41},{2,42},{3,43},{4,44},{5,45},{6,46},{7,47},{8,32},{9,... | collective-permute-start | bytes 1253384 | tf_op jit(solution)/shard_map/ppermute | solution.py:331
  44.6 12.0 %collective-permute-start.5 = (f32[4,136,384]{2,1,0:T(8,128)S(1)}, f32[4,136,384]{2,1,0:T(8,128)S(1)}, u32[]{:S(2)}, u32[]{:S(2)}) collective-permute-start(f32[4,136,384]{2,1,0:T(8,128)S(1)} %bitcast.23), channel_id=1, source_target_pairs={{0,16},{1,17},{2,18},{3,19},{4,20},{5,21},{6,22},{7,23},{8,24},{9,... | collective-permute-start | bytes 2506760 | tf_op jit(solution)/shard_map/ppermute | solution.py:331
  47.1 9.5 %copy-start.2 = (f32[2,136,384]{2,1,0:T(8,128)}, f32[2,136,384]{2,1,0:T(8,128)S(1)}, u32[]{:S(2)}) copy-start(f32[2,136,384]{2,1,0:T(8,128)S(1)} %collective-permute-done.3.refs_6_) | copy-start | bytes 1253380
  47.1 8.7 %collective-permute-start.6 = (f32[2,136,384]{2,1,0:T(8,128)S(1)}, f32[2,136,384]{2,1,0:T(8,128)S(1)}, u32[]{:S(2)}, u32[]{:S(2)}) collective-permute-start(f32[2,136,384]{2,1,0:T(8,128)S(1)} %collective-permute-done.3.refs_6_), channel_id=1, source_target_pairs={{0,16},{1,17},{2,18},{3,19},{4,20},{5,21},{6,22},{7,23},{8,24},{9,... | collective-permute-start | bytes 1253384 | tf_op jit(solution)/shard_map/ppermute | solution.py:331
  52.7 3.9 %copy-start.3 = (f32[2,136,384]{2,1,0:T(8,128)}, f32[2,136,384]{2,1,0:T(8,128)S(1)}, u32[]{:S(2)}) copy-start(f32[2,136,384]{2,1,0:T(8,128)S(1)} %collective-permute-done.4.refs_7_) | copy-start | bytes 1253380
  52.7 3.9 %collective-permute-start.7 = (f32[2,136,384]{2,1,0:T(8,128)S(1)}, f32[2,136,384]{2,1,0:T(8,128)S(1)}, u32[]{:S(2)}, u32[]{:S(2)}) collective-permute-start(f32[2,136,384]{2,1,0:T(8,128)S(1)} %collective-permute-done.4.refs_7_), channel_id=1, source_target_pairs={{0,16},{1,17},{2,18},{3,19},{4,20},{5,21},{6,22},{7,23},{8,24},{9,... | collective-permute-start | bytes 1253384 | tf_op jit(solution)/shard_map/ppermute | solution.py:331
  55.8 0.8 copy-start.4
  56.6 0.8 copy-start.5
  57.4 1.0 %copy-start.1 = (f32[4,136,384]{2,1,0:T(8,128)}, f32[4,136,384]{2,1,0:T(8,128)S(1)}, u32[]{:S(2)}) copy-start(f32[4,136,384]{2,1,0:T(8,128)S(1)} %collective-permute-done.5.refs_8_) | copy-start | bytes 2506756

commit v5 on v4

--- a/solution.py
+++ b/solution.py
@@ -25,6 +25,22 @@
 
 def spread(x):
     return jnp.broadcast_to(x, (x.shape[0], BW))
+
+
+def with_first(x, row):
+    index = lax.broadcasted_iota(jnp.int32, (8, BW), 0)
+    return jnp.concatenate([jnp.where(index == 0, row, x[:8]), x[8:]], 0)
+
+
+def with_last(x, row):
+    index = lax.broadcasted_iota(jnp.int32, (8, BW), 0)
+    return jnp.concatenate([x[:-8], jnp.where(index == 7, row, x[-8:])], 0)
+
+
+def tree_sum(terms):
+    while len(terms) > 1:
+        terms = [sum(terms[i : i + 2][1:], terms[i]) for i in range(0, len(terms), 2)]
+    return terms[0]
 
 
 def in_three(x):
@@ -45,16 +61,15 @@
 
 def outer_sum(u, y, entering, unit):
     index = lax.broadcasted_iota(jnp.int32, (16, BW), 0)
+    zero = jnp.zeros((16, BW), jnp.float32)
     u1, u2, u3 = in_three(u)
-    left = fill(index, jnp.zeros((16, BW), jnp.float32), [((0, 1, 2), u1), ((3, 4), u2), ((5,), u3)])
-    right = fill(index, jnp.zeros((16, BW), jnp.float32), [((6, 7, 8), u1), ((9, 10), u2), ((11,), u3)])
+    left, right = zero, fill(index, zero, [((0, 2, 5), u1), ((1, 3), u2), ((4,), u3)])
     if entering is not None:
         e1, e2, e3 = in_three(entering)
-        left = fill(index, left, [((12,), e1), ((13,), e2), ((14,), e3)])
-        right = fill(index, right, [((12, 13, 14), unit)])
+        left = fill(index, left, [((6,), e1), ((7,), e2), ((8,), e3)])
+        right = fill(index, right, [((6, 7, 8), unit)])
     y1, y2, y3 = in_three(y)
-    left = fill(index, left, [((6, 9, 11), y1), ((7, 10), y2), ((8,), y3)])
-    right = fill(index, right, [((0, 3, 5), y1), ((1, 4), y2), ((2,), y3)])
+    left = fill(index, left, [((0, 1, 4), y1), ((2, 3), y2), ((5,), y3)])
     return lax.dot_general(
         left.astype(jnp.bfloat16),
         right.astype(jnp.bfloat16),
@@ -70,8 +85,8 @@
     scratch = refs[7 + len(kinds) :]
     lefts = scratch[0:5]
     diags = scratch[5:10]
-    beneath, rows, work, held, turned = scratch[10:15]
-    kept = scratch[15:19]
+    rows, work, held, turned = scratch[10:14]
+    kept = scratch[14:18]
     order = kinds[0][3]
     steps = order // BW - 2
     device, slice_index = place[0], place[1]
@@ -80,7 +95,7 @@
     lane = lax.broadcasted_iota(jnp.int32, (BW, BW), 1)
     sub = lax.broadcasted_iota(jnp.int32, (BW, BW), 0)
     line = lax.broadcasted_iota(jnp.int32, (1, BW), 1)
-    turn = (lane - sub) & (BW - 1)
+    turn8 = (lane[:8] - sub[:8]) & (BW - 1)
 
     zero_block = jnp.zeros((BW, BW), jnp.float32)
     for ref in lefts + diags:
@@ -90,7 +105,6 @@
         start = (order + OFF) // 8 * 8
         ref[pl.ds(start, ref.shape[0] - start), :] = jnp.zeros((ref.shape[0] - start, BW), jnp.float32)
     for s in range(SWEEPS):
-        beneath[s] = zero_block
         rows[s] = jnp.zeros((8, BW), jnp.float32)
         for slot in range(SLOTS):
             kept[s][slot] = zero_block
@@ -144,26 +158,29 @@
             here = pl.ds(base, BW)
             below = pl.ds(base + BW, BW)
             u_col = kept[s][slot_of(jnp.where(following == k + 1, k, -1000))]
-            b_before = beneath[s]
             u_row = rows[s, 0:1, :]
             u_before = rows[s, 1:2, :]
             u_head = rows[s, 2:3, :]
             corner = rows[s, 3:4, :]
-
+            b_last = rows[s, 5:6, :]
+
+            left = lefts[s][here, :]
             low = lefts[s][below, :]
             if s > 0:
                 other = rows[s - 1, 3:4, :]
                 patch = jnp.where(line == s - 1, other, left_over(s - 1, k == steps - 2))
-                low = jnp.where(sub == BW - 1, patch, low)
-            b = lane_sum(low * u_row)
+                low = with_last(low, patch)
+            b = spread(lane_sum(low * u_row))
             pick = jnp.where(following == 0, (s - 1) % BW, s)
-            first = lane_sum(jnp.where(lane == pick, low, 0.0))
-            b = spread(b)
+            first = lane_sum(jnp.where(line == pick, low, 0.0))
             x_col = spread(first) - b * u_head
-            x_row = row_sum(jnp.where(turn == s, x_col, 0.0))
+            low = low - b * u_row
+            x_row = row_sum(
+                tree_sum([jnp.where(turn8 == s + 8 * i, x_col[8 * i : 8 * i + 8], 0.0) for i in range(BW // 8)])
+            )
             x_head = x_col[0:1, :]
             rest_row = jnp.where(line == s, 0.0, x_row)
-            rest_col = jnp.where(sub == 0, 0.0, x_col)
+            rest_col = with_first(x_col, jnp.zeros((1, BW), jnp.float32))
             rest = row_sum(rest_col * rest_col)
             length = jnp.sqrt(rest + x_head * x_head)
             head = x_head + length
@@ -172,10 +189,12 @@
             scale = jnp.where(valid, lax.rsqrt(0.5 * size), 0.0)
             next_head = jnp.where(valid, scale * head, 0.0)
             next_row = scale * rest_row + jnp.where(line == s, next_head, 0.0)
-            next_col = jnp.where(sub == 0, next_head, scale * x_col)
+            next_col = with_first(scale * x_col, next_head)
             next_corner = jnp.where(valid, -length, x_head)
 
-            left = lefts[s][here, :] - b_before * u_before
+            left_last = left[BW - 1 : BW, :]
+            if s > 0:
+                left = with_last(left, left_last - b_last * u_before)
             a_row = row_sum(u_col * left)
             left = left - u_col * a_row
             mid = diags[s][here, :]
@@ -185,7 +204,7 @@
                 last_row = mid[BW - 1 : BW, :]
                 column = line == s - 1
                 y_row = jnp.where(column, lane_sum(u_row * last_row), y_row)
-                mid = jnp.where((lane == s - 1) & (sub < BW - 1), 0.0, mid)
+                mid = with_last(jnp.where(column, 0.0, mid), last_row)
                 entering = jnp.where(column, 0.0, last_row)
                 unit = jnp.where(column, -1.0, 0.0)
             product = lane_sum(u_row * y_row)
@@ -194,21 +213,20 @@
                 turned[s, 0:BW, :] = change
                 turned[s, BW : BW + 8, :] = change[0:8, :]
                 change = turned[s, s : s + BW, :]
-            mid = mid + u_col * (product * u_row) - change
-            new_left = jnp.where(lane == s, mid, left)
-            new_left = jnp.where(
-                sub == 0, jnp.where(line == s, corner, left_over(s, k == steps)), new_left
-            )
-            new_mid = jnp.where((sub == 0) & (lane != s), left, mid)
+            mid = mid - u_col * (y_row - product * u_row) - change
+            new_left = jnp.where(line == s, mid, left)
+            new_left = with_first(new_left, jnp.where(line == s, corner, left_over(s, k == steps)))
+            new_mid = with_first(mid, jnp.where(line == s, mid[0:1, :], left[0:1, :]))
+            lefts[s][below, :] = low
             lefts[s + 1][here, :] = new_left
             diags[s + 1][here, :] = new_mid
-            beneath[s] = b
             rows[s, 0:1, :] = next_row
             rows[s, 1:2, :] = u_row
             rows[s, 2:3, :] = next_head
             rows[s, 3:4, :] = next_corner
             kept[s][slot_of(following)] = next_col
             rows[s, 4:5, :] = corner
+            rows[s, 5:6, :] = b[BW - 1 : BW, :]
 
         @pl.when((t < 2 * SWEEPS) | (t >= steps - 1))
         def _():
@@ -218,9 +236,11 @@
                 @pl.when(t - 2 * s == steps - 1)
                 def _():
                     low = lefts[s][pl.ds(base + BW, BW), :]
-                    low = jnp.where((lane == s) & (sub < BW - 1 + (s == 0)), low, 0.0)
-                    head = lane_sum(jnp.where(line == s, rows[s, 1:2, :], 0.0))
-                    work[s] = spread(lane_sum(low)) - beneath[s] * head
+                    column = spread(lane_sum(jnp.where(line == s, low, 0.0)))
+                    if s > 0:
+                        head = lane_sum(jnp.where(line == s, rows[s, 1:2, :], 0.0))
+                        column = with_last(column, -rows[s, 5:6, :] * head)
+                    work[s] = column
 
                 @pl.when(t == 2 * s)
                 def _():
@@ -288,7 +308,6 @@
         out_specs=(vmem, vmem),
         scratch_shapes=[pltpu.VMEM((rows, BW), jnp.float32)] * 10
         + [
-            pltpu.VMEM((SWEEPS, BW, BW), jnp.float32),
             pltpu.VMEM((SWEEPS, 8, BW), jnp.float32),
             pltpu.VMEM((SWEEPS + 1, BW, BW), jnp.float32),
             pltpu.VMEM((HALO + slab_shape[0] + TAIL, slab_shape[1]), jnp.float32),
@@ -311,11 +330,15 @@
     beyond = lax.ppermute(eigenvectors[:TAIL], "band", up(-1))
 
     peers = lax.axis_size("cols")
-    turned = band_diagonals[::-1]
-    pieces = lax.all_to_all(jnp.broadcast_to(turned[None], (peers, *turned.shape)), "cols", 0, 0, tiled=True)
+    count_dev, length = band_diagonals.shape
+    place_in = lax.broadcasted_iota(jnp.int32, (peers * count_dev, count_dev), 0) % count_dev
+    place_of = lax.broadcasted_iota(jnp.int32, (peers * count_dev, count_dev), 1)
+    pick = jnp.where(place_in + place_of == count_dev - 1, 1.0, 0.0)
+    copies = jnp.dot(pick, band_diagonals, precision=lax.Precision.HIGHEST)
+    pieces = lax.all_to_all(copies.reshape(peers, count_dev, length), "cols", 0, 0, tiled=True)
     pieces, above_1, above_2, beyond = lax.optimization_barrier((pieces, above_1, above_2, beyond))
     slabs = (above_2, above_1, eigenvectors, beyond)
-    count = BW // turned.shape[0]
+    count = BW // count_dev
     parts = [pieces[i] for i in reversed(range(count))] + [pieces[count, -8:]]
     own_part = jnp.concatenate(parts, 0)
     quarter = devices // 4

time: 93.7 us -> 92.6 us (0.988)
  local copies, waits for them, and re-layouts: 4.61 us -> 3.11 us
  matrix products: 0 us -> 1.31 us
    rev x1 -> x0, local copies, waits for them, and re-layouts: 1.4 us -> none  [body(): turned = band_diagonals[::-1]]
    dot_general x0 -> x1, matrix products: none -> 1.31 us  [body(): copies = jnp.dot(pick, band_diagonals, precision=lax.Precision.HIGHEST)]
where the time goes in v5:
time: 92.6 us; the launch traced here: 92.3 us
  Pallas kernels  34.8 us (38%)
  starting transfers between devices  34.6 us (37%)
  blocking collectives  12.2 us (13%)
  waiting for transfers between devices  4.75 us (5%)
  local copies, waits for them, and re-layouts  3.11 us (3%)
  matrix products  1.31 us (1%)
    pallas_call x1, Pallas kernels, run_chase(): pl.pallas_call(functools.partial(chase_kernel, kinds), out_shape=(jax.Sha...  34.8 us
    ppermute x5, starting transfers between devices, swap(): return lax.ppermute(x, ('band', 'cols'), pairs)  14.5 us
    all_gather x1, blocking collectives, body(): part_y = lax.all_gather(own_part, 'band', axis=0, axis_index_groups=groups)  12.2 us
    all_to_all x1, starting transfers between devices, body(): lax.all_to_all(copies.reshape(peers, count_dev, length), 'cols', 0, 0, ti...  11 us
    ppermute x1, starting transfers between devices, body(): lax.ppermute(eigenvectors[rows_dev - (HALO - rows_dev):], 'band', up(2))  4.07 us
    ppermute x1, waiting for transfers between devices, body(): beyond = lax.ppermute(eigenvectors[:TAIL], 'band', up(-1))  3.4 us
    ppermute x1, starting transfers between devices, body(): above_1 = lax.ppermute(eigenvectors, 'band', up(1))  3.06 us
    unnamed x28, local copies, waits for them, and re-layouts  3.04 us
  transfers between devices with their start and end apart: 9, of which 3 were waited for; matrix products, arithmetic and copies ran while one was open for 1% of the time, Pallas kernels for 0%

profile of v5, /device:TPU:1, one launch (start us, length us, event | category | flops | bytes accessed | tf_op | source)
XLA Modules:
  0.0 92.3 jit_solution(18125897806038504397)
XLA Ops:
  0.6 0.0 copy-start
  0.7 0.7 copy-done
  1.4 1.3 %fusion = f32[256,384]{1,0:T(8,128)} fusion(f32[16,384]{1,0:T(8,128)S(1)} %copy-done, s32[256]{0:T(256)S(1)} %get-tuple-element.12, s32[256]{0:T(256)S(1)} %get-tuple-element.13, pred[256]{0:T(512)(128)(4,1)S(1)} %compare_and_fusion), kind=kOutput, calls=%fused_computation | convolution fusion | flops 18890752 | bytes 420096 | tf_op jit(solution)/shard_map/dot_general | solution.py:337
  2.7 0.0 copy-start.7
  2.7 11.0 %all-to-all-start = ((f32[16,16,384]{2,1,0:T(8,128)}), f32[16,16,384]{2,1,0:T(8,128)S(1)}, u32[]{:S(2)}, u32[]{:S(2)}) async-start(f32[16,16,384]{2,1,0:T(8,128)} %bitcast.2), calls=%async_computation | async-start | bytes 786432 | tf_op jit(solution)/shard_map/all_to_all | solution.py:338
  13.7 0.0 copy-done.7
  13.7 3.1 %collective-permute-start = (f32[384,128]{1,0:T(8,128)S(1)}, f32[384,128]{1,0:T(8,128)}, u32[]{:S(2)}, u32[]{:S(2)}) collective-permute-start(f32[384,128]{1,0:T(8,128)S(1)} %copy-done.7), channel_id=1, source_target_pairs={{0,16},{16,32},{32,48},{48,64},{64,80},{80,96},{96,112},{112,128},... | collective-permute-start | bytes 589832 | tf_op jit(solution)/shard_map/ppermute | solution.py:328
  16.8 4.1 %collective-permute-start.1 = (f32[128,128]{1,0:T(8,128)S(1)}, f32[128,128]{1,0:T(8,128)S(1)}, u32[]{:S(2)}, u32[]{:S(2)}) collective-permute-start(f32[128,128]{1,0:T(8,128)S(1)} %slice.39), channel_id=1, source_target_pairs={{0,32},{16,48},{32,64},{48,80},{64,96},{80,112},{96,128},{112,144}... | collective-permute-start | bytes 196616 | tf_op jit(solution)/shard_map/ppermute | solution.py:329
  20.9 1.9 %collective-permute-start.2 = (f32[8,128]{1,0:T(8,128)S(1)}, f32[8,128]{1,0:T(8,128)S(1)}, u32[]{:S(2)}, u32[]{:S(2)}) collective-permute-start(f32[8,128]{1,0:T(8,128)S(1)} %slice.40), channel_id=1, source_target_pairs={{16,0},{32,16},{48,32},{64,48},{80,64},{96,80},{112,96},{128,112},... | collective-permute-start | bytes 12296 | tf_op jit(solution)/shard_map/ppermute | solution.py:330
  22.8 3.4 %collective-permute-done.2.refs_4_ = f32[8,128]{1,0:T(8,128)S(1)} collective-permute-done((f32[8,128]{1,0:T(8,128)S(1)}, f32[8,128]{1,0:T(8,128)S(1)}, u32[]{:S(2)}, u32[]{:S(2)}) %collective-permute-start.2) | collective-permute-done | bytes 4128 | tf_op jit(solution)/shard_map/ppermute | solution.py:330
  26.2 0.0 copy-start.9
  26.2 0.0 collective-permute-done.1.refs_1_
  26.2 0.0 copy-start.8
  26.2 0.0 collective-permute-done.refs_2_
  26.2 0.0 all-to-all-done
  26.3 0.6 copy-done.9
  26.8 0.0 copy-done.8
  26.9 12.2 %all-gather = f32[544,384]{1,0:T(8,128)S(1)} all-gather(f32[136,384]{1,0:T(8,128)S(1)} %constant_dynamic-update-slice_fusion), channel_id=2, replica_groups={{0,64,128,192},{16,80,144,208},{32,96,160,224},{48,112,176,240},{1,65,1..., dimensions={0}, use_global_device_ids=true | all-gather | bytes 1044480 | tf_op jit(solution)/shard_map/all_gather | solution.py:346
  39.1 0.0 copy-start.1
  39.1 0.1 fusion.12
  39.2 1.4 %collective-permute-start.3 = (f32[2,136,384]{2,1,0:T(8,128)S(1)}, f32[2,136,384]{2,1,0:T(8,128)S(1)}, u32[]{:S(2)}, u32[]{:S(2)}) collective-permute-start(f32[2,136,384]{2,1,0:T(8,128)S(1)} %bitcast.28), channel_id=1, source_target_pairs={{0,32},{1,33},{2,34},{3,35},{4,36},{5,37},{6,38},{7,39},{8,40},{9,... | collective-permute-start | bytes 1253384 | tf_op jit(solution)/shard_map/ppermute | solution.py:354
  40.6 3.1 %collective-permute-start.4 = (f32[2,136,384]{2,1,0:T(8,128)S(1)}, f32[2,136,384]{2,1,0:T(8,128)S(1)}, u32[]{:S(2)}, u32[]{:S(2)}) collective-permute-start(f32[2,136,384]{2,1,0:T(8,128)S(1)} %bitcast.27), channel_id=1, source_target_pairs={{0,40},{1,41},{2,42},{3,43},{4,44},{5,45},{6,46},{7,47},{8,32},{9,... | collective-permute-start | bytes 1253384 | tf_op jit(solution)/shard_map/ppermute | solution.py:354
  43.7 0.0 copy-done.1
  43.7 1.8 %collective-permute-start.5 = (f32[4,136,384]{2,1,0:T(8,128)S(1)}, f32[4,136,384]{2,1,0:T(8,128)S(1)}, u32[]{:S(2)}, u32[]{:S(2)}) collective-permute-start(f32[4,136,384]{2,1,0:T(8,128)S(1)} %bitcast.25), channel_id=1, source_target_pairs={{0,16},{1,17},{2,18},{3,19},{4,20},{5,21},{6,22},{7,23},{8,24},{9,... | collective-permute-start | bytes 2506760 | tf_op jit(solution)/shard_map/ppermute | solution.py:354
  45.6 0.6 collective-permute-done.3.refs_6_
  46.2 0.0 copy-start.3
  46.2 5.7 %collective-permute-start.6 = (f32[2,136,384]{2,1,0:T(8,128)S(1)}, f32[2,136,384]{2,1,0:T(8,128)S(1)}, u32[]{:S(2)}, u32[]{:S(2)}) collective-permute-start(f32[2,136,384]{2,1,0:T(8,128)S(1)} %collective-permute-done.3.refs_6_), channel_id=1, source_target_pairs={{0,16},{1,17},{2,18},{3,19},{4,20},{5,21},{6,22},{7,23},{8,24},{9,... | collective-permute-start | bytes 1253384 | tf_op jit(solution)/shard_map/ppermute | solution.py:354
  51.9 0.0 collective-permute-done.4.refs_7_
  51.9 0.0 copy-start.4
  51.9 2.4 %collective-permute-start.7 = (f32[2,136,384]{2,1,0:T(8,128)S(1)}, f32[2,136,384]{2,1,0:T(8,128)S(1)}, u32[]{:S(2)}, u32[]{:S(2)}) collective-permute-start(f32[2,136,384]{2,1,0:T(8,128)S(1)} %collective-permute-done.4.refs_7_), channel_id=1, source_target_pairs={{0,16},{1,17},{2,18},{3,19},{4,20},{5,21},{6,22},{7,23},{8,24},{9,... | collective-permute-start | bytes 1253384 | tf_op jit(solution)/shard_map/ppermute | solution.py:354
  54.3 0.6 pad_add_fusion.refs_0_
  55.0 0.0 collective-permute-done.6.refs_9_
  55.0 0.0 copy-start.5
  55.0 0.7 collective-permute-done.7.refs_10_
  55.7 0.0 copy-start.6
  55.7 0.0 collective-permute-done.5.refs_8_
  55.7 0.0 copy-done.3
  55.7 0.0 copy-done.4
  55.7 0.0 copy-done.5
  55.7 0.7 copy-done.6
  56.5 0.0 copy-start.2
  56.5 1.0 %copy-done.2 = f32[4,136,384]{2,1,0:T(8,128)} copy-done((f32[4,136,384]{2,1,0:T(8,128)}, f32[4,136,384]{2,1,0:T(8,128)S(1)}, u32[]{:S(2)}) %copy-start.2) | copy-done | bytes 835608
  57.4 34.8 %shard_map.41 = (f32[16,384]{1,0:T(8,128)}, f32[384,128]{1,0:T(8,128)}) custom-call(s32[2]{0:T(128)} %pad_add_fusion.refs_0_, f32[128,128]{1,0:T(8,128)} %copy-done.8, f32[384,128]{1,0:T(8,128)} %collective-permute-done.refs_2_, f32[384,128]{1,0:T(8,128)} %refs_3_.1, f32[8,128]{1,0:T(8,128)} %copy-done.9, f32[4,136,384]{2,1,0:T(8,128)} %bitcast.26, ...), custom_call_target="tpu_custom_call" | custom-call | tf_op jit(solution)/shard_map/pallas_call | solution.py:301
  (13 shorter events, 0.0 us)
Async XLA Ops:
  0.6 0.7 copy-start
  2.7 11.0 %copy-start.7 = (f32[384,128]{1,0:T(8,128)S(1)}, f32[384,128]{1,0:T(8,128)}, u32[]{:S(2)}) copy-start(f32[384,128]{1,0:T(8,128)} %refs_3_.1) | copy-start | bytes 589828
  2.7 23.6 %all-to-all-start = ((f32[16,16,384]{2,1,0:T(8,128)}), f32[16,16,384]{2,1,0:T(8,128)S(1)}, u32[]{:S(2)}, u32[]{:S(2)}) async-start(f32[16,16,384]{2,1,0:T(8,128)} %bitcast.2), calls=%async_computation | async-start | bytes 786432 | tf_op jit(solution)/shard_map/all_to_all | solution.py:338
  13.7 12.5 %collective-permute-start = (f32[384,128]{1,0:T(8,128)S(1)}, f32[384,128]{1,0:T(8,128)}, u32[]{:S(2)}, u32[]{:S(2)}) collective-permute-start(f32[384,128]{1,0:T(8,128)S(1)} %copy-done.7), channel_id=1, source_target_pairs={{0,16},{16,32},{32,48},{48,64},{64,80},{80,96},{96,112},{112,128},... | collective-permute-start | bytes 589832 | tf_op jit(solution)/shard_map/ppermute | solution.py:328
  16.8 9.4 %collective-permute-start.1 = (f32[128,128]{1,0:T(8,128)S(1)}, f32[128,128]{1,0:T(8,128)S(1)}, u32[]{:S(2)}, u32[]{:S(2)}) collective-permute-start(f32[128,128]{1,0:T(8,128)S(1)} %slice.39), channel_id=1, source_target_pairs={{0,32},{16,48},{32,64},{48,80},{64,96},{80,112},{96,128},{112,144}... | collective-permute-start | bytes 196616 | tf_op jit(solution)/shard_map/ppermute | solution.py:329
  20.9 5.3 %collective-permute-start.2 = (f32[8,128]{1,0:T(8,128)S(1)}, f32[8,128]{1,0:T(8,128)S(1)}, u32[]{:S(2)}, u32[]{:S(2)}) collective-permute-start(f32[8,128]{1,0:T(8,128)S(1)} %slice.40), channel_id=1, source_target_pairs={{16,0},{32,16},{48,32},{64,48},{80,64},{96,80},{112,96},{128,112},... | collective-permute-start | bytes 12296 | tf_op jit(solution)/shard_map/ppermute | solution.py:330
  26.2 0.6 copy-start.9
  26.2 0.6 copy-start.8
  39.1 4.6 %copy-start.1 = (f32[544,384]{1,0:T(8,128)}, f32[544,384]{1,0:T(8,128)S(1)}, u32[]{:S(2)}) copy-start(f32[544,384]{1,0:T(8,128)S(1)} %all-gather) | copy-start | bytes 2506756
  39.2 7.0 %collective-permute-start.3 = (f32[2,136,384]{2,1,0:T(8,128)S(1)}, f32[2,136,384]{2,1,0:T(8,128)S(1)}, u32[]{:S(2)}, u32[]{:S(2)}) collective-permute-start(f32[2,136,384]{2,1,0:T(8,128)S(1)} %bitcast.28), channel_id=1, source_target_pairs={{0,32},{1,33},{2,34},{3,35},{4,36},{5,37},{6,38},{7,39},{8,40},{9,... | collective-permute-start | bytes 1253384 | tf_op jit(solution)/shard_map/ppermute | solution.py:354
  40.6 11.3 %collective-permute-start.4 = (f32[2,136,384]{2,1,0:T(8,128)S(1)}, f32[2,136,384]{2,1,0:T(8,128)S(1)}, u32[]{:S(2)}, u32[]{:S(2)}) collective-permute-start(f32[2,136,384]{2,1,0:T(8,128)S(1)} %bitcast.27), channel_id=1, source_target_pairs={{0,40},{1,41},{2,42},{3,43},{4,44},{5,45},{6,46},{7,47},{8,32},{9,... | collective-permute-start | bytes 1253384 | tf_op jit(solution)/shard_map/ppermute | solution.py:354
  43.7 12.0 %collective-permute-start.5 = (f32[4,136,384]{2,1,0:T(8,128)S(1)}, f32[4,136,384]{2,1,0:T(8,128)S(1)}, u32[]{:S(2)}, u32[]{:S(2)}) collective-permute-start(f32[4,136,384]{2,1,0:T(8,128)S(1)} %bitcast.25), channel_id=1, source_target_pairs={{0,16},{1,17},{2,18},{3,19},{4,20},{5,21},{6,22},{7,23},{8,24},{9,... | collective-permute-start | bytes 2506760 | tf_op jit(solution)/shard_map/ppermute | solution.py:354
  46.2 9.6 %copy-start.3 = (f32[2,136,384]{2,1,0:T(8,128)}, f32[2,136,384]{2,1,0:T(8,128)S(1)}, u32[]{:S(2)}) copy-start(f32[2,136,384]{2,1,0:T(8,128)S(1)} %collective-permute-done.3.refs_6_) | copy-start | bytes 1253380
  46.2 8.8 %collective-permute-start.6 = (f32[2,136,384]{2,1,0:T(8,128)S(1)}, f32[2,136,384]{2,1,0:T(8,128)S(1)}, u32[]{:S(2)}, u32[]{:S(2)}) collective-permute-start(f32[2,136,384]{2,1,0:T(8,128)S(1)} %collective-permute-done.3.refs_6_), channel_id=1, source_target_pairs={{0,16},{1,17},{2,18},{3,19},{4,20},{5,21},{6,22},{7,23},{8,24},{9,... | collective-permute-start | bytes 1253384 | tf_op jit(solution)/shard_map/ppermute | solution.py:354
  51.9 3.8 %copy-start.4 = (f32[2,136,384]{2,1,0:T(8,128)}, f32[2,136,384]{2,1,0:T(8,128)S(1)}, u32[]{:S(2)}) copy-start(f32[2,136,384]{2,1,0:T(8,128)S(1)} %collective-permute-done.4.refs_7_) | copy-start | bytes 1253380
  51.9 3.8 %collective-permute-start.7 = (f32[2,136,384]{2,1,0:T(8,128)S(1)}, f32[2,136,384]{2,1,0:T(8,128)S(1)}, u32[]{:S(2)}, u32[]{:S(2)}) collective-permute-start(f32[2,136,384]{2,1,0:T(8,128)S(1)} %collective-permute-done.4.refs_7_), channel_id=1, source_target_pairs={{0,16},{1,17},{2,18},{3,19},{4,20},{5,21},{6,22},{7,23},{8,24},{9,... | collective-permute-start | bytes 1253384 | tf_op jit(solution)/shard_map/ppermute | solution.py:354
  55.0 0.8 copy-start.5
  55.7 0.8 copy-start.6
  56.5 1.0 %copy-start.2 = (f32[4,136,384]{2,1,0:T(8,128)}, f32[4,136,384]{2,1,0:T(8,128)S(1)}, u32[]{:S(2)}) copy-start(f32[4,136,384]{2,1,0:T(8,128)S(1)} %collective-permute-done.5.refs_8_) | copy-start | bytes 2506756

commit v6 on v5

--- a/solution.py
+++ b/solution.py
@@ -165,6 +165,28 @@
             b_last = rows[s, 5:6, :]
 
             left = lefts[s][here, :]
+            left_last = left[BW - 1 : BW, :]
+            if s > 0:
+                left = with_last(left, left_last - b_last * u_before)
+            a_row = row_sum(u_col * left)
+            left = left - u_col * a_row
+            mid = diags[s][here, :]
+            y_row = row_sum(u_col * mid)
+            entering, unit = None, None
+            if s > 0:
+                last_row = mid[BW - 1 : BW, :]
+                column = line == s - 1
+                y_row = jnp.where(column, lane_sum(u_row * last_row), y_row)
+                mid = with_last(jnp.where(column, 0.0, mid), last_row)
+                entering = jnp.where(column, 0.0, last_row)
+                unit = jnp.where(column, -1.0, 0.0)
+            product = lane_sum(u_row * y_row)
+            change = outer_sum(u_row, y_row, entering, unit)
+            if s > 0:
+                turned[s, 0:BW, :] = change
+                turned[s, BW : BW + 8, :] = change[0:8, :]
+                change = turned[s, s : s + BW, :]
+            mid = mid - u_col * (y_row - product * u_row) - change
             low = lefts[s][below, :]
             if s > 0:
                 other = rows[s - 1, 3:4, :]
@@ -191,29 +213,6 @@
             next_row = scale * rest_row + jnp.where(line == s, next_head, 0.0)
             next_col = with_first(scale * x_col, next_head)
             next_corner = jnp.where(valid, -length, x_head)
-
-            left_last = left[BW - 1 : BW, :]
-            if s > 0:
-                left = with_last(left, left_last - b_last * u_before)
-            a_row = row_sum(u_col * left)
-            left = left - u_col * a_row
-            mid = diags[s][here, :]
-            y_row = row_sum(u_col * mid)
-            entering, unit = None, None
-            if s > 0:
-                last_row = mid[BW - 1 : BW, :]
-                column = line == s - 1
-                y_row = jnp.where(column, lane_sum(u_row * last_row), y_row)
-                mid = with_last(jnp.where(column, 0.0, mid), last_row)
-                entering = jnp.where(column, 0.0, last_row)
-                unit = jnp.where(column, -1.0, 0.0)
-            product = lane_sum(u_row * y_row)
-            change = outer_sum(u_row, y_row, entering, unit)
-            if s > 0:
-                turned[s, 0:BW, :] = change
-                turned[s, BW : BW + 8, :] = change[0:8, :]
-                change = turned[s, s : s + BW, :]
-            mid = mid - u_col * (y_row - product * u_row) - change
             new_left = jnp.where(line == s, mid, left)
             new_left = with_first(new_left, jnp.where(line == s, corner, left_over(s, k == steps)))
             new_mid = with_first(mid, jnp.where(line == s, mid[0:1, :], left[0:1, :]))

time: 92.6 us -> 92.2 us (level)
  no operation moved by 1% of the time
where the time goes in v6:
time: 92.2 us; the launch traced here: 91.8 us
  starting transfers between devices  34.6 us (38%)
  Pallas kernels  34.4 us (37%)
  blocking collectives  12.2 us (13%)
  waiting for transfers between devices  4.75 us (5%)
  local copies, waits for them, and re-layouts  3.11 us (3%)
  matrix products  1.31 us (1%)
    pallas_call x1, Pallas kernels, run_chase(): pl.pallas_call(functools.partial(chase_kernel, kinds), out_shape=(jax.Sha...  34.4 us
    ppermute x5, starting transfers between devices, swap(): return lax.ppermute(x, ('band', 'cols'), pairs)  14.5 us
    all_gather x1, blocking collectives, body(): part_y = lax.all_gather(own_part, 'band', axis=0, axis_index_groups=groups)  12.2 us
    all_to_all x1, starting transfers between devices, body(): lax.all_to_all(copies.reshape(peers, count_dev, length), 'cols', 0, 0, ti...  11 us
    ppermute x1, starting transfers between devices, body(): lax.ppermute(eigenvectors[rows_dev - (HALO - rows_dev):], 'band', up(2))  4.07 us
    ppermute x1, waiting for transfers between devices, body(): beyond = lax.ppermute(eigenvectors[:TAIL], 'band', up(-1))  3.4 us
    ppermute x1, starting transfers between devices, body(): above_1 = lax.ppermute(eigenvectors, 'band', up(1))  3.06 us
    unnamed x28, local copies, waits for them, and re-layouts  3.04 us
  transfers between devices with their start and end apart: 9, of which 3 were waited for; matrix products, arithmetic and copies ran while one was open for 1% of the time, Pallas kernels for 0%

profile of v6, /device:TPU:1, one launch (start us, length us, event | category | flops | bytes accessed | tf_op | source)
XLA Modules:
  0.0 91.8 jit_solution(6797366433202361986)
XLA Ops:
  0.6 0.0 copy-start
  0.7 0.7 copy-done
  1.4 1.3 %fusion = f32[256,384]{1,0:T(8,128)} fusion(f32[16,384]{1,0:T(8,128)S(1)} %copy-done, s32[256]{0:T(256)S(1)} %get-tuple-element.12, s32[256]{0:T(256)S(1)} %get-tuple-element.13, pred[256]{0:T(512)(128)(4,1)S(1)} %compare_and_fusion), kind=kOutput, calls=%fused_computation | convolution fusion | flops 18890752 | bytes 420096 | tf_op jit(solution)/shard_map/dot_general | solution.py:336
  2.7 0.0 copy-start.7
  2.7 11.0 %all-to-all-start = ((f32[16,16,384]{2,1,0:T(8,128)}), f32[16,16,384]{2,1,0:T(8,128)S(1)}, u32[]{:S(2)}, u32[]{:S(2)}) async-start(f32[16,16,384]{2,1,0:T(8,128)} %bitcast.2), calls=%async_computation | async-start | bytes 786432 | tf_op jit(solution)/shard_map/all_to_all | solution.py:337
  13.7 0.0 copy-done.7
  13.7 3.1 %collective-permute-start = (f32[384,128]{1,0:T(8,128)S(1)}, f32[384,128]{1,0:T(8,128)}, u32[]{:S(2)}, u32[]{:S(2)}) collective-permute-start(f32[384,128]{1,0:T(8,128)S(1)} %copy-done.7), channel_id=1, source_target_pairs={{0,16},{16,32},{32,48},{48,64},{64,80},{80,96},{96,112},{112,128},... | collective-permute-start | bytes 589832 | tf_op jit(solution)/shard_map/ppermute | solution.py:327
  16.8 4.1 %collective-permute-start.1 = (f32[128,128]{1,0:T(8,128)S(1)}, f32[128,128]{1,0:T(8,128)S(1)}, u32[]{:S(2)}, u32[]{:S(2)}) collective-permute-start(f32[128,128]{1,0:T(8,128)S(1)} %slice.39), channel_id=1, source_target_pairs={{0,32},{16,48},{32,64},{48,80},{64,96},{80,112},{96,128},{112,144}... | collective-permute-start | bytes 196616 | tf_op jit(solution)/shard_map/ppermute | solution.py:328
  20.9 1.9 %collective-permute-start.2 = (f32[8,128]{1,0:T(8,128)S(1)}, f32[8,128]{1,0:T(8,128)S(1)}, u32[]{:S(2)}, u32[]{:S(2)}) collective-permute-start(f32[8,128]{1,0:T(8,128)S(1)} %slice.40), channel_id=1, source_target_pairs={{16,0},{32,16},{48,32},{64,48},{80,64},{96,80},{112,96},{128,112},... | collective-permute-start | bytes 12296 | tf_op jit(solution)/shard_map/ppermute | solution.py:329
  22.8 3.4 %collective-permute-done.2.refs_4_ = f32[8,128]{1,0:T(8,128)S(1)} collective-permute-done((f32[8,128]{1,0:T(8,128)S(1)}, f32[8,128]{1,0:T(8,128)S(1)}, u32[]{:S(2)}, u32[]{:S(2)}) %collective-permute-start.2) | collective-permute-done | bytes 4128 | tf_op jit(solution)/shard_map/ppermute | solution.py:329
  26.2 0.0 copy-start.9
  26.2 0.0 collective-permute-done.1.refs_1_
  26.2 0.0 copy-start.8
  26.2 0.0 collective-permute-done.refs_2_
  26.2 0.0 all-to-all-done
  26.3 0.6 copy-done.9
  26.8 0.0 copy-done.8
  26.9 12.2 %all-gather = f32[544,384]{1,0:T(8,128)S(1)} all-gather(f32[136,384]{1,0:T(8,128)S(1)} %constant_dynamic-update-slice_fusion), channel_id=2, replica_groups={{0,64,128,192},{16,80,144,208},{32,96,160,224},{48,112,176,240},{1,65,1..., dimensions={0}, use_global_device_ids=true | all-gather | bytes 1044480 | tf_op jit(solution)/shard_map/all_gather | solution.py:345
  39.1 0.0 copy-start.1
  39.1 0.1 fusion.12
  39.2 1.4 %collective-permute-start.3 = (f32[2,136,384]{2,1,0:T(8,128)S(1)}, f32[2,136,384]{2,1,0:T(8,128)S(1)}, u32[]{:S(2)}, u32[]{:S(2)}) collective-permute-start(f32[2,136,384]{2,1,0:T(8,128)S(1)} %bitcast.28), channel_id=1, source_target_pairs={{0,32},{1,33},{2,34},{3,35},{4,36},{5,37},{6,38},{7,39},{8,40},{9,... | collective-permute-start | bytes 1253384 | tf_op jit(solution)/shard_map/ppermute | solution.py:353
  40.6 3.1 %collective-permute-start.4 = (f32[2,136,384]{2,1,0:T(8,128)S(1)}, f32[2,136,384]{2,1,0:T(8,128)S(1)}, u32[]{:S(2)}, u32[]{:S(2)}) collective-permute-start(f32[2,136,384]{2,1,0:T(8,128)S(1)} %bitcast.27), channel_id=1, source_target_pairs={{0,40},{1,41},{2,42},{3,43},{4,44},{5,45},{6,46},{7,47},{8,32},{9,... | collective-permute-start | bytes 1253384 | tf_op jit(solution)/shard_map/ppermute | solution.py:353
  43.7 0.0 copy-done.1
  43.7 1.8 %collective-permute-start.5 = (f32[4,136,384]{2,1,0:T(8,128)S(1)}, f32[4,136,384]{2,1,0:T(8,128)S(1)}, u32[]{:S(2)}, u32[]{:S(2)}) collective-permute-start(f32[4,136,384]{2,1,0:T(8,128)S(1)} %bitcast.25), channel_id=1, source_target_pairs={{0,16},{1,17},{2,18},{3,19},{4,20},{5,21},{6,22},{7,23},{8,24},{9,... | collective-permute-start | bytes 2506760 | tf_op jit(solution)/shard_map/ppermute | solution.py:353
  45.6 0.6 collective-permute-done.3.refs_6_
  46.2 0.0 copy-start.3
  46.2 5.7 %collective-permute-start.6 = (f32[2,136,384]{2,1,0:T(8,128)S(1)}, f32[2,136,384]{2,1,0:T(8,128)S(1)}, u32[]{:S(2)}, u32[]{:S(2)}) collective-permute-start(f32[2,136,384]{2,1,0:T(8,128)S(1)} %collective-permute-done.3.refs_6_), channel_id=1, source_target_pairs={{0,16},{1,17},{2,18},{3,19},{4,20},{5,21},{6,22},{7,23},{8,24},{9,... | collective-permute-start | bytes 1253384 | tf_op jit(solution)/shard_map/ppermute | solution.py:353
  51.9 0.0 collective-permute-done.4.refs_7_
  51.9 0.0 copy-start.4
  51.9 2.4 %collective-permute-start.7 = (f32[2,136,384]{2,1,0:T(8,128)S(1)}, f32[2,136,384]{2,1,0:T(8,128)S(1)}, u32[]{:S(2)}, u32[]{:S(2)}) collective-permute-start(f32[2,136,384]{2,1,0:T(8,128)S(1)} %collective-permute-done.4.refs_7_), channel_id=1, source_target_pairs={{0,16},{1,17},{2,18},{3,19},{4,20},{5,21},{6,22},{7,23},{8,24},{9,... | collective-permute-start | bytes 1253384 | tf_op jit(solution)/shard_map/ppermute | solution.py:353
  54.3 0.6 pad_add_fusion.refs_0_
  55.0 0.0 collective-permute-done.6.refs_9_
  55.0 0.0 copy-start.5
  55.0 0.7 collective-permute-done.7.refs_10_
  55.7 0.0 copy-start.6
  55.7 0.0 collective-permute-done.5.refs_8_
  55.7 0.0 copy-done.3
  55.7 0.0 copy-done.4
  55.7 0.0 copy-done.5
  55.7 0.7 copy-done.6
  56.5 0.0 copy-start.2
  56.5 1.0 %copy-done.2 = f32[4,136,384]{2,1,0:T(8,128)} copy-done((f32[4,136,384]{2,1,0:T(8,128)}, f32[4,136,384]{2,1,0:T(8,128)S(1)}, u32[]{:S(2)}) %copy-start.2) | copy-done | bytes 835608
  57.4 34.4 %shard_map.41 = (f32[16,384]{1,0:T(8,128)}, f32[384,128]{1,0:T(8,128)}) custom-call(s32[2]{0:T(128)} %pad_add_fusion.refs_0_, f32[128,128]{1,0:T(8,128)} %copy-done.8, f32[384,128]{1,0:T(8,128)} %collective-permute-done.refs_2_, f32[384,128]{1,0:T(8,128)} %refs_3_.1, f32[8,128]{1,0:T(8,128)} %copy-done.9, f32[4,136,384]{2,1,0:T(8,128)} %bitcast.26, ...), custom_call_target="tpu_custom_call" | custom-call | tf_op jit(solution)/shard_map/pallas_call | solution.py:300
  (13 shorter events, 0.0 us)
Async XLA Ops:
  0.6 0.7 copy-start
  2.7 11.0 %copy-start.7 = (f32[384,128]{1,0:T(8,128)S(1)}, f32[384,128]{1,0:T(8,128)}, u32[]{:S(2)}) copy-start(f32[384,128]{1,0:T(8,128)} %refs_3_.1) | copy-start | bytes 589828
  2.7 23.6 %all-to-all-start = ((f32[16,16,384]{2,1,0:T(8,128)}), f32[16,16,384]{2,1,0:T(8,128)S(1)}, u32[]{:S(2)}, u32[]{:S(2)}) async-start(f32[16,16,384]{2,1,0:T(8,128)} %bitcast.2), calls=%async_computation | async-start | bytes 786432 | tf_op jit(solution)/shard_map/all_to_all | solution.py:337
  13.7 12.5 %collective-permute-start = (f32[384,128]{1,0:T(8,128)S(1)}, f32[384,128]{1,0:T(8,128)}, u32[]{:S(2)}, u32[]{:S(2)}) collective-permute-start(f32[384,128]{1,0:T(8,128)S(1)} %copy-done.7), channel_id=1, source_target_pairs={{0,16},{16,32},{32,48},{48,64},{64,80},{80,96},{96,112},{112,128},... | collective-permute-start | bytes 589832 | tf_op jit(solution)/shard_map/ppermute | solution.py:327
  16.8 9.4 %collective-permute-start.1 = (f32[128,128]{1,0:T(8,128)S(1)}, f32[128,128]{1,0:T(8,128)S(1)}, u32[]{:S(2)}, u32[]{:S(2)}) collective-permute-start(f32[128,128]{1,0:T(8,128)S(1)} %slice.39), channel_id=1, source_target_pairs={{0,32},{16,48},{32,64},{48,80},{64,96},{80,112},{96,128},{112,144}... | collective-permute-start | bytes 196616 | tf_op jit(solution)/shard_map/ppermute | solution.py:328
  20.9 5.3 %collective-permute-start.2 = (f32[8,128]{1,0:T(8,128)S(1)}, f32[8,128]{1,0:T(8,128)S(1)}, u32[]{:S(2)}, u32[]{:S(2)}) collective-permute-start(f32[8,128]{1,0:T(8,128)S(1)} %slice.40), channel_id=1, source_target_pairs={{16,0},{32,16},{48,32},{64,48},{80,64},{96,80},{112,96},{128,112},... | collective-permute-start | bytes 12296 | tf_op jit(solution)/shard_map/ppermute | solution.py:329
  26.2 0.6 copy-start.9
  26.2 0.6 copy-start.8
  39.1 4.6 %copy-start.1 = (f32[544,384]{1,0:T(8,128)}, f32[544,384]{1,0:T(8,128)S(1)}, u32[]{:S(2)}) copy-start(f32[544,384]{1,0:T(8,128)S(1)} %all-gather) | copy-start | bytes 2506756
  39.2 7.0 %collective-permute-start.3 = (f32[2,136,384]{2,1,0:T(8,128)S(1)}, f32[2,136,384]{2,1,0:T(8,128)S(1)}, u32[]{:S(2)}, u32[]{:S(2)}) collective-permute-start(f32[2,136,384]{2,1,0:T(8,128)S(1)} %bitcast.28), channel_id=1, source_target_pairs={{0,32},{1,33},{2,34},{3,35},{4,36},{5,37},{6,38},{7,39},{8,40},{9,... | collective-permute-start | bytes 1253384 | tf_op jit(solution)/shard_map/ppermute | solution.py:353
  40.6 11.3 %collective-permute-start.4 = (f32[2,136,384]{2,1,0:T(8,128)S(1)}, f32[2,136,384]{2,1,0:T(8,128)S(1)}, u32[]{:S(2)}, u32[]{:S(2)}) collective-permute-start(f32[2,136,384]{2,1,0:T(8,128)S(1)} %bitcast.27), channel_id=1, source_target_pairs={{0,40},{1,41},{2,42},{3,43},{4,44},{5,45},{6,46},{7,47},{8,32},{9,... | collective-permute-start | bytes 1253384 | tf_op jit(solution)/shard_map/ppermute | solution.py:353
  43.7 12.0 %collective-permute-start.5 = (f32[4,136,384]{2,1,0:T(8,128)S(1)}, f32[4,136,384]{2,1,0:T(8,128)S(1)}, u32[]{:S(2)}, u32[]{:S(2)}) collective-permute-start(f32[4,136,384]{2,1,0:T(8,128)S(1)} %bitcast.25), channel_id=1, source_target_pairs={{0,16},{1,17},{2,18},{3,19},{4,20},{5,21},{6,22},{7,23},{8,24},{9,... | collective-permute-start | bytes 2506760 | tf_op jit(solution)/shard_map/ppermute | solution.py:353
  46.2 9.6 %copy-start.3 = (f32[2,136,384]{2,1,0:T(8,128)}, f32[2,136,384]{2,1,0:T(8,128)S(1)}, u32[]{:S(2)}) copy-start(f32[2,136,384]{2,1,0:T(8,128)S(1)} %collective-permute-done.3.refs_6_) | copy-start | bytes 1253380
  46.2 8.8 %collective-permute-start.6 = (f32[2,136,384]{2,1,0:T(8,128)S(1)}, f32[2,136,384]{2,1,0:T(8,128)S(1)}, u32[]{:S(2)}, u32[]{:S(2)}) collective-permute-start(f32[2,136,384]{2,1,0:T(8,128)S(1)} %collective-permute-done.3.refs_6_), channel_id=1, source_target_pairs={{0,16},{1,17},{2,18},{3,19},{4,20},{5,21},{6,22},{7,23},{8,24},{9,... | collective-permute-start | bytes 1253384 | tf_op jit(solution)/shard_map/ppermute | solution.py:353
  51.9 3.8 %copy-start.4 = (f32[2,136,384]{2,1,0:T(8,128)}, f32[2,136,384]{2,1,0:T(8,128)S(1)}, u32[]{:S(2)}) copy-start(f32[2,136,384]{2,1,0:T(8,128)S(1)} %collective-permute-done.4.refs_7_) | copy-start | bytes 1253380
  51.9 3.8 %collective-permute-start.7 = (f32[2,136,384]{2,1,0:T(8,128)S(1)}, f32[2,136,384]{2,1,0:T(8,128)S(1)}, u32[]{:S(2)}, u32[]{:S(2)}) collective-permute-start(f32[2,136,384]{2,1,0:T(8,128)S(1)} %collective-permute-done.4.refs_7_), channel_id=1, source_target_pairs={{0,16},{1,17},{2,18},{3,19},{4,20},{5,21},{6,22},{7,23},{8,24},{9,... | collective-permute-start | bytes 1253384 | tf_op jit(solution)/shard_map/ppermute | solution.py:353
  55.0 0.8 copy-start.5
  55.7 0.8 copy-start.6
  56.5 1.0 %copy-start.2 = (f32[4,136,384]{2,1,0:T(8,128)}, f32[4,136,384]{2,1,0:T(8,128)S(1)}, u32[]{:S(2)}) copy-start(f32[4,136,384]{2,1,0:T(8,128)S(1)} %collective-permute-done.5.refs_8_) | copy-start | bytes 2506756

commit v7 on v6

--- a/solution.py
+++ b/solution.py
@@ -106,7 +106,7 @@
         ref[pl.ds(start, ref.shape[0] - start), :] = jnp.zeros((ref.shape[0] - start, BW), jnp.float32)
     for s in range(SWEEPS):
         rows[s] = jnp.zeros((8, BW), jnp.float32)
-        for slot in range(SLOTS):
+        for slot in (0, 1, 2, 3, SLOTS - 1):
             kept[s][slot] = zero_block
 
     own = (sub - 1) & (BW - 1)
@@ -114,21 +114,22 @@
     for part, (core, side, first, _) in zip(parts, kinds):
         length = part.shape[2]
 
-        def lay_out(index, carry):
-            owner = (index + first) * 4 + ((device & 3) ^ (2 * side + core))
-            for block in range(length // BW):
-                source = pl.ds(block * BW, BW)
-                begin = pl.multiple_of(owner * length + block * BW, BW) + OFF
-                tile = part[index, 0:BW, source].T
-                tile = pltpu.roll(tile, 0, 1, stride=1, stride_axis=0)
-                far = pltpu.roll(part[index, BW : BW + 8, source], BW - 1, 1)
-                far = jnp.broadcast_to(far[7:8, :], (BW, BW))
-                left = jnp.where(lane > own, tile, jnp.where(lane == own, far, 0.0))
-                lefts[0][pl.ds(begin, BW), :] = left
-                diags[0][pl.ds(begin, BW), :] = jnp.where(lane <= own, tile, 0.0)
+        def lay_out(pair, carry):
+            for index in (2 * pair, 2 * pair + 1):
+                owner = (index + first) * 4 + ((device & 3) ^ (2 * side + core))
+                for block in range(length // BW):
+                    source = pl.ds(block * BW, BW)
+                    begin = pl.multiple_of(owner * length + block * BW, BW) + OFF
+                    tile = part[index, 0:BW, source].T
+                    tile = pltpu.roll(tile, 0, 1, stride=1, stride_axis=0)
+                    far = pltpu.roll(part[index, BW : BW + 8, source], BW - 1, 1)
+                    far = jnp.broadcast_to(far[7:8, :], (BW, BW))
+                    left = jnp.where(lane > own, tile, jnp.where(lane == own, far, 0.0))
+                    lefts[0][pl.ds(begin, BW), :] = left
+                    diags[0][pl.ds(begin, BW), :] = jnp.where(lane <= own, tile, 0.0)
             return carry
 
-        lax.fori_loop(0, part.shape[0], lay_out, 0)
+        lax.fori_loop(0, part.shape[0] // 2, lay_out, 0)
 
     def mirror(index, carry):
         places = [pl.ds(pl.multiple_of((index * 7 + i) * BW + BW, 8), BW) for i in range(7)]

time: 92.2 us -> 90.8 us (0.985)
  Pallas kernels: 34.4 us -> 33 us
    pallas_call x1, Pallas kernels: 34.4 us -> 33 us  [run_chase(): pl.pallas_call(functools.partial(chase_kernel, kinds), out_shape=(jax.Sha...]
where the time goes in v7:
time: 90.8 us; the launch traced here: 90.4 us
  starting transfers between devices  34.6 us (38%)
  Pallas kernels  33 us (36%)
  blocking collectives  12.2 us (13%)
  waiting for transfers between devices  4.75 us (5%)
  local copies, waits for them, and re-layouts  3.11 us (3%)
  matrix products  1.31 us (1%)
    pallas_call x1, Pallas kernels, run_chase(): pl.pallas_call(functools.partial(chase_kernel, kinds), out_shape=(jax.Sha...  33 us
    ppermute x5, starting transfers between devices, swap(): return lax.ppermute(x, ('band', 'cols'), pairs)  14.5 us
    all_gather x1, blocking collectives, body(): part_y = lax.all_gather(own_part, 'band', axis=0, axis_index_groups=groups)  12.2 us
    all_to_all x1, starting transfers between devices, body(): lax.all_to_all(copies.reshape(peers, count_dev, length), 'cols', 0, 0, ti...  11 us
    ppermute x1, starting transfers between devices, body(): lax.ppermute(eigenvectors[rows_dev - (HALO - rows_dev):], 'band', up(2))  4.07 us
    ppermute x1, waiting for transfers between devices, body(): beyond = lax.ppermute(eigenvectors[:TAIL], 'band', up(-1))  3.4 us
    ppermute x1, starting transfers between devices, body(): above_1 = lax.ppermute(eigenvectors, 'band', up(1))  3.06 us
    unnamed x28, local copies, waits for them, and re-layouts  3.04 us
  transfers between devices with their start and end apart: 9, of which 3 were waited for; matrix products, arithmetic and copies ran while one was open for 1% of the time, Pallas kernels for 0%

profile of v7, /device:TPU:1, one launch (start us, length us, event | category | flops | bytes accessed | tf_op | source)
XLA Modules:
  0.0 90.4 jit_solution(14257495361193975870)
XLA Ops:
  0.6 0.0 copy-start
  0.7 0.7 copy-done
  1.4 1.3 %fusion = f32[256,384]{1,0:T(8,128)} fusion(f32[16,384]{1,0:T(8,128)S(1)} %copy-done, s32[256]{0:T(256)S(1)} %get-tuple-element.12, s32[256]{0:T(256)S(1)} %get-tuple-element.13, pred[256]{0:T(512)(128)(4,1)S(1)} %compare_and_fusion), kind=kOutput, calls=%fused_computation | convolution fusion | flops 18890752 | bytes 420096 | tf_op jit(solution)/shard_map/dot_general | solution.py:337
  2.7 0.0 copy-start.7
  2.7 11.0 %all-to-all-start = ((f32[16,16,384]{2,1,0:T(8,128)}), f32[16,16,384]{2,1,0:T(8,128)S(1)}, u32[]{:S(2)}, u32[]{:S(2)}) async-start(f32[16,16,384]{2,1,0:T(8,128)} %bitcast.2), calls=%async_computation | async-start | bytes 786432 | tf_op jit(solution)/shard_map/all_to_all | solution.py:338
  13.7 0.0 copy-done.7
  13.7 3.1 %collective-permute-start = (f32[384,128]{1,0:T(8,128)S(1)}, f32[384,128]{1,0:T(8,128)}, u32[]{:S(2)}, u32[]{:S(2)}) collective-permute-start(f32[384,128]{1,0:T(8,128)S(1)} %copy-done.7), channel_id=1, source_target_pairs={{0,16},{16,32},{32,48},{48,64},{64,80},{80,96},{96,112},{112,128},... | collective-permute-start | bytes 589832 | tf_op jit(solution)/shard_map/ppermute | solution.py:328
  16.8 4.1 %collective-permute-start.1 = (f32[128,128]{1,0:T(8,128)S(1)}, f32[128,128]{1,0:T(8,128)S(1)}, u32[]{:S(2)}, u32[]{:S(2)}) collective-permute-start(f32[128,128]{1,0:T(8,128)S(1)} %slice.39), channel_id=1, source_target_pairs={{0,32},{16,48},{32,64},{48,80},{64,96},{80,112},{96,128},{112,144}... | collective-permute-start | bytes 196616 | tf_op jit(solution)/shard_map/ppermute | solution.py:329
  20.9 1.9 %collective-permute-start.2 = (f32[8,128]{1,0:T(8,128)S(1)}, f32[8,128]{1,0:T(8,128)S(1)}, u32[]{:S(2)}, u32[]{:S(2)}) collective-permute-start(f32[8,128]{1,0:T(8,128)S(1)} %slice.40), channel_id=1, source_target_pairs={{16,0},{32,16},{48,32},{64,48},{80,64},{96,80},{112,96},{128,112},... | collective-permute-start | bytes 12296 | tf_op jit(solution)/shard_map/ppermute | solution.py:330
  22.8 3.4 %collective-permute-done.2.refs_4_ = f32[8,128]{1,0:T(8,128)S(1)} collective-permute-done((f32[8,128]{1,0:T(8,128)S(1)}, f32[8,128]{1,0:T(8,128)S(1)}, u32[]{:S(2)}, u32[]{:S(2)}) %collective-permute-start.2) | collective-permute-done | bytes 4128 | tf_op jit(solution)/shard_map/ppermute | solution.py:330
  26.2 0.0 copy-start.9
  26.2 0.0 collective-permute-done.1.refs_1_
  26.2 0.0 copy-start.8
  26.2 0.0 collective-permute-done.refs_2_
  26.2 0.0 all-to-all-done
  26.3 0.6 copy-done.9
  26.8 0.0 copy-done.8
  26.9 12.2 %all-gather = f32[544,384]{1,0:T(8,128)S(1)} all-gather(f32[136,384]{1,0:T(8,128)S(1)} %constant_dynamic-update-slice_fusion), channel_id=2, replica_groups={{0,64,128,192},{16,80,144,208},{32,96,160,224},{48,112,176,240},{1,65,1..., dimensions={0}, use_global_device_ids=true | all-gather | bytes 1044480 | tf_op jit(solution)/shard_map/all_gather | solution.py:346
  39.1 0.0 copy-start.1
  39.1 0.1 fusion.12
  39.2 1.4 %collective-permute-start.3 = (f32[2,136,384]{2,1,0:T(8,128)S(1)}, f32[2,136,384]{2,1,0:T(8,128)S(1)}, u32[]{:S(2)}, u32[]{:S(2)}) collective-permute-start(f32[2,136,384]{2,1,0:T(8,128)S(1)} %bitcast.28), channel_id=1, source_target_pairs={{0,32},{1,33},{2,34},{3,35},{4,36},{5,37},{6,38},{7,39},{8,40},{9,... | collective-permute-start | bytes 1253384 | tf_op jit(solution)/shard_map/ppermute | solution.py:354
  40.6 3.1 %collective-permute-start.4 = (f32[2,136,384]{2,1,0:T(8,128)S(1)}, f32[2,136,384]{2,1,0:T(8,128)S(1)}, u32[]{:S(2)}, u32[]{:S(2)}) collective-permute-start(f32[2,136,384]{2,1,0:T(8,128)S(1)} %bitcast.27), channel_id=1, source_target_pairs={{0,40},{1,41},{2,42},{3,43},{4,44},{5,45},{6,46},{7,47},{8,32},{9,... | collective-permute-start | bytes 1253384 | tf_op jit(solution)/shard_map/ppermute | solution.py:354
  43.7 0.0 copy-done.1
  43.7 1.8 %collective-permute-start.5 = (f32[4,136,384]{2,1,0:T(8,128)S(1)}, f32[4,136,384]{2,1,0:T(8,128)S(1)}, u32[]{:S(2)}, u32[]{:S(2)}) collective-permute-start(f32[4,136,384]{2,1,0:T(8,128)S(1)} %bitcast.25), channel_id=1, source_target_pairs={{0,16},{1,17},{2,18},{3,19},{4,20},{5,21},{6,22},{7,23},{8,24},{9,... | collective-permute-start | bytes 2506760 | tf_op jit(solution)/shard_map/ppermute | solution.py:354
  45.6 0.6 collective-permute-done.3.refs_6_
  46.2 0.0 copy-start.3
  46.2 5.7 %collective-permute-start.6 = (f32[2,136,384]{2,1,0:T(8,128)S(1)}, f32[2,136,384]{2,1,0:T(8,128)S(1)}, u32[]{:S(2)}, u32[]{:S(2)}) collective-permute-start(f32[2,136,384]{2,1,0:T(8,128)S(1)} %collective-permute-done.3.refs_6_), channel_id=1, source_target_pairs={{0,16},{1,17},{2,18},{3,19},{4,20},{5,21},{6,22},{7,23},{8,24},{9,... | collective-permute-start | bytes 1253384 | tf_op jit(solution)/shard_map/ppermute | solution.py:354
  51.9 0.0 collective-permute-done.4.refs_7_
  51.9 0.0 copy-start.4
  51.9 2.4 %collective-permute-start.7 = (f32[2,136,384]{2,1,0:T(8,128)S(1)}, f32[2,136,384]{2,1,0:T(8,128)S(1)}, u32[]{:S(2)}, u32[]{:S(2)}) collective-permute-start(f32[2,136,384]{2,1,0:T(8,128)S(1)} %collective-permute-done.4.refs_7_), channel_id=1, source_target_pairs={{0,16},{1,17},{2,18},{3,19},{4,20},{5,21},{6,22},{7,23},{8,24},{9,... | collective-permute-start | bytes 1253384 | tf_op jit(solution)/shard_map/ppermute | solution.py:354
  54.3 0.6 pad_add_fusion.refs_0_
  55.0 0.0 collective-permute-done.6.refs_9_
  55.0 0.0 copy-start.5
  55.0 0.7 collective-permute-done.7.refs_10_
  55.7 0.0 copy-start.6
  55.7 0.0 collective-permute-done.5.refs_8_
  55.7 0.0 copy-done.3
  55.7 0.0 copy-done.4
  55.7 0.0 copy-done.5
  55.7 0.7 copy-done.6
  56.5 0.0 copy-start.2
  56.5 1.0 %copy-done.2 = f32[4,136,384]{2,1,0:T(8,128)} copy-done((f32[4,136,384]{2,1,0:T(8,128)}, f32[4,136,384]{2,1,0:T(8,128)S(1)}, u32[]{:S(2)}) %copy-start.2) | copy-done | bytes 835608
  57.4 33.0 %shard_map.41 = (f32[16,384]{1,0:T(8,128)}, f32[384,128]{1,0:T(8,128)}) custom-call(s32[2]{0:T(128)} %pad_add_fusion.refs_0_, f32[128,128]{1,0:T(8,128)} %copy-done.8, f32[384,128]{1,0:T(8,128)} %collective-permute-done.refs_2_, f32[384,128]{1,0:T(8,128)} %refs_3_.1, f32[8,128]{1,0:T(8,128)} %copy-done.9, f32[4,136,384]{2,1,0:T(8,128)} %bitcast.26, ...), custom_call_target="tpu_custom_call" | custom-call | tf_op jit(solution)/shard_map/pallas_call | solution.py:301
  (13 shorter events, 0.0 us)
Async XLA Ops:
  0.6 0.7 copy-start
  2.7 11.0 %copy-start.7 = (f32[384,128]{1,0:T(8,128)S(1)}, f32[384,128]{1,0:T(8,128)}, u32[]{:S(2)}) copy-start(f32[384,128]{1,0:T(8,128)} %refs_3_.1) | copy-start | bytes 589828
  2.7 23.6 %all-to-all-start = ((f32[16,16,384]{2,1,0:T(8,128)}), f32[16,16,384]{2,1,0:T(8,128)S(1)}, u32[]{:S(2)}, u32[]{:S(2)}) async-start(f32[16,16,384]{2,1,0:T(8,128)} %bitcast.2), calls=%async_computation | async-start | bytes 786432 | tf_op jit(solution)/shard_map/all_to_all | solution.py:338
  13.7 12.5 %collective-permute-start = (f32[384,128]{1,0:T(8,128)S(1)}, f32[384,128]{1,0:T(8,128)}, u32[]{:S(2)}, u32[]{:S(2)}) collective-permute-start(f32[384,128]{1,0:T(8,128)S(1)} %copy-done.7), channel_id=1, source_target_pairs={{0,16},{16,32},{32,48},{48,64},{64,80},{80,96},{96,112},{112,128},... | collective-permute-start | bytes 589832 | tf_op jit(solution)/shard_map/ppermute | solution.py:328
  16.8 9.4 %collective-permute-start.1 = (f32[128,128]{1,0:T(8,128)S(1)}, f32[128,128]{1,0:T(8,128)S(1)}, u32[]{:S(2)}, u32[]{:S(2)}) collective-permute-start(f32[128,128]{1,0:T(8,128)S(1)} %slice.39), channel_id=1, source_target_pairs={{0,32},{16,48},{32,64},{48,80},{64,96},{80,112},{96,128},{112,144}... | collective-permute-start | bytes 196616 | tf_op jit(solution)/shard_map/ppermute | solution.py:329
  20.9 5.3 %collective-permute-start.2 = (f32[8,128]{1,0:T(8,128)S(1)}, f32[8,128]{1,0:T(8,128)S(1)}, u32[]{:S(2)}, u32[]{:S(2)}) collective-permute-start(f32[8,128]{1,0:T(8,128)S(1)} %slice.40), channel_id=1, source_target_pairs={{16,0},{32,16},{48,32},{64,48},{80,64},{96,80},{112,96},{128,112},... | collective-permute-start | bytes 12296 | tf_op jit(solution)/shard_map/ppermute | solution.py:330
  26.2 0.6 copy-start.9
  26.2 0.6 copy-start.8
  39.1 4.6 %copy-start.1 = (f32[544,384]{1,0:T(8,128)}, f32[544,384]{1,0:T(8,128)S(1)}, u32[]{:S(2)}) copy-start(f32[544,384]{1,0:T(8,128)S(1)} %all-gather) | copy-start | bytes 2506756
  39.2 7.0 %collective-permute-start.3 = (f32[2,136,384]{2,1,0:T(8,128)S(1)}, f32[2,136,384]{2,1,0:T(8,128)S(1)}, u32[]{:S(2)}, u32[]{:S(2)}) collective-permute-start(f32[2,136,384]{2,1,0:T(8,128)S(1)} %bitcast.28), channel_id=1, source_target_pairs={{0,32},{1,33},{2,34},{3,35},{4,36},{5,37},{6,38},{7,39},{8,40},{9,... | collective-permute-start | bytes 1253384 | tf_op jit(solution)/shard_map/ppermute | solution.py:354
  40.6 11.3 %collective-permute-start.4 = (f32[2,136,384]{2,1,0:T(8,128)S(1)}, f32[2,136,384]{2,1,0:T(8,128)S(1)}, u32[]{:S(2)}, u32[]{:S(2)}) collective-permute-start(f32[2,136,384]{2,1,0:T(8,128)S(1)} %bitcast.27), channel_id=1, source_target_pairs={{0,40},{1,41},{2,42},{3,43},{4,44},{5,45},{6,46},{7,47},{8,32},{9,... | collective-permute-start | bytes 1253384 | tf_op jit(solution)/shard_map/ppermute | solution.py:354
  43.7 12.0 %collective-permute-start.5 = (f32[4,136,384]{2,1,0:T(8,128)S(1)}, f32[4,136,384]{2,1,0:T(8,128)S(1)}, u32[]{:S(2)}, u32[]{:S(2)}) collective-permute-start(f32[4,136,384]{2,1,0:T(8,128)S(1)} %bitcast.25), channel_id=1, source_target_pairs={{0,16},{1,17},{2,18},{3,19},{4,20},{5,21},{6,22},{7,23},{8,24},{9,... | collective-permute-start | bytes 2506760 | tf_op jit(solution)/shard_map/ppermute | solution.py:354
  46.2 9.6 %copy-start.3 = (f32[2,136,384]{2,1,0:T(8,128)}, f32[2,136,384]{2,1,0:T(8,128)S(1)}, u32[]{:S(2)}) copy-start(f32[2,136,384]{2,1,0:T(8,128)S(1)} %collective-permute-done.3.refs_6_) | copy-start | bytes 1253380
  46.2 8.8 %collective-permute-start.6 = (f32[2,136,384]{2,1,0:T(8,128)S(1)}, f32[2,136,384]{2,1,0:T(8,128)S(1)}, u32[]{:S(2)}, u32[]{:S(2)}) collective-permute-start(f32[2,136,384]{2,1,0:T(8,128)S(1)} %collective-permute-done.3.refs_6_), channel_id=1, source_target_pairs={{0,16},{1,17},{2,18},{3,19},{4,20},{5,21},{6,22},{7,23},{8,24},{9,... | collective-permute-start | bytes 1253384 | tf_op jit(solution)/shard_map/ppermute | solution.py:354
  51.9 3.8 %copy-start.4 = (f32[2,136,384]{2,1,0:T(8,128)}, f32[2,136,384]{2,1,0:T(8,128)S(1)}, u32[]{:S(2)}) copy-start(f32[2,136,384]{2,1,0:T(8,128)S(1)} %collective-permute-done.4.refs_7_) | copy-start | bytes 1253380
  51.9 3.8 %collective-permute-start.7 = (f32[2,136,384]{2,1,0:T(8,128)S(1)}, f32[2,136,384]{2,1,0:T(8,128)S(1)}, u32[]{:S(2)}, u32[]{:S(2)}) collective-permute-start(f32[2,136,384]{2,1,0:T(8,128)S(1)} %collective-permute-done.4.refs_7_), channel_id=1, source_target_pairs={{0,16},{1,17},{2,18},{3,19},{4,20},{5,21},{6,22},{7,23},{8,24},{9,... | collective-permute-start | bytes 1253384 | tf_op jit(solution)/shard_map/ppermute | solution.py:354
  55.0 0.8 copy-start.5
  55.7 0.8 copy-start.6
  56.5 1.0 %copy-start.2 = (f32[4,136,384]{2,1,0:T(8,128)}, f32[4,136,384]{2,1,0:T(8,128)S(1)}, u32[]{:S(2)}) copy-start(f32[4,136,384]{2,1,0:T(8,128)S(1)} %collective-permute-done.5.refs_8_) | copy-start | bytes 2506756
